TPU v7x, 256 devices: a whole 4x4x8 slice. The times are simulated.
256 devices in a mesh: node: 32 (over x, z_hi, core), col: 8 (over z_lo, y).
Axes of the slice: x: 4, y: 4, z: 8 (z_hi: 4, z_lo: 2; z = z_hi * 2 + z_lo), core: 2. Of those that a mesh axis runs over, the one named last changes fastest.
Arguments:
- coefficients: float32 [8, 128, 256, 1024], P('col', 'node'), may hold values from -6 to 6
- self_weights: bfloat16 [8, 6, 128, 256, 256], P('col', None, 'node'), may hold values from -0.25 to 0.25
- cross_weights: bfloat16 [8, 6, 128, 256, 256], P('col', None, 'node'), may hold values from -0.25 to 0.25
- true_ranks: int32 [8, 128], P('col', 'node'), may hold values from 128 to 256
Outputs:
- field: float32 [128, 256, 1024], P('node', None, 'col')
Inputs may be any that keep to these rules, and one draw needn't show every extreme that they name: `true_ranks`: each node's true rank within its padded rank 256.
All inputs are finite; a program needn't handle non-finite values.
Results may differ from a plain program's by a relative error of at most 0.0003.
Values sent between devices are 32-bit elements; how exact they have to be, the bound alone decides.
No kernel may reach another device: no remote copies, remote signals or barrier semaphores. Data moves between devices by JAX's collectives and lax.ppermute only.
A program may use at most 64 MiB of HBM per device.

v0:
```python
import jax
import jax.numpy as jnp
from jax import lax
from jax.sharding import PartitionSpec as P


def partner(value, axis, stride):
    mask = 2**stride
    pairs = [(source, source ^ mask) for source in range(lax.axis_size(axis))]
    return lax.ppermute(value, axis, pairs)


def cut_along(array, dim, count):
    before, after = (array.shape[:dim], array.shape[dim + 1 :])
    return jnp.moveaxis(array.reshape(*before, count, -1, *after), dim, 0)


def sum_at_owner(array, axis, dim):
    count = lax.axis_size(axis)
    blocks = lax.all_to_all(cut_along(array, dim, count), axis, 0, 0, tiled=True)
    return jnp.sum(blocks, axis=0)


def apply_mats(weights, coeffs):
    return jnp.einsum(
        "nrk,nki->nri", weights.astype(jnp.float32), coeffs, precision=lax.Precision.HIGHEST
    )


def partner_view(values, section):
    node_count = values.shape[0]
    shaped = values.reshape((node_count >> section + 1, 2, 1 << section) + values.shape[1:])
    return shaped[:, ::-1].reshape(values.shape)


def shards(coefficients, self_weights, cross_weights, true_ranks):
    coeffs = coefficients[0]
    self_mats = self_weights[0]
    cross_mats = cross_weights[0]
    rank_vec = true_ranks[0]
    node_count = coeffs.shape[0]
    local_bits = node_count.bit_length() - 1
    level_count = self_mats.shape[0]
    row_index = lax.broadcasted_iota(jnp.int32, (node_count, coeffs.shape[1], 1), 1)
    row_keep = (row_index < rank_vec[:, None, None]).astype(jnp.float32)
    for section in range(level_count - 1):
        self_term = apply_mats(self_mats[section], coeffs)
        sent_term = apply_mats(cross_mats[section], coeffs)
        if section < local_bits:
            recv_term = partner_view(sent_term, section)
        else:
            recv_term = partner(sent_term, "node", section - local_bits)
        coeffs = row_keep * (self_term + recv_term)
    final_section = level_count - 1
    self_term = apply_mats(self_mats[final_section], coeffs)
    sent_term = apply_mats(cross_mats[final_section], coeffs)
    recv_term = partner(sent_term, "node", final_section - local_bits)
    return sum_at_owner(row_keep * (self_term + recv_term), "col", 2)


def solution(mesh):
    placed = (
        P("col", "node", None, None),
        P("col", None, "node", None, None),
        P("col", None, "node", None, None),
        P("col", "node"),
    )
    return jax.shard_map(
        shards, mesh=mesh, in_specs=placed, out_specs=P("node", None, "col"), check_vma=False
    )
```

profile of v0, /device:TPU:2, one launch (start us, length us, event | category | flops | bytes accessed | tf_op | source)
XLA Modules:
  0.0 580.9 jit_solution(14468429532370033426)
XLA Ops:
  0.0 0.7 fusion.45
  0.7 6.6 %fusion.7 = f32[4,256,1024]{2,1,0:T(8,128)} fusion(f32[1,4,256,1024]{3,2,1,0:T(8,128)} %param.4, bf16[1,6,4,256,256]{4,3,2,1,0:T(8,128)(2,1)} %param.6), kind=kOutput, calls=%fused_computation.14 | convolution fusion | flops 3221225472 | bytes 8912896 | tf_op jit(solution)/shard_map/nrk,nki->nri/dot_general | solution.py:25
  7.3 4.7 rev.6
  12.0 0.0 copy-start.1
  12.0 6.5 %fusion.6 = f32[4,256,1024]{2,1,0:T(8,128)S(1)} fusion(f32[2,2,1,256,1024]{4,3,1,0,2:T(8,128)} %rev.6, f32[1,4,256,1024]{3,2,1,0:T(8,128)} %param.4, f32[4,256]{1,0:T(4,128)S(1)} %fusion.45, bf16[1,6,4,256,256]{4,3,2,1,0:T(8,128)(2,1)} %param.5), kind=kOutput, calls=%fused_computation.13 | convolution fusion | flops 3223322624 | bytes 13111296 | tf_op jit(solution)/shard_map/nrk,nki->nri/dot_general | solution.py:25
  18.5 0.0 copy-done.1
  18.5 0.0 copy-start
  18.5 5.6 fusion.28
  24.1 0.0 copy-done
  24.1 5.4 copy.28
  29.5 4.7 rev.7
  34.2 6.4 %fusion.5 = f32[4,256,1024]{2,1,0:T(8,128)S(1)} fusion(f32[1,2,2,256,1024]{4,3,2,1,0:T(8,128)} %rev.7, f32[4,256,1024]{2,1,0:T(8,128)} %copy-done, f32[4,256]{1,0:T(4,128)S(1)} %fusion.45, bf16[1,6,4,256,256]{4,3,2,1,0:T(8,128)(2,1)} %param.5), kind=kOutput, calls=%fused_computation.11 | convolution fusion | flops 3223322624 | bytes 13111296 | tf_op jit(solution)/shard_map/nrk,nki->nri/dot_general | solution.py:25
  40.6 0.0 copy-start.2
  40.6 2.3 convolution_bitcast_fusion.3
  42.9 0.1 collective-permute-start
  43.0 7.1 %collective-permute-done = f32[4,256,1024]{2,1,0:T(8,128)S(1)} collective-permute-done((f32[4,256,1024]{2,1,0:T(8,128)S(1)}, f32[4,256,1024]{2,1,0:T(8,128)S(1)}, u32[]{:S(2)}, u32[]{:S(2)}) %collective-permute-start) | collective-permute-done | bytes 4194336 | tf_op jit(solution)/shard_map/ppermute | solution.py:10
  50.2 0.0 copy-done.2
  50.2 2.9 fusion.4
  53.1 2.3 convolution_bitcast_fusion.2
  55.4 3.6 collective-permute-start.1
  59.0 2.4 fusion.24
  61.4 178.3 %collective-permute-done.1 = f32[4,256,1024]{2,1,0:T(8,128)S(1)} collective-permute-done((f32[4,256,1024]{2,1,0:T(8,128)S(1)}, f32[4,256,1024]{2,1,0:T(8,128)S(1)}, u32[]{:S(2)}, u32[]{:S(2)}) %collective-permute-start.1) | collective-permute-done | bytes 4194336 | tf_op jit(solution)/shard_map/ppermute | solution.py:10
  239.7 2.8 convolution_bitcast_fusion.1
  242.6 6.6 %collective-permute-start.2 = (f32[4,256,1024]{2,1,0:T(8,128)S(1)}, f32[4,256,1024]{2,1,0:T(8,128)S(1)}, u32[]{:S(2)}, u32[]{:S(2)}) collective-permute-start(f32[4,256,1024]{2,1,0:T(8,128)S(1)} %convolution_bitcast_fusion.1), channel_id=1, source_target_pairs={{0,32},{8,40},{16,48},{24,56},{32,0},{40,8},{48,16},{56,24},{64,96... | collective-permute-start | bytes 12582920 | tf_op jit(solution)/shard_map/ppermute | solution.py:10
  249.3 2.8 fusion.14
  252.1 178.3 %collective-permute-done.2 = f32[4,256,1024]{2,1,0:T(8,128)S(1)} collective-permute-done((f32[4,256,1024]{2,1,0:T(8,128)S(1)}, f32[4,256,1024]{2,1,0:T(8,128)S(1)}, u32[]{:S(2)}, u32[]{:S(2)}) %collective-permute-start.2) | collective-permute-done | bytes 4194336 | tf_op jit(solution)/shard_map/ppermute | solution.py:10
  430.4 2.8 convolution_bitcast_fusion
  433.2 1.1 collective-permute-start.3
  434.3 2.8 fusion.17
  437.2 87.8 %collective-permute-done.3 = f32[4,256,1024]{2,1,0:T(8,128)S(1)} collective-permute-done((f32[4,256,1024]{2,1,0:T(8,128)S(1)}, f32[4,256,1024]{2,1,0:T(8,128)S(1)}, u32[]{:S(2)}, u32[]{:S(2)}) %collective-permute-start.3) | collective-permute-done | bytes 4194336 | tf_op jit(solution)/shard_map/ppermute | solution.py:10
  525.0 0.7 bitcast_bitcast_fusion
  525.7 51.9 %all_to_all.5 = f32[8,4,256,128]{3,2,1,0:T(8,128)} all-to-all(f32[8,4,256,128]{3,2,1,0:T(8,128)S(1)} %bitcast_bitcast_fusion), channel_id=1, replica_groups=mesh['node'=32,'col'=8] {'col'}, dimensions={0} | all-to-all | bytes 8388608 | tf_op jit(solution)/shard_map/all_to_all | solution.py:20
  577.6 3.2 reduce_sum.9
Async XLA Ops:
  12.0 6.5 %copy-start.1 = (bf16[1,6,4,256,256]{4,3,2,1,0:T(8,128)(2,1)S(1)}, bf16[1,6,4,256,256]{4,3,2,1,0:T(8,128)(2,1)}, u32[]{:S(2)}) copy-start(bf16[1,6,4,256,256]{4,3,2,1,0:T(8,128)(2,1)} %param.6) | copy-start | bytes 9437188
  18.5 5.6 copy-start
  40.6 9.6 %copy-start.2 = (bf16[1,6,4,256,256]{4,3,2,1,0:T(8,128)(2,1)S(1)}, bf16[1,6,4,256,256]{4,3,2,1,0:T(8,128)(2,1)}, u32[]{:S(2)}) copy-start(bf16[1,6,4,256,256]{4,3,2,1,0:T(8,128)(2,1)} %param.5) | copy-start | bytes 9437188
  42.9 7.2 %collective-permute-start = (f32[4,256,1024]{2,1,0:T(8,128)S(1)}, f32[4,256,1024]{2,1,0:T(8,128)S(1)}, u32[]{:S(2)}, u32[]{:S(2)}) collective-permute-start(f32[4,256,1024]{2,1,0:T(8,128)S(1)} %convolution_bitcast_fusion.3), channel_id=1, source_target_pairs={{0,8},{8,0},{16,24},{24,16},{32,40},{40,32},{48,56},{56,48},{64,72... | collective-permute-start | bytes 12582920 | tf_op jit(solution)/shard_map/ppermute | solution.py:10
  55.4 184.3 %collective-permute-start.1 = (f32[4,256,1024]{2,1,0:T(8,128)S(1)}, f32[4,256,1024]{2,1,0:T(8,128)S(1)}, u32[]{:S(2)}, u32[]{:S(2)}) collective-permute-start(f32[4,256,1024]{2,1,0:T(8,128)S(1)} %convolution_bitcast_fusion.2), channel_id=1, source_target_pairs={{0,16},{8,24},{16,0},{24,8},{32,48},{40,56},{48,32},{56,40},{64,80... | collective-permute-start | bytes 12582920 | tf_op jit(solution)/shard_map/ppermute | solution.py:10
  242.6 187.8 %collective-permute-start.2 = (f32[4,256,1024]{2,1,0:T(8,128)S(1)}, f32[4,256,1024]{2,1,0:T(8,128)S(1)}, u32[]{:S(2)}, u32[]{:S(2)}) collective-permute-start(f32[4,256,1024]{2,1,0:T(8,128)S(1)} %convolution_bitcast_fusion.1), channel_id=1, source_target_pairs={{0,32},{8,40},{16,48},{24,56},{32,0},{40,8},{48,16},{56,24},{64,96... | collective-permute-start | bytes 12582920 | tf_op jit(solution)/shard_map/ppermute | solution.py:10
  433.2 91.8 %collective-permute-start.3 = (f32[4,256,1024]{2,1,0:T(8,128)S(1)}, f32[4,256,1024]{2,1,0:T(8,128)S(1)}, u32[]{:S(2)}, u32[]{:S(2)}) collective-permute-start(f32[4,256,1024]{2,1,0:T(8,128)S(1)} %convolution_bitcast_fusion), channel_id=1, source_target_pairs={{0,64},{8,72},{16,80},{24,88},{32,96},{40,104},{48,112},{56,120},{... | collective-permute-start | bytes 12582920 | tf_op jit(solution)/shard_map/ppermute | solution.py:10
where the time goes:
time: 581 us
  waiting for transfers between devices  452 us (78%)
  blocking collectives  51.9 us (9%)
  matrix products  46.3 us (8%)
  local copies, waits for them, and re-layouts  14.9 us (3%)
  starting transfers between devices  11.4 us (2%)
    ppermute x4, waiting for transfers between devices, partner(): return lax.ppermute(value, axis, pairs)  452 us
    all_to_all x1, blocking collectives, sum_at_owner(): lax.all_to_all(cut_along(array, dim, count), axis, 0, 0, tiled=True)  51.9 us
    dot_general x12, matrix products, apply_mats(): jnp.einsum('nrk,nki->nri', weights.astype(jnp.float32), coeffs, precision...  46.3 us
  transfers between devices with their start and end apart: 4, of which 4 were waited for; matrix products, arithmetic and copies ran while one was open for 1% of the time, Pallas kernels for 0%

commit v1 on v0

v1 whole, which is shorter than its diff:
```python
import jax
import jax.numpy as jnp
from jax import lax
from jax.experimental import pallas as pl
from jax.experimental.pallas import tpu as pltpu
from jax.sharding import PartitionSpec as P

F32 = jnp.float32
BF16 = jnp.bfloat16
VMEM_LIMIT = 48 * 1024 * 1024


def params():
    return pltpu.CompilerParams(vmem_limit_bytes=VMEM_LIMIT)


SMALL = pl.CostEstimate(flops=1000, bytes_accessed=1000, transcendentals=0)


def split(state):
    hi = state.astype(BF16)
    return hi, (state - hi.astype(F32)).astype(BF16)


def times(weight, parts):
    hi, lo = parts
    return jnp.dot(weight, hi, preferred_element_type=F32) + jnp.dot(
        weight, lo, preferred_element_type=F32
    )


def masked(rank, value):
    return jnp.where(lax.broadcasted_iota(jnp.int32, value.shape, 0) < rank, value, 0.0)


def local_kernel(ranks, state, self_w, cross_w, keep_out, send_out):
    count = state.shape[1]
    nodes = [state[0, n] for n in range(count)]
    for level in range(2):
        parts = [split(v) for v in nodes]
        kept = [times(self_w[0, level, n], parts[n]) for n in range(count)]
        sent = [times(cross_w[0, level, n], parts[n]) for n in range(count)]
        nodes = [masked(ranks[n], kept[n] + sent[n ^ (1 << level)]) for n in range(count)]
    for n in range(count):
        parts = split(nodes[n])
        keep_out[n] = times(self_w[0, 2, n], parts)
        send_out[n] = times(cross_w[0, 2, n], parts)


def local_levels(part, parts, coefficients, self_weights, cross_weights, ranks):
    _, count, rank, illum = coefficients.shape
    width = illum // parts
    block = 256
    steps = width // block
    mats = pl.BlockSpec((1, 3, count, rank, rank), lambda i, r: (0, 0, 0, 0, 0))
    out = pl.BlockSpec((count, rank, block), lambda i, r: (0, 0, i))
    return pl.pallas_call(
        local_kernel,
        grid_spec=pltpu.PrefetchScalarGridSpec(
            num_scalar_prefetch=1,
            grid=(steps,),
            in_specs=[
                pl.BlockSpec((1, count, rank, block), lambda i, r: (0, 0, 0, part * steps + i)),
                mats,
                mats,
            ],
            out_specs=[out, out],
        ),
        out_shape=[jax.ShapeDtypeStruct((count, rank, width), F32)] * 2,
        compiler_params=params(),
        cost_estimate=SMALL,
        name=f"local_part{part}",
    )(ranks, coefficients, self_weights, cross_weights)


def level3_kernel(node, info, kept, recv, self_w, cross_w, keep_out, send_out):
    parts = split(masked(info[node], kept[0] + recv[0]))
    mine = times(self_w[0, 0, 0], parts)
    other = times(cross_w[0, 0, 0], parts)
    flag = info[4]

    @pl.when(flag == 0)
    def _():
        keep_out[...] = mine
        send_out[...] = other

    @pl.when(flag != 0)
    def _():
        keep_out[...] = other
        send_out[...] = mine


def level3(node, part, info, kept, recv, self_weights, cross_weights):
    _, rank, width = kept.shape
    block = 256
    tile = pl.BlockSpec((1, rank, block), lambda i, r: (node, 0, i))
    mat = pl.BlockSpec((1, 1, 1, rank, rank), lambda i, r: (0, 3, node, 0, 0))
    out = pl.BlockSpec((rank, block), lambda i, r: (0, i))
    return pl.pallas_call(
        lambda *refs: level3_kernel(node, *refs),
        grid_spec=pltpu.PrefetchScalarGridSpec(
            num_scalar_prefetch=1,
            grid=(width // block,),
            in_specs=[tile, tile, mat, mat],
            out_specs=[out, out],
        ),
        out_shape=[jax.ShapeDtypeStruct((rank, width), F32)] * 2,
        compiler_params=params(),
        cost_estimate=SMALL,
        name=f"level3_{node}{part}",
    )(info, kept, recv, self_weights, cross_weights)


def moved_kernel(node, info, kept, recv, self_w, cross_w, moved, keep_out, send_out, mats):
    @pl.when(pl.program_id(0) == 0)
    def _():
        @pl.when(info[4] == 0)
        def _():
            mats[0] = self_w[0, 0, 0]
            mats[1] = cross_w[0, 0, 0]

        @pl.when(info[4] != 0)
        def _():
            mats[0] = moved[0].astype(BF16)
            mats[1] = moved[1].astype(BF16)

    parts = split(masked(info[node], kept[...] + recv[...]))
    keep_out[...] = times(mats[0], parts)
    send_out[...] = times(mats[1], parts)


def moved_level(level, node, part, info, kept, recv, self_weights, cross_weights, moved):
    rank, width = kept.shape
    block = 256
    tile = pl.BlockSpec((rank, block), lambda i, r: (0, i))
    mat = pl.BlockSpec((1, 1, 1, rank, rank), lambda i, r: (0, level, node, 0, 0))
    return pl.pallas_call(
        lambda *refs: moved_kernel(node, *refs),
        grid_spec=pltpu.PrefetchScalarGridSpec(
            num_scalar_prefetch=1,
            grid=(width // block,),
            in_specs=[tile, tile, mat, mat, pl.BlockSpec((2, rank, rank), lambda i, r: (0, 0, 0))],
            out_specs=[tile, tile],
            scratch_shapes=[pltpu.VMEM((2, rank, rank), BF16)],
        ),
        out_shape=[jax.ShapeDtypeStruct((rank, width), F32)] * 2,
        compiler_params=params(),
        cost_estimate=SMALL,
        name=f"level{level}_{node}{part}",
    )(info, kept, recv, self_weights, cross_weights, moved)


def halve_kernel(node, spot, info, kept_a, recv_a, kept_b, recv_b, keep_out, send_out):
    for kept, recv, out in ((kept_a, recv_a, keep_out), (kept_b, recv_b, send_out)):
        total = kept[...] + recv[...]
        out[...] = total if node is None else masked(info[node], total)


def halve(node, spot, info, kept, recv):
    rank, width = kept.shape
    block = width // 2
    mine = pl.BlockSpec((rank, block), lambda i, s, r: (0, s[0]))
    theirs = pl.BlockSpec((rank, block), lambda i, s, r: (0, s[1]))
    out = pl.BlockSpec((rank, block), lambda i, s, r: (0, 0))
    return pl.pallas_call(
        lambda *refs: halve_kernel(node, *refs),
        grid_spec=pltpu.PrefetchScalarGridSpec(
            num_scalar_prefetch=2,
            grid=(1,),
            in_specs=[mine, mine, theirs, theirs],
            out_specs=[out, out],
        ),
        out_shape=[jax.ShapeDtypeStruct((rank, block), F32)] * 2,
        compiler_params=params(),
        cost_estimate=SMALL,
        name="halve",
    )(spot, info, kept, recv, kept, recv)


def swap(value, axis, mask, chosen=lambda index: True):
    pairs = [(i, i ^ mask) for i in range(lax.axis_size(axis)) if chosen(i)]
    return lax.ppermute(value, axis, pairs)


def tie(value, *before):
    return lax.optimization_barrier((value, *before))[0]


CORE, Z1, Z2, X0 = 1, 2, 4, 8
PARTS = 2


def moves(index):
    return (index & 1) == ((index >> 2) & 1)


def shards(coefficients, self_weights, cross_weights, true_ranks):
    ranks = true_ranks[0]
    count = ranks.shape[0]
    nodes, cols = lax.axis_size("node"), lax.axis_size("col")
    flag = moves(lax.axis_index("node")).astype(jnp.int32)
    col = lax.axis_index("col")
    y0, y1, z0 = col & 1, (col >> 1) & 1, (col >> 2) & 1
    spot_y1 = jnp.stack([y1, 1 - y1]).astype(jnp.int32)
    spot_y0 = jnp.stack([y0, 1 - y0]).astype(jnp.int32)

    held = jnp.where(flag == 1, swap(ranks, "node", Z1, moves), ranks)
    own_info = jnp.concatenate([ranks, flag[None]])
    held_info = jnp.concatenate([held, flag[None]])

    def wide(level, node):
        pair = jnp.stack([self_weights[0, level, node], cross_weights[0, level, node]])
        return pair.astype(F32)

    def fetch(level, node, *before):
        return swap(tie(wide(level, node), *before), "node", Z1, moves)

    early = [(4, 0), (5, 0), (4, 1)]
    start_ranks, *mats = lax.optimization_barrier((ranks, *[wide(*key) for key in early]))
    moved = {key: swap(mat, "node", Z1, moves) for key, mat in zip(early, mats)}
    later = [(5, 1), (4, 2), (5, 2), (4, 3), (5, 3)]

    first = []
    for part in range(PARTS):
        k, s = local_levels(part, PARTS, coefficients, self_weights, cross_weights, start_ranks)
        first.append((k, swap(s, "node", CORE)))

    pieces = [(node, part) for node in range(count) for part in range(PARTS)]
    gates = [moved[4, 0], moved[5, 0]]
    done = {}

    def past(*keys):
        return [done[key] for key in keys if key in done]

    sums, results = {}, []
    for turn, (node, part) in enumerate(pieces):
        k, s = level3(node, part, own_info, *first[part], self_weights, cross_weights)
        gates += past((5, turn - 4), (6, turn - 5), (7, turn - 6))
        s = tie(s, *gates)
        if turn < len(later):
            moved[later[turn]] = fetch(*later[turn], *gates)
        r = swap(s, "node", Z1)
        gates = [r, moved[4, 1]] if turn == 0 else [r]
        if turn < len(later):
            gates.append(moved[later[turn]])
        k, s = moved_level(4, node, part, held_info, k, r, self_weights, cross_weights, moved[4, node])
        s = tie(s, *past((4, turn - 2)))
        r = done[4, turn] = swap(s, "node", Z1 | Z2)
        k, s = moved_level(5, node, part, held_info, k, r, self_weights, cross_weights, moved[5, node])
        r = done[5, turn] = swap(s, "node", X0)
        k, s = halve(node, spot_y1, held_info, k, r)
        r = done[6, turn] = swap(s, "col", 2)
        k, s = halve(None, spot_y0, held_info, k, r)
        r = done[7, turn] = swap(s, "col", 1)
        sums[part] = k + r
        if part == PARTS - 1:
            mine = jnp.where(z0 == 1, sums[1], sums[0])
            theirs = jnp.where(z0 == 1, sums[0], sums[1])
            home, across = [], []
            for d in range(nodes):
                for c in range(cols):
                    to = d ^ Z1 if moves(d) else d
                    across.append((d * cols + c, to * cols + (c ^ 4)))
                    if moves(d):
                        home.append((d * cols + c, to * cols + c))
            away = lax.ppermute(mine, ("node", "col"), home)
            other = lax.ppermute(theirs, ("node", "col"), across)
            results.append(jnp.where(flag == 1, away, mine) + other)
    return jnp.stack(results)


def solution(mesh):
    placed = (
        P("col", "node", None, None),
        P("col", None, "node", None, None),
        P("col", None, "node", None, None),
        P("col", "node"),
    )
    return jax.shard_map(
        shards, mesh=mesh, in_specs=placed, out_specs=P("node", None, "col"), check_vma=False
    )
```

time: 581 us -> 467 us (0.80); the launches traced: 581 us -> 458 us
  waiting for transfers between devices: 452 us -> 183 us
  starting transfers between devices: 11.4 us -> 142 us
  Pallas kernels: 0 us -> 98.5 us
  blocking collectives: 51.9 us -> 0 us
  matrix products: 46.3 us -> 0 us
  local copies, waits for them, and re-layouts: 14.9 us -> 26.8 us
    ppermute x4 -> x59, waiting for transfers between devices: 452 us -> 183 us  [the longest x51 177 us: swap(): return lax.ppermute(value, axis, pairs)]
    ppermute x4 -> x59, starting transfers between devices: 11.4 us -> 142 us  [the longest x51 118 us: swap(): return lax.ppermute(value, axis, pairs)]
    pallas_call x0 -> x42, Pallas kernels: none -> 98.5 us  [the longest x16 44.2 us: moved_level(): pl.pallas_call(lambda *refs: moved_kernel(node, *refs), grid_spec=pltpu.P...]
    all_to_all x1 -> x0, blocking collectives: 51.9 us -> none  [sum_at_owner(): lax.all_to_all(cut_along(array, dim, count), axis, 0, 0, tiled=True)]
    dot_general x12 -> x0, matrix products: 46.3 us -> none  [apply_mats(): jnp.einsum('nrk,nki->nri', weights.astype(jnp.float32), coeffs, precision...]
    unnamed x6 -> x146, local copies, waits for them, and re-layouts: 0.01 us -> 22.7 us
    rev x2 -> x0, local copies, waits for them, and re-layouts: 9.45 us -> none  [partner_view(): return shaped[:, ::-1].reshape(values.shape)]
  transfers between devices with their start and end apart: 4 -> 59, of which waited for: 4 -> 21; matrix products, arithmetic and copies ran while one was open for 1% -> 1% of each run, Pallas kernels for 0% -> 20%
where the time goes in v1:
time: 467 us; the launch traced here: 458 us
  waiting for transfers between devices  183 us (39%)
  starting transfers between devices  142 us (30%)
  Pallas kernels  98.5 us (21%)
  local copies, waits for them, and re-layouts  26.8 us (6%)
  other arithmetic  5.98 us (1%)
    ppermute x51, waiting for transfers between devices, swap(): return lax.ppermute(value, axis, pairs)  177 us
    ppermute x51, starting transfers between devices, swap(): return lax.ppermute(value, axis, pairs)  118 us
    pallas_call x16, Pallas kernels, moved_level(): pl.pallas_call(lambda *refs: moved_kernel(node, *refs), grid_spec=pltpu.P...  44.2 us
    pallas_call x8, Pallas kernels, level3(): pl.pallas_call(lambda *refs: level3_kernel(node, *refs), grid_spec=pltpu....  24.1 us
    unnamed x146, local copies, waits for them, and re-layouts  22.7 us
    ppermute x4, starting transfers between devices, shards(): away = lax.ppermute(mine, ('node', 'col'), home)  17.8 us
    pallas_call x2, Pallas kernels, local_levels(): pl.pallas_call(local_kernel, grid_spec=pltpu.PrefetchScalarGridSpec(num_s...  16.2 us
    pallas_call x16, Pallas kernels, halve(): pl.pallas_call(lambda *refs: halve_kernel(node, *refs), grid_spec=pltpu.P...  14 us
  transfers between devices with their start and end apart: 59, of which 21 were waited for; matrix products, arithmetic and copies ran while one was open for 1% of the time, Pallas kernels for 20%

profile of v1, /device:TPU:2, one launch (start us, length us, event | category | flops | bytes accessed | tf_op | source)
XLA Modules:
  0.0 458.1 jit_solution(7956578944404036126)
XLA Ops:
  6.0 8.0 %local_part0.1 = (f32[4,256,512]{2,1,0:T(8,128)S(1)}, f32[4,256,512]{2,1,0:T(8,128)}) custom-call(s32[4]{0:T(128)S(1)} %bitcast.47, f32[1,4,256,1024]{3,2,1,0:T(8,128)} %state.3, bf16[1,6,4,256,256]{4,3,2,1,0:T(8,128)(2,1)} %refs_3_.47, bf16[1,6,4,256,256]{4,3,2,1,0:T(8,128)(2,1)} %refs_4_.47), custom_call_target="tpu_custom_call" | custom-call | flops 1000 | bytes 1000 | tf_op jit(solution)/shard_map/local_part0/pallas_call | solution.py:57
  14.1 8.2 %local_part1.1 = (f32[4,256,512]{2,1,0:T(8,128)S(1)}, f32[4,256,512]{2,1,0:T(8,128)}) custom-call(s32[4]{0:T(128)S(1)} %bitcast.48, f32[1,4,256,1024]{3,2,1,0:T(8,128)} %state.3, bf16[1,6,4,256,256]{4,3,2,1,0:T(8,128)(2,1)} %refs_3_.47, bf16[1,6,4,256,256]{4,3,2,1,0:T(8,128)(2,1)} %refs_4_.47), custom_call_target="tpu_custom_call" | custom-call | flops 1000 | bytes 1000 | tf_op jit(solution)/shard_map/local_part1/pallas_call | solution.py:57
  22.6 5.2 %collective-permute-start.3 = (f32[2,256,256]{2,1,0:T(8,128)}, f32[2,256,256]{2,1,0:T(8,128)}, u32[]{:S(2)}, u32[]{:S(2)}) collective-permute-start(f32[2,256,256]{2,1,0:T(8,128)} %get-tuple-element.120), channel_id=1, source_target_pairs={{0,16},{16,0},{40,56},{56,40},{64,80},{80,64},{104,120},{120,104},... | collective-permute-start | bytes 1572872 | tf_op jit(solution)/shard_map/ppermute | solution.py:182
  29.7 4.8 %collective-permute-start.6 = (f32[2,256,256]{2,1,0:T(8,128)}, f32[2,256,256]{2,1,0:T(8,128)S(1)}, u32[]{:S(2)}, u32[]{:S(2)}) collective-permute-start(f32[2,256,256]{2,1,0:T(8,128)} %maximum_convert_fusion.2), channel_id=1, source_target_pairs={{0,16},{16,0},{40,56},{56,40},{64,80},{80,64},{104,120},{120,104},... | collective-permute-start | bytes 1572872 | tf_op jit(solution)/shard_map/ppermute | solution.py:182
  35.6 26.2 %collective-permute-done.3.refs_5_ = f32[2,256,256]{2,1,0:T(8,128)} collective-permute-done((f32[2,256,256]{2,1,0:T(8,128)}, f32[2,256,256]{2,1,0:T(8,128)}, u32[]{:S(2)}, u32[]{:S(2)}) %collective-permute-start.3) | collective-permute-done | bytes 524320 | tf_op jit(solution)/shard_map/ppermute | solution.py:182
  61.8 7.0 %collective-permute-done.4.refs_5_ = f32[2,256,256]{2,1,0:T(8,128)S(1)} collective-permute-done((f32[2,256,256]{2,1,0:T(8,128)}, f32[2,256,256]{2,1,0:T(8,128)S(1)}, u32[]{:S(2)}, u32[]{:S(2)}) %collective-permute-start.4) | collective-permute-done | bytes 524320 | tf_op jit(solution)/shard_map/ppermute | solution.py:182
  74.9 3.0 collective-permute-start.5
  78.7 3.1 level3_01.1
  86.1 5.3 %collective-permute-done.7.refs_5_ = f32[2,256,256]{2,1,0:T(8,128)S(1)} collective-permute-done((f32[2,256,256]{2,1,0:T(8,128)S(1)}, f32[2,256,256]{2,1,0:T(8,128)S(1)}, u32[]{:S(2)}, u32[]{:S(2)}) %collective-permute-start.7) | collective-permute-done | bytes 524320 | tf_op jit(solution)/shard_map/ppermute | solution.py:182
  92.2 16.0 %collective-permute-done.5.refs_2_ = f32[256,512]{1,0:T(8,128)S(1)} collective-permute-done((f32[256,512]{1,0:T(8,128)S(1)}, f32[256,512]{1,0:T(8,128)S(1)}, u32[]{:S(2)}, u32[]{:S(2)}) %collective-permute-start.5) | collective-permute-done | bytes 524320 | tf_op jit(solution)/shard_map/ppermute | solution.py:182
  109.0 4.8 %collective-permute-start.19 = (f32[2,256,256]{2,1,0:T(8,128)}, f32[2,256,256]{2,1,0:T(8,128)}, u32[]{:S(2)}, u32[]{:S(2)}) collective-permute-start(f32[2,256,256]{2,1,0:T(8,128)} %maximum_convert_fusion.4), channel_id=1, source_target_pairs={{0,16},{16,0},{40,56},{56,40},{64,80},{80,64},{104,120},{120,104},... | collective-permute-start | bytes 1572872 | tf_op jit(solution)/shard_map/ppermute | solution.py:182
  115.8 20.4 %collective-permute-done = s32[4]{0:T(128)S(1)} collective-permute-done((s32[4]{0:T(128)S(1)}, s32[4]{0:T(128)S(1)}, u32[]{:S(2)}, u32[]{:S(2)}) %collective-permute-start) | collective-permute-done | bytes 48 | tf_op jit(solution)/shard_map/ppermute | solution.py:182
  145.4 3.0 collective-permute-start.20
  154.7 12.0 %collective-permute-done.13.refs_2_ = f32[256,512]{1,0:T(8,128)S(1)} collective-permute-done((f32[256,512]{1,0:T(8,128)S(1)}, f32[256,512]{1,0:T(8,128)S(1)}, u32[]{:S(2)}, u32[]{:S(2)}) %collective-permute-start.13) | collective-permute-done | bytes 524320 | tf_op jit(solution)/shard_map/ppermute | solution.py:182
  172.1 9.7 %collective-permute-done.20.refs_2_ = f32[256,512]{1,0:T(8,128)S(1)} collective-permute-done((f32[256,512]{1,0:T(8,128)S(1)}, f32[256,512]{1,0:T(8,128)S(1)}, u32[]{:S(2)}, u32[]{:S(2)}) %collective-permute-start.20) | collective-permute-done | bytes 524320 | tf_op jit(solution)/shard_map/ppermute | solution.py:182
  182.1 4.8 %collective-permute-start.33 = (f32[2,256,256]{2,1,0:T(8,128)S(1)}, f32[2,256,256]{2,1,0:T(8,128)S(1)}, u32[]{:S(2)}, u32[]{:S(2)}) collective-permute-start(f32[2,256,256]{2,1,0:T(8,128)S(1)} %maximum_convert_fusion.6), channel_id=1, source_target_pairs={{0,16},{16,0},{40,56},{56,40},{64,80},{80,64},{104,120},{120,104},... | collective-permute-start | bytes 1572872 | tf_op jit(solution)/shard_map/ppermute | solution.py:182
  187.7 3.4 level3_20.1
  191.9 2.9 level5_01.1
  195.7 3.8 collective-permute-start.10
  199.5 2.9 level4_10.1
  204.0 6.0 %collective-permute-done.22.refs_2_ = f32[256,512]{1,0:T(8,128)S(1)} collective-permute-done((f32[256,512]{1,0:T(8,128)S(1)}, f32[256,512]{1,0:T(8,128)S(1)}, u32[]{:S(2)}, u32[]{:S(2)}) %collective-permute-start.22) | collective-permute-done | bytes 524320 | tf_op jit(solution)/shard_map/ppermute | solution.py:182
  210.8 24.8 %collective-permute-done.33.refs_5_ = f32[2,256,256]{2,1,0:T(8,128)S(1)} collective-permute-done((f32[2,256,256]{2,1,0:T(8,128)S(1)}, f32[2,256,256]{2,1,0:T(8,128)S(1)}, u32[]{:S(2)}, u32[]{:S(2)}) %collective-permute-start.33) | collective-permute-done | bytes 524320 | tf_op jit(solution)/shard_map/ppermute | solution.py:182
  238.4 3.0 collective-permute-start.34
  245.9 3.5 level3_21.1
  250.2 3.0 level4_11.1
  254.0 3.0 level5_10.1
  261.1 3.5 collective-permute-start.11
  266.2 12.6 %collective-permute-start.16 = (f32[256,128]{1,0:T(8,128)S(1)}, f32[256,128]{1,0:T(8,128)S(1)}, u32[]{:S(2)}, u32[]{:S(2)}) collective-permute-start(f32[256,128]{1,0:T(8,128)S(1)} %get-tuple-element.142), channel_id=1, source_target_pairs={{0,1},{1,0},{2,3},{3,2},{4,5},{5,4},{6,7},{7,6},{8,9},{9,8},{10,11... | collective-permute-start | bytes 393224 | tf_op jit(solution)/shard_map/ppermute | solution.py:182
  278.8 3.4 level3_30.1
  284.8 6.0 %collective-permute-done.36.refs_2_ = f32[256,512]{1,0:T(8,128)} collective-permute-done((f32[256,512]{1,0:T(8,128)}, f32[256,512]{1,0:T(8,128)}, u32[]{:S(2)}, u32[]{:S(2)}) %collective-permute-start.36) | collective-permute-done | bytes 524320 | tf_op jit(solution)/shard_map/ppermute | solution.py:182
  294.0 3.3 level4_20.1
  297.8 6.5 %collective-permute-start.12 = (f32[256,128]{1,0:T(8,128)S(1)}, f32[256,128]{1,0:T(8,128)S(1)}, u32[]{:S(2)}, u32[]{:S(2)}) collective-permute-start(f32[256,128]{1,0:T(8,128)S(1)} %get-tuple-element.133), channel_id=1, source_target_pairs={{0,1},{1,0},{2,3},{3,2},{4,5},{5,4},{6,7},{7,6},{8,9},{9,8},{10,11... | collective-permute-start | bytes 393224 | tf_op jit(solution)/shard_map/ppermute | solution.py:182
  309.8 11.9 %collective-permute-start.48 = (f32[256,512]{1,0:T(8,128)S(1)}, f32[256,512]{1,0:T(8,128)S(1)}, u32[]{:S(2)}, u32[]{:S(2)}) collective-permute-start(f32[256,512]{1,0:T(8,128)S(1)} %get-tuple-element.199), channel_id=1, source_target_pairs={{0,16},{8,24},{16,0},{24,8},{32,48},{40,56},{48,32},{56,40},{64,80... | collective-permute-start | bytes 1572872 | tf_op jit(solution)/shard_map/ppermute | solution.py:182
  321.7 4.1 collective-permute-start.37
  330.3 3.5 collective-permute-done.48.refs_2_
  336.1 25.4 %collective-permute-done.37.refs_2_ = f32[256,512]{1,0:T(8,128)S(1)} collective-permute-done((f32[256,512]{1,0:T(8,128)S(1)}, f32[256,512]{1,0:T(8,128)S(1)}, u32[]{:S(2)}, u32[]{:S(2)}) %collective-permute-start.37) | collective-permute-done | bytes 524320 | tf_op jit(solution)/shard_map/ppermute | solution.py:182
  361.5 4.6 %collective-permute-start.49 = (f32[256,512]{1,0:T(8,128)S(1)}, f32[256,512]{1,0:T(8,128)S(1)}, u32[]{:S(2)}, u32[]{:S(2)}) collective-permute-start(f32[256,512]{1,0:T(8,128)S(1)} %get-tuple-element.202), channel_id=1, source_target_pairs={{0,48},{8,56},{16,32},{24,40},{32,16},{40,24},{48,0},{56,8},{64,11... | collective-permute-start | bytes 1572872 | tf_op jit(solution)/shard_map/ppermute | solution.py:182
  366.1 3.0 level5_20.1
  374.8 3.1 level5_30.1
  379.9 3.1 collective-permute-start.25
  383.1 3.2 level5_31.1
  390.2 3.0 collective-permute-start.30
  400.2 5.2 %collective-permute-start.17 = (f32[256,128]{1,0:T(8,128)S(1)}, f32[256,128]{1,0:T(8,128)S(1)}, u32[]{:S(2)}, u32[]{:S(2)}) collective-permute-start(f32[256,128]{1,0:T(8,128)S(1)} %get-tuple-element.235), channel_id=1, source_target_pairs={{0,16},{1,17},{2,18},{3,19},{4,20},{5,21},{6,22},{7,23},{16,0},{17... | collective-permute-start | bytes 393224 | tf_op jit(solution)/shard_map/ppermute | solution.py:266
  412.9 8.8 %collective-permute-start.31 = (f32[256,128]{1,0:T(8,128)S(1)}, f32[256,128]{1,0:T(8,128)S(1)}, u32[]{:S(2)}, u32[]{:S(2)}) collective-permute-start(f32[256,128]{1,0:T(8,128)S(1)} %get-tuple-element.237), channel_id=1, source_target_pairs={{0,16},{1,17},{2,18},{3,19},{4,20},{5,21},{6,22},{7,23},{16,0},{17... | collective-permute-start | bytes 393224 | tf_op jit(solution)/shard_map/ppermute | solution.py:266
  422.6 3.5 collective-permute-start.51
  436.5 3.1 collective-permute-start.52
  442.7 4.7 %collective-permute-start.46 = (f32[256,128]{1,0:T(8,128)S(1)}, f32[256,128]{1,0:T(8,128)S(1)}, u32[]{:S(2)}, u32[]{:S(2)}) collective-permute-start(f32[256,128]{1,0:T(8,128)S(1)} %get-tuple-element.240), channel_id=1, source_target_pairs={{0,20},{1,21},{2,22},{3,23},{4,16},{5,17},{6,18},{7,19},{8,12},{9,... | collective-permute-start | bytes 393224 | tf_op jit(solution)/shard_map/ppermute | solution.py:267
  451.8 5.2 %collective-permute-done.57 = f32[256,128]{1,0:T(8,128)S(1)} collective-permute-done((f32[256,128]{1,0:T(8,128)S(1)}, f32[256,128]{1,0:T(8,128)S(1)}, u32[]{:S(2)}, u32[]{:S(2)}) %collective-permute-start.57) | collective-permute-done | bytes 131104 | tf_op jit(solution)/shard_map/ppermute | solution.py:266
  (281 shorter events, 128.3 us)
Async XLA Ops:
  14.1 56.7 %collective-permute-start.2 = (f32[4,256,512]{2,1,0:T(8,128)}, f32[4,256,512]{2,1,0:T(8,128)}, u32[]{:S(2)}, u32[]{:S(2)}) collective-permute-start(f32[4,256,512]{2,1,0:T(8,128)} %get-tuple-element.118), channel_id=1, source_target_pairs={{0,8},{8,0},{16,24},{24,16},{32,40},{40,32},{48,56},{56,48},{64,72... | collective-permute-start | bytes 6291464 | tf_op jit(solution)/shard_map/ppermute | solution.py:182
  22.3 56.5 %collective-permute-start.1 = (f32[4,256,512]{2,1,0:T(8,128)}, f32[4,256,512]{2,1,0:T(8,128)}, u32[]{:S(2)}, u32[]{:S(2)}) collective-permute-start(f32[4,256,512]{2,1,0:T(8,128)} %get-tuple-element.114), channel_id=1, source_target_pairs={{0,8},{8,0},{16,24},{24,16},{32,40},{40,32},{48,56},{56,48},{64,72... | collective-permute-start | bytes 6291464 | tf_op jit(solution)/shard_map/ppermute | solution.py:182
  22.6 39.2 %collective-permute-start.3 = (f32[2,256,256]{2,1,0:T(8,128)}, f32[2,256,256]{2,1,0:T(8,128)}, u32[]{:S(2)}, u32[]{:S(2)}) collective-permute-start(f32[2,256,256]{2,1,0:T(8,128)} %get-tuple-element.120), channel_id=1, source_target_pairs={{0,16},{16,0},{40,56},{56,40},{64,80},{80,64},{104,120},{120,104},... | collective-permute-start | bytes 1572872 | tf_op jit(solution)/shard_map/ppermute | solution.py:182
  27.8 41.1 %collective-permute-start.4 = (f32[2,256,256]{2,1,0:T(8,128)}, f32[2,256,256]{2,1,0:T(8,128)S(1)}, u32[]{:S(2)}, u32[]{:S(2)}) collective-permute-start(f32[2,256,256]{2,1,0:T(8,128)} %get-tuple-element.121), channel_id=1, source_target_pairs={{0,16},{16,0},{40,56},{56,40},{64,80},{80,64},{104,120},{120,104},... | collective-permute-start | bytes 1572872 | tf_op jit(solution)/shard_map/ppermute | solution.py:182
  29.7 55.5 %collective-permute-start.6 = (f32[2,256,256]{2,1,0:T(8,128)}, f32[2,256,256]{2,1,0:T(8,128)S(1)}, u32[]{:S(2)}, u32[]{:S(2)}) collective-permute-start(f32[2,256,256]{2,1,0:T(8,128)} %maximum_convert_fusion.2), channel_id=1, source_target_pairs={{0,16},{16,0},{40,56},{56,40},{64,80},{80,64},{104,120},{120,104},... | collective-permute-start | bytes 1572872 | tf_op jit(solution)/shard_map/ppermute | solution.py:182
  68.9 22.5 %collective-permute-start.7 = (f32[2,256,256]{2,1,0:T(8,128)S(1)}, f32[2,256,256]{2,1,0:T(8,128)S(1)}, u32[]{:S(2)}, u32[]{:S(2)}) collective-permute-start(f32[2,256,256]{2,1,0:T(8,128)S(1)} %maximum_convert_fusion.3), channel_id=1, source_target_pairs={{0,16},{16,0},{40,56},{56,40},{64,80},{80,64},{104,120},{120,104},... | collective-permute-start | bytes 1572872 | tf_op jit(solution)/shard_map/ppermute | solution.py:182
  74.9 33.3 %collective-permute-start.5 = (f32[256,512]{1,0:T(8,128)S(1)}, f32[256,512]{1,0:T(8,128)S(1)}, u32[]{:S(2)}, u32[]{:S(2)}) collective-permute-start(f32[256,512]{1,0:T(8,128)S(1)} %get-tuple-element.122), channel_id=1, source_target_pairs={{0,16},{8,24},{16,0},{24,8},{32,48},{40,56},{48,32},{56,40},{64,80... | collective-permute-start | bytes 1572872 | tf_op jit(solution)/shard_map/ppermute | solution.py:182
  109.0 34.5 %collective-permute-start.8 = (f32[256,512]{1,0:T(8,128)}, f32[256,512]{1,0:T(8,128)}, u32[]{:S(2)}, u32[]{:S(2)}) collective-permute-start(f32[256,512]{1,0:T(8,128)} %get-tuple-element.125), channel_id=1, source_target_pairs={{0,16},{8,24},{16,0},{24,8},{32,48},{40,56},{48,32},{56,40},{64,80... | collective-permute-start | bytes 1572872 | tf_op jit(solution)/shard_map/ppermute | solution.py:182
  109.0 34.5 %collective-permute-start.19 = (f32[2,256,256]{2,1,0:T(8,128)}, f32[2,256,256]{2,1,0:T(8,128)}, u32[]{:S(2)}, u32[]{:S(2)}) collective-permute-start(f32[2,256,256]{2,1,0:T(8,128)} %maximum_convert_fusion.4), channel_id=1, source_target_pairs={{0,16},{16,0},{40,56},{56,40},{64,80},{80,64},{104,120},{120,104},... | collective-permute-start | bytes 1572872 | tf_op jit(solution)/shard_map/ppermute | solution.py:182
  113.8 22.4 %collective-permute-start = (s32[4]{0:T(128)S(1)}, s32[4]{0:T(128)S(1)}, u32[]{:S(2)}, u32[]{:S(2)}) collective-permute-start(s32[4]{0:T(128)S(1)} %bitcast.50), channel_id=1, source_target_pairs={{0,16},{16,0},{40,56},{56,40},{64,80},{80,64},{104,120},{120,104},... | collective-permute-start | bytes 56 | tf_op jit(solution)/shard_map/ppermute | solution.py:182
  143.4 23.4 %collective-permute-start.13 = (f32[256,512]{1,0:T(8,128)S(1)}, f32[256,512]{1,0:T(8,128)S(1)}, u32[]{:S(2)}, u32[]{:S(2)}) collective-permute-start(f32[256,512]{1,0:T(8,128)S(1)} %get-tuple-element.136), channel_id=1, source_target_pairs={{0,48},{8,56},{16,32},{24,40},{32,16},{40,24},{48,0},{56,8},{64,11... | collective-permute-start | bytes 1572872 | tf_op jit(solution)/shard_map/ppermute | solution.py:182
  143.5 28.6 %collective-permute-start.21 = (f32[2,256,256]{2,1,0:T(8,128)S(1)}, f32[2,256,256]{2,1,0:T(8,128)S(1)}, u32[]{:S(2)}, u32[]{:S(2)}) collective-permute-start(f32[2,256,256]{2,1,0:T(8,128)S(1)} %maximum_convert_fusion.5), channel_id=1, source_target_pairs={{0,16},{16,0},{40,56},{56,40},{64,80},{80,64},{104,120},{120,104},... | collective-permute-start | bytes 1572872 | tf_op jit(solution)/shard_map/ppermute | solution.py:182
  145.4 36.4 %collective-permute-start.20 = (f32[256,512]{1,0:T(8,128)S(1)}, f32[256,512]{1,0:T(8,128)S(1)}, u32[]{:S(2)}, u32[]{:S(2)}) collective-permute-start(f32[256,512]{1,0:T(8,128)S(1)} %get-tuple-element.147), channel_id=1, source_target_pairs={{0,16},{8,24},{16,0},{24,8},{32,48},{40,56},{48,32},{56,40},{64,80... | collective-permute-start | bytes 1572872 | tf_op jit(solution)/shard_map/ppermute | solution.py:182
  154.6 37.3 %collective-permute-start.9 = (f32[256,512]{1,0:T(8,128)S(1)}, f32[256,512]{1,0:T(8,128)S(1)}, u32[]{:S(2)}, u32[]{:S(2)}) collective-permute-start(f32[256,512]{1,0:T(8,128)S(1)} %get-tuple-element.127), channel_id=1, source_target_pairs={{0,48},{8,56},{16,32},{24,40},{32,16},{40,24},{48,0},{56,8},{64,11... | collective-permute-start | bytes 1572872 | tf_op jit(solution)/shard_map/ppermute | solution.py:182
  169.9 33.4 %collective-permute-start.14 = (f32[256,512]{1,0:T(8,128)S(1)}, f32[256,512]{1,0:T(8,128)S(1)}, u32[]{:S(2)}, u32[]{:S(2)}) collective-permute-start(f32[256,512]{1,0:T(8,128)S(1)} %get-tuple-element.138), channel_id=1, source_target_pairs={{0,64},{8,72},{16,80},{24,88},{32,96},{40,104},{48,112},{56,120},{... | collective-permute-start | bytes 1572872 | tf_op jit(solution)/shard_map/ppermute | solution.py:182
  181.8 28.2 %collective-permute-start.22 = (f32[256,512]{1,0:T(8,128)S(1)}, f32[256,512]{1,0:T(8,128)S(1)}, u32[]{:S(2)}, u32[]{:S(2)}) collective-permute-start(f32[256,512]{1,0:T(8,128)S(1)} %get-tuple-element.149), channel_id=1, source_target_pairs={{0,16},{8,24},{16,0},{24,8},{32,48},{40,56},{48,32},{56,40},{64,80... | collective-permute-start | bytes 1572872 | tf_op jit(solution)/shard_map/ppermute | solution.py:182
  182.1 53.6 %collective-permute-start.33 = (f32[2,256,256]{2,1,0:T(8,128)S(1)}, f32[2,256,256]{2,1,0:T(8,128)S(1)}, u32[]{:S(2)}, u32[]{:S(2)}) collective-permute-start(f32[2,256,256]{2,1,0:T(8,128)S(1)} %maximum_convert_fusion.6), channel_id=1, source_target_pairs={{0,16},{16,0},{40,56},{56,40},{64,80},{80,64},{104,120},{120,104},... | collective-permute-start | bytes 1572872 | tf_op jit(solution)/shard_map/ppermute | solution.py:182
  195.7 63.0 %collective-permute-start.10 = (f32[256,512]{1,0:T(8,128)}, f32[256,512]{1,0:T(8,128)}, u32[]{:S(2)}, u32[]{:S(2)}) collective-permute-start(f32[256,512]{1,0:T(8,128)} %get-tuple-element.129), channel_id=1, source_target_pairs={{0,64},{8,72},{16,80},{24,88},{32,96},{40,104},{48,112},{56,120},{... | collective-permute-start | bytes 1572872 | tf_op jit(solution)/shard_map/ppermute | solution.py:182
  203.2 50.7 %collective-permute-start.27 = (f32[256,512]{1,0:T(8,128)}, f32[256,512]{1,0:T(8,128)}, u32[]{:S(2)}, u32[]{:S(2)}) collective-permute-start(f32[256,512]{1,0:T(8,128)} %get-tuple-element.162), channel_id=1, source_target_pairs={{0,48},{8,56},{16,32},{24,40},{32,16},{40,24},{48,0},{56,8},{64,11... | collective-permute-start | bytes 1572872 | tf_op jit(solution)/shard_map/ppermute | solution.py:182
  236.5 22.2 %collective-permute-start.35 = (f32[2,256,256]{2,1,0:T(8,128)}, f32[2,256,256]{2,1,0:T(8,128)}, u32[]{:S(2)}, u32[]{:S(2)}) collective-permute-start(f32[2,256,256]{2,1,0:T(8,128)} %maximum_convert_fusion.7), channel_id=1, source_target_pairs={{0,16},{16,0},{40,56},{56,40},{64,80},{80,64},{104,120},{120,104},... | collective-permute-start | bytes 1572872 | tf_op jit(solution)/shard_map/ppermute | solution.py:182
  238.4 20.3 %collective-permute-start.34 = (f32[256,512]{1,0:T(8,128)}, f32[256,512]{1,0:T(8,128)}, u32[]{:S(2)}, u32[]{:S(2)}) collective-permute-start(f32[256,512]{1,0:T(8,128)} %get-tuple-element.173), channel_id=1, source_target_pairs={{0,16},{8,24},{16,0},{24,8},{32,48},{40,56},{48,32},{56,40},{64,80... | collective-permute-start | bytes 1572872 | tf_op jit(solution)/shard_map/ppermute | solution.py:182
  244.2 12.8 %collective-permute-start.15 = (f32[256,256]{1,0:T(8,128)S(1)}, f32[256,256]{1,0:T(8,128)S(1)}, u32[]{:S(2)}, u32[]{:S(2)}) collective-permute-start(f32[256,256]{1,0:T(8,128)S(1)} %get-tuple-element.140), channel_id=1, source_target_pairs={{0,2},{1,3},{2,0},{3,1},{4,6},{5,7},{6,4},{7,5},{8,10},{9,11},{10,... | collective-permute-start | bytes 786440 | tf_op jit(solution)/shard_map/ppermute | solution.py:182
  254.0 28.3 %collective-permute-start.23 = (f32[256,512]{1,0:T(8,128)}, f32[256,512]{1,0:T(8,128)}, u32[]{:S(2)}, u32[]{:S(2)}) collective-permute-start(f32[256,512]{1,0:T(8,128)} %get-tuple-element.152), channel_id=1, source_target_pairs={{0,48},{8,56},{16,32},{24,40},{32,16},{40,24},{48,0},{56,8},{64,11... | collective-permute-start | bytes 1572872 | tf_op jit(solution)/shard_map/ppermute | solution.py:182
  257.0 27.7 %collective-permute-start.28 = (f32[256,512]{1,0:T(8,128)}, f32[256,512]{1,0:T(8,128)S(1)}, u32[]{:S(2)}, u32[]{:S(2)}) collective-permute-start(f32[256,512]{1,0:T(8,128)} %get-tuple-element.164), channel_id=1, source_target_pairs={{0,64},{8,72},{16,80},{24,88},{32,96},{40,104},{48,112},{56,120},{... | collective-permute-start | bytes 1572872 | tf_op jit(solution)/shard_map/ppermute | solution.py:182
  258.7 32.2 %collective-permute-start.36 = (f32[256,512]{1,0:T(8,128)}, f32[256,512]{1,0:T(8,128)}, u32[]{:S(2)}, u32[]{:S(2)}) collective-permute-start(f32[256,512]{1,0:T(8,128)} %get-tuple-element.175), channel_id=1, source_target_pairs={{0,16},{8,24},{16,0},{24,8},{32,48},{40,56},{48,32},{56,40},{64,80... | collective-permute-start | bytes 1572872 | tf_op jit(solution)/shard_map/ppermute | solution.py:182
  261.1 23.7 %collective-permute-start.11 = (f32[256,256]{1,0:T(8,128)}, f32[256,256]{1,0:T(8,128)S(1)}, u32[]{:S(2)}, u32[]{:S(2)}) collective-permute-start(f32[256,256]{1,0:T(8,128)} %get-tuple-element.131), channel_id=1, source_target_pairs={{0,2},{1,3},{2,0},{3,1},{4,6},{5,7},{6,4},{7,5},{8,10},{9,11},{10,... | collective-permute-start | bytes 786440 | tf_op jit(solution)/shard_map/ppermute | solution.py:182
  266.2 18.5 %collective-permute-start.16 = (f32[256,128]{1,0:T(8,128)S(1)}, f32[256,128]{1,0:T(8,128)S(1)}, u32[]{:S(2)}, u32[]{:S(2)}) collective-permute-start(f32[256,128]{1,0:T(8,128)S(1)} %get-tuple-element.142), channel_id=1, source_target_pairs={{0,1},{1,0},{2,3},{3,2},{4,5},{5,4},{6,7},{7,6},{8,9},{9,8},{10,11... | collective-permute-start | bytes 393224 | tf_op jit(solution)/shard_map/ppermute | solution.py:182
  284.6 25.2 %collective-permute-start.24 = (f32[256,512]{1,0:T(8,128)S(1)}, f32[256,512]{1,0:T(8,128)S(1)}, u32[]{:S(2)}, u32[]{:S(2)}) collective-permute-start(f32[256,512]{1,0:T(8,128)S(1)} %get-tuple-element.154), channel_id=1, source_target_pairs={{0,64},{8,72},{16,80},{24,88},{32,96},{40,104},{48,112},{56,120},{... | collective-permute-start | bytes 1572872 | tf_op jit(solution)/shard_map/ppermute | solution.py:182
  290.8 19.0 %collective-permute-start.47 = (f32[256,512]{1,0:T(8,128)}, f32[256,512]{1,0:T(8,128)S(1)}, u32[]{:S(2)}, u32[]{:S(2)}) collective-permute-start(f32[256,512]{1,0:T(8,128)} %get-tuple-element.198), channel_id=1, source_target_pairs={{0,16},{8,24},{16,0},{24,8},{32,48},{40,56},{48,32},{56,40},{64,80... | collective-permute-start | bytes 1572872 | tf_op jit(solution)/shard_map/ppermute | solution.py:182
  291.4 18.3 %collective-permute-start.29 = (f32[256,256]{1,0:T(8,128)S(1)}, f32[256,256]{1,0:T(8,128)S(1)}, u32[]{:S(2)}, u32[]{:S(2)}) collective-permute-start(f32[256,256]{1,0:T(8,128)S(1)} %get-tuple-element.166), channel_id=1, source_target_pairs={{0,2},{1,3},{2,0},{3,1},{4,6},{5,7},{6,4},{7,5},{8,10},{9,11},{10,... | collective-permute-start | bytes 786440 | tf_op jit(solution)/shard_map/ppermute | solution.py:182
  297.2 30.9 %collective-permute-start.41 = (f32[256,512]{1,0:T(8,128)}, f32[256,512]{1,0:T(8,128)S(1)}, u32[]{:S(2)}, u32[]{:S(2)}) collective-permute-start(f32[256,512]{1,0:T(8,128)} %get-tuple-element.188), channel_id=1, source_target_pairs={{0,48},{8,56},{16,32},{24,40},{32,16},{40,24},{48,0},{56,8},{64,11... | collective-permute-start | bytes 1572872 | tf_op jit(solution)/shard_map/ppermute | solution.py:182
  309.8 24.0 %collective-permute-start.48 = (f32[256,512]{1,0:T(8,128)S(1)}, f32[256,512]{1,0:T(8,128)S(1)}, u32[]{:S(2)}, u32[]{:S(2)}) collective-permute-start(f32[256,512]{1,0:T(8,128)S(1)} %get-tuple-element.199), channel_id=1, source_target_pairs={{0,16},{8,24},{16,0},{24,8},{32,48},{40,56},{48,32},{56,40},{64,80... | collective-permute-start | bytes 1572872 | tf_op jit(solution)/shard_map/ppermute | solution.py:182
  321.7 39.8 %collective-permute-start.37 = (f32[256,512]{1,0:T(8,128)S(1)}, f32[256,512]{1,0:T(8,128)S(1)}, u32[]{:S(2)}, u32[]{:S(2)}) collective-permute-start(f32[256,512]{1,0:T(8,128)S(1)} %get-tuple-element.178), channel_id=1, source_target_pairs={{0,48},{8,56},{16,32},{24,40},{32,16},{40,24},{48,0},{56,8},{64,11... | collective-permute-start | bytes 1572872 | tf_op jit(solution)/shard_map/ppermute | solution.py:182
  328.1 46.7 %collective-permute-start.53 = (f32[256,512]{1,0:T(8,128)S(1)}, f32[256,512]{1,0:T(8,128)S(1)}, u32[]{:S(2)}, u32[]{:S(2)}) collective-permute-start(f32[256,512]{1,0:T(8,128)S(1)} %get-tuple-element.212), channel_id=1, source_target_pairs={{0,48},{8,56},{16,32},{24,40},{32,16},{40,24},{48,0},{56,8},{64,11... | collective-permute-start | bytes 1572872 | tf_op jit(solution)/shard_map/ppermute | solution.py:182
  361.5 21.6 %collective-permute-start.49 = (f32[256,512]{1,0:T(8,128)S(1)}, f32[256,512]{1,0:T(8,128)S(1)}, u32[]{:S(2)}, u32[]{:S(2)}) collective-permute-start(f32[256,512]{1,0:T(8,128)S(1)} %get-tuple-element.202), channel_id=1, source_target_pairs={{0,48},{8,56},{16,32},{24,40},{32,16},{40,24},{48,0},{56,8},{64,11... | collective-permute-start | bytes 1572872 | tf_op jit(solution)/shard_map/ppermute | solution.py:182
  369.8 25.9 %collective-permute-start.42 = (f32[256,512]{1,0:T(8,128)}, f32[256,512]{1,0:T(8,128)}, u32[]{:S(2)}, u32[]{:S(2)}) collective-permute-start(f32[256,512]{1,0:T(8,128)} %get-tuple-element.190), channel_id=1, source_target_pairs={{0,64},{8,72},{16,80},{24,88},{32,96},{40,104},{48,112},{56,120},{... | collective-permute-start | bytes 1572872 | tf_op jit(solution)/shard_map/ppermute | solution.py:182
  372.7 24.7 %collective-permute-start.38 = (f32[256,512]{1,0:T(8,128)}, f32[256,512]{1,0:T(8,128)S(1)}, u32[]{:S(2)}, u32[]{:S(2)}) collective-permute-start(f32[256,512]{1,0:T(8,128)} %get-tuple-element.180), channel_id=1, source_target_pairs={{0,64},{8,72},{16,80},{24,88},{32,96},{40,104},{48,112},{56,120},{... | collective-permute-start | bytes 1572872 | tf_op jit(solution)/shard_map/ppermute | solution.py:182
  377.9 29.4 %collective-permute-start.54 = (f32[256,512]{1,0:T(8,128)}, f32[256,512]{1,0:T(8,128)S(1)}, u32[]{:S(2)}, u32[]{:S(2)}) collective-permute-start(f32[256,512]{1,0:T(8,128)} %get-tuple-element.214), channel_id=1, source_target_pairs={{0,64},{8,72},{16,80},{24,88},{32,96},{40,104},{48,112},{56,120},{... | collective-permute-start | bytes 1572872 | tf_op jit(solution)/shard_map/ppermute | solution.py:182
  386.2 26.7 %collective-permute-start.50 = (f32[256,512]{1,0:T(8,128)}, f32[256,512]{1,0:T(8,128)S(1)}, u32[]{:S(2)}, u32[]{:S(2)}) collective-permute-start(f32[256,512]{1,0:T(8,128)} %get-tuple-element.204), channel_id=1, source_target_pairs={{0,64},{8,72},{16,80},{24,88},{32,96},{40,104},{48,112},{56,120},{... | collective-permute-start | bytes 1572872 | tf_op jit(solution)/shard_map/ppermute | solution.py:182
  397.5 25.1 %collective-permute-start.43 = (f32[256,256]{1,0:T(8,128)S(1)}, f32[256,256]{1,0:T(8,128)S(1)}, u32[]{:S(2)}, u32[]{:S(2)}) collective-permute-start(f32[256,256]{1,0:T(8,128)S(1)} %get-tuple-element.192), channel_id=1, source_target_pairs={{0,2},{1,3},{2,0},{3,1},{4,6},{5,7},{6,4},{7,5},{8,10},{9,11},{10,... | collective-permute-start | bytes 786440 | tf_op jit(solution)/shard_map/ppermute | solution.py:182
  400.2 22.2 %collective-permute-start.17 = (f32[256,128]{1,0:T(8,128)S(1)}, f32[256,128]{1,0:T(8,128)S(1)}, u32[]{:S(2)}, u32[]{:S(2)}) collective-permute-start(f32[256,128]{1,0:T(8,128)S(1)} %get-tuple-element.235), channel_id=1, source_target_pairs={{0,16},{1,17},{2,18},{3,19},{4,20},{5,21},{6,22},{7,23},{16,0},{17... | collective-permute-start | bytes 393224 | tf_op jit(solution)/shard_map/ppermute | solution.py:266
  405.3 17.1 %collective-permute-start.18 = (f32[256,128]{1,0:T(8,128)S(1)}, f32[256,128]{1,0:T(8,128)S(1)}, u32[]{:S(2)}, u32[]{:S(2)}) collective-permute-start(f32[256,128]{1,0:T(8,128)S(1)} %get-tuple-element.236), channel_id=1, source_target_pairs={{0,20},{1,21},{2,22},{3,23},{4,16},{5,17},{6,18},{7,19},{8,12},{9,... | collective-permute-start | bytes 393224 | tf_op jit(solution)/shard_map/ppermute | solution.py:267
  407.3 19.4 %collective-permute-start.39 = (f32[256,256]{1,0:T(8,128)S(1)}, f32[256,256]{1,0:T(8,128)S(1)}, u32[]{:S(2)}, u32[]{:S(2)}) collective-permute-start(f32[256,256]{1,0:T(8,128)S(1)} %get-tuple-element.182), channel_id=1, source_target_pairs={{0,2},{1,3},{2,0},{3,1},{4,6},{5,7},{6,4},{7,5},{8,10},{9,11},{10,... | collective-permute-start | bytes 786440 | tf_op jit(solution)/shard_map/ppermute | solution.py:182
  412.9 14.7 %collective-permute-start.31 = (f32[256,128]{1,0:T(8,128)S(1)}, f32[256,128]{1,0:T(8,128)S(1)}, u32[]{:S(2)}, u32[]{:S(2)}) collective-permute-start(f32[256,128]{1,0:T(8,128)S(1)} %get-tuple-element.237), channel_id=1, source_target_pairs={{0,16},{1,17},{2,18},{3,19},{4,20},{5,21},{6,22},{7,23},{16,0},{17... | collective-permute-start | bytes 393224 | tf_op jit(solution)/shard_map/ppermute | solution.py:266
  422.6 13.3 %collective-permute-start.51 = (f32[256,256]{1,0:T(8,128)S(1)}, f32[256,256]{1,0:T(8,128)S(1)}, u32[]{:S(2)}, u32[]{:S(2)}) collective-permute-start(f32[256,256]{1,0:T(8,128)S(1)} %get-tuple-element.206), channel_id=1, source_target_pairs={{0,2},{1,3},{2,0},{3,1},{4,6},{5,7},{6,4},{7,5},{8,10},{9,11},{10,... | collective-permute-start | bytes 786440 | tf_op jit(solution)/shard_map/ppermute | solution.py:182
  426.7 12.9 %collective-permute-start.44 = (f32[256,128]{1,0:T(8,128)S(1)}, f32[256,128]{1,0:T(8,128)S(1)}, u32[]{:S(2)}, u32[]{:S(2)}) collective-permute-start(f32[256,128]{1,0:T(8,128)S(1)} %get-tuple-element.194), channel_id=1, source_target_pairs={{0,1},{1,0},{2,3},{3,2},{4,5},{5,4},{6,7},{7,6},{8,9},{9,8},{10,11... | collective-permute-start | bytes 393224 | tf_op jit(solution)/shard_map/ppermute | solution.py:182
  427.7 13.1 %collective-permute-start.40 = (f32[256,128]{1,0:T(8,128)S(1)}, f32[256,128]{1,0:T(8,128)S(1)}, u32[]{:S(2)}, u32[]{:S(2)}) collective-permute-start(f32[256,128]{1,0:T(8,128)S(1)} %get-tuple-element.184), channel_id=1, source_target_pairs={{0,1},{1,0},{2,3},{3,2},{4,5},{5,4},{6,7},{7,6},{8,9},{9,8},{10,11... | collective-permute-start | bytes 393224 | tf_op jit(solution)/shard_map/ppermute | solution.py:182
  433.2 14.3 %collective-permute-start.56 = (f32[256,128]{1,0:T(8,128)S(1)}, f32[256,128]{1,0:T(8,128)S(1)}, u32[]{:S(2)}, u32[]{:S(2)}) collective-permute-start(f32[256,128]{1,0:T(8,128)S(1)} %get-tuple-element.218), channel_id=1, source_target_pairs={{0,1},{1,0},{2,3},{3,2},{4,5},{5,4},{6,7},{7,6},{8,9},{9,8},{10,11... | collective-permute-start | bytes 393224 | tf_op jit(solution)/shard_map/ppermute | solution.py:182
  (84 other events, 635.3 us)

commit v2 on v0

v2 whole, which is shorter than its diff:
```python
import jax
import jax.numpy as jnp
from jax import lax
from jax.experimental import pallas as pl
from jax.experimental.pallas import tpu as pltpu
from jax.sharding import PartitionSpec as P

F32 = jnp.float32
BF16 = jnp.bfloat16
VMEM_LIMIT = 48 * 1024 * 1024


def params():
    return pltpu.CompilerParams(vmem_limit_bytes=VMEM_LIMIT)


COST = pl.CostEstimate(flops=10**11, bytes_accessed=10**9, transcendentals=0)


def split(state):
    hi = state.astype(BF16)
    return jnp.concatenate([hi, (state - hi.astype(F32)).astype(BF16)], axis=0)


def times(weight, pieces):
    doubled = jnp.concatenate([weight, weight], axis=1)
    return jnp.dot(doubled, pieces, preferred_element_type=F32)


def masked(rank, value):
    return jnp.where(lax.broadcasted_iota(jnp.int32, value.shape, 0) < rank, value, 0.0)


def hbm(*shape):
    return pltpu.HBM(shape, F32)


def placed(*arrays):
    return [pltpu.with_memory_space_constraint(array, pltpu.HBM) for array in arrays]


def local_kernel(ranks, state, self_w, cross_w, keep_out, send_out):
    count = state.shape[1]
    nodes = [state[0, n] for n in range(count)]
    for level in range(2):
        parts = [split(v) for v in nodes]
        kept = [times(self_w[0, level, n], parts[n]) for n in range(count)]
        sent = [times(cross_w[0, level, n], parts[n]) for n in range(count)]
        nodes = [masked(ranks[n], kept[n] + sent[n ^ (1 << level)]) for n in range(count)]
    for n in range(count):
        parts = split(nodes[n])
        keep_out[n] = times(self_w[0, 2, n], parts)
        send_out[n] = times(cross_w[0, 2, n], parts)


def local_levels(part, parts, coefficients, self_weights, cross_weights, ranks):
    _, count, rank, illum = coefficients.shape
    width = illum // parts
    block = 256
    steps = width // block
    mats = pl.BlockSpec((1, 3, count, rank, rank), lambda i, r: (0, 0, 0, 0, 0))
    out = pl.BlockSpec((count, rank, block), lambda i, r: (0, 0, i))
    return pl.pallas_call(
        local_kernel,
        grid_spec=pltpu.PrefetchScalarGridSpec(
            num_scalar_prefetch=1,
            grid=(steps,),
            in_specs=[
                pl.BlockSpec((1, count, rank, block), lambda i, r: (0, 0, 0, part * steps + i)),
                mats,
                mats,
            ],
            out_specs=[out, out],
        ),
        out_shape=[hbm(count, rank, width)] * 2,
        compiler_params=params(),
        cost_estimate=COST,
        name=f"local_part{part}",
    )(ranks, *placed(coefficients, self_weights, cross_weights))


def widen_kernel(self_w, cross_w, *outs):
    each = 2 // len(outs)
    for n in range(2):
        outs[n // each][n % each, 0] = self_w[0, n, 0].astype(F32)
        outs[n // each][n % each, 1] = cross_w[0, n, 0].astype(F32)


def widen(node, arrays, self_weights, cross_weights):
    rank = self_weights.shape[-1]
    shape = (2 // arrays, 2, rank, rank)
    mats = pl.BlockSpec((1, 2, 1, rank, rank), lambda i: (0, 2, node, 0, 0))
    return pl.pallas_call(
        widen_kernel,
        grid=(1,),
        in_specs=[mats, mats],
        out_specs=[pl.BlockSpec(shape, lambda i: (0, 0, 0, 0))] * arrays,
        out_shape=[hbm(*shape)] * arrays,
        compiler_params=params(),
        cost_estimate=COST,
        name=f"widen_{node}",
    )(*placed(self_weights, cross_weights))


def level3_kernel(node, count, info, *refs):
    self_w, cross_w, keep_out, send_out = refs[2 * count :]
    taken = info[4] != 0
    keep_w = jnp.where(taken, cross_w[0, 0, 0], self_w[0, 0, 0])
    send_w = jnp.where(taken, self_w[0, 0, 0], cross_w[0, 0, 0])
    step = pl.program_id(0)
    steps = pl.num_programs(0) // count
    for c in range(count):

        @pl.when(step // steps == c)
        def _():
            parts = split(masked(info[node], refs[2 * c][0] + refs[2 * c + 1][0]))
            keep_out[...] = times(keep_w, parts)
            send_out[...] = times(send_w, parts)


def level3(node, info, pairs, self_weights, cross_weights):
    _, rank, width = pairs[0][0].shape
    count = len(pairs)
    block = 256
    steps = width // block

    def tiles(c):
        def at(i):
            return jnp.clip(i - c * steps, 0, steps - 1)

        return [pl.BlockSpec((1, rank, block), lambda i, r: (node, 0, at(i)))] * 2

    mat = pl.BlockSpec((1, 1, 1, rank, rank), lambda i, r: (0, 3, node, 0, 0))
    out = pl.BlockSpec((rank, block), lambda i, r: (0, i))
    return pl.pallas_call(
        lambda *refs: level3_kernel(node, count, *refs),
        grid_spec=pltpu.PrefetchScalarGridSpec(
            num_scalar_prefetch=1,
            grid=(count * steps,),
            in_specs=[tile for c in range(count) for tile in tiles(c)] + [mat, mat],
            out_specs=[out, out],
        ),
        out_shape=[hbm(rank, count * width)] * 2,
        compiler_params=params(),
        cost_estimate=COST,
        name=f"level3_{node}",
    )(info, *[v for pair in pairs for v in pair], *placed(self_weights, cross_weights))


def moved_kernel(node, count, info, *refs):
    self_w, cross_w, moved, keep_out, send_out, mats = refs[2 * count :]
    step = pl.program_id(0)

    @pl.when(step == 0)
    def _():
        @pl.when(info[4] == 0)
        def _():
            mats[0] = self_w[0, 0, 0]
            mats[1] = cross_w[0, 0, 0]

        @pl.when(info[4] != 0)
        def _():
            mats[0] = moved[0, 0].astype(BF16)
            mats[1] = moved[0, 1].astype(BF16)

    steps = pl.num_programs(0) // count
    for c in range(count):

        @pl.when(step // steps == c)
        def _():
            parts = split(masked(info[node], refs[2 * c][...] + refs[2 * c + 1][...]))
            keep_out[...] = times(mats[0], parts)
            send_out[...] = times(mats[1], parts)


def moved_level(level, node, info, pairs, self_weights, cross_weights, moved):
    rank, width = pairs[0][0].shape
    count = len(pairs)
    block = 256
    steps = width // block
    spot = level - 4 if moved.shape[0] == 2 else 0

    def tile(c):
        return pl.BlockSpec(
            (rank, block), lambda i, r: (0, jnp.clip(i - c * steps, 0, steps - 1))
        )

    mat = pl.BlockSpec((1, 1, 1, rank, rank), lambda i, r: (0, level, node, 0, 0))
    out = pl.BlockSpec((rank, block), lambda i, r: (0, i))
    return pl.pallas_call(
        lambda *refs: moved_kernel(node, count, *refs),
        grid_spec=pltpu.PrefetchScalarGridSpec(
            num_scalar_prefetch=1,
            grid=(count * steps,),
            in_specs=[tile(c) for c in range(count) for _ in range(2)]
            + [mat, mat, pl.BlockSpec((1, 2, rank, rank), lambda i, r: (spot, 0, 0, 0))],
            out_specs=[out, out],
            scratch_shapes=[pltpu.VMEM((2, rank, rank), BF16)],
        ),
        out_shape=[hbm(rank, count * width)] * 2,
        compiler_params=params(),
        cost_estimate=COST,
        name=f"level{level}_{node}",
    )(info, *[v for pair in pairs for v in pair], *placed(self_weights, cross_weights), moved)


def total_kernel(node, count, info, *refs):
    out = refs[-1]
    step = pl.program_id(0)
    steps = pl.num_programs(0) // count
    block = out.shape[2]
    for c in range(count):

        @pl.when(step // steps == c)
        def _():
            value = masked(info[node], refs[2 * c][...] + refs[2 * c + 1][...])
            for j in range(out.shape[0]):
                out[j] = value[:, j * block : (j + 1) * block]


def total(node, info, pairs, cols):
    rank, width = pairs[0][0].shape
    count = len(pairs)
    block = count * width // cols
    each = 4
    steps = cols // (count * each)

    def tile(c):
        return pl.BlockSpec(
            (rank, each * block), lambda i, r: (0, jnp.clip(i - c * steps, 0, steps - 1))
        )

    return pl.pallas_call(
        lambda *refs: total_kernel(node, count, *refs),
        grid_spec=pltpu.PrefetchScalarGridSpec(
            num_scalar_prefetch=1,
            grid=(count * steps,),
            in_specs=[tile(c) for c in range(count) for _ in range(2)],
            out_specs=pl.BlockSpec((each, rank, block), lambda i, r: (i, 0, 0)),
        ),
        out_shape=hbm(cols, rank, block),
        compiler_params=params(),
        cost_estimate=COST,
        name=f"total_{node}",
    )(info, *[v for pair in pairs for v in pair])


def swap(value, axis, mask, chosen=lambda index: True):
    pairs = [(i, i ^ mask) for i in range(lax.axis_size(axis)) if chosen(i)]
    return lax.ppermute(value, axis, pairs)


def tie(value, *before):
    return lax.optimization_barrier((value, *before))[0]


CORE, Z1, Z2, X0 = 1, 2, 4, 8
PARTS = 2


def moves(index):
    return (index & 1) == ((index >> 2) & 1)


def shards(coefficients, self_weights, cross_weights, true_ranks):
    ranks = true_ranks[0]
    count = ranks.shape[0]
    cols = lax.axis_size("col")
    flag = moves(lax.axis_index("node")).astype(jnp.int32)
    weights = (self_weights, cross_weights)

    wide = [widen(0, 1, *weights)[0]]
    moved = {0: swap(wide[0], "node", Z1, moves)}
    fetches, arrivals = {0: 1, 2: 2, 5: 3}, {3: 1, 5: 2, 7: 3}
    sends = {1: 2, 2: 3, 3: 4, 4: 5, 6: 6, 7: 7}
    pieces = [(node, part) for node in range(count) for part in range(PARTS)]
    final = len(pieces)

    own_info = jnp.concatenate([ranks, flag[None]])
    kept3, sent3 = {}, {}
    first = []
    for part in range(PARTS):
        start = tie(ranks, sent3[0] if part else wide[0])
        k, sent = local_levels(part, PARTS, coefficients, *weights, start)
        first.append((k, swap(sent, "node", CORE)))
        kept3[part], sent3[part] = level3(0, own_info, [first[part]], *weights)
    later_ranks, later_weights = tie(ranks, sent3[0]), tie(self_weights, sent3[0])
    wide += [widen(node, 1, later_weights, cross_weights)[0] for node in range(1, count)]
    other_ranks = swap(later_ranks, "node", Z1, moves)
    held = jnp.where(flag == 1, other_ranks, ranks)
    held_info = jnp.concatenate([held, flag[None]])

    def third(turn):
        node, part = pieces[turn]
        return level3(node, own_info, [first[part]], *weights)

    def fourth(turn):
        node = pieces[turn][0]
        k, s = moved_level(4, node, held_info, [(kept3[turn], r3[turn])], *weights, moved[node])
        kept4[turn], r4[turn] = k, swap(s, "node", Z1 | Z2)

    def fifth(node, turns):
        state = [(kept4[t], r4[t]) for t in turns]
        k, s = moved_level(5, node, held_info, state, *weights, moved[node])
        return k, swap(s, "node", X0)

    def homeward(group):
        mine = jnp.stack(group)
        return jnp.where(flag == 1, swap(mine, "node", Z1, moves), mine)

    for turn in range(PARTS, final):
        kept3[turn], sent3[turn] = third(turn)
    r3 = {turn: swap(sent3[turn], "node", Z1) for turn in (0, 1)}
    moved[1] = swap(tie(wide[1], sent3[1]), "node", Z1, moves)
    kept4, r4, fives, sums = {}, {}, {}, []

    def column_sum(node, terms):
        blocks = total(node, held_info, terms, cols)
        sums.append(jnp.sum(lax.all_to_all(blocks, "col", 0, 0, tiled=True), axis=0))

    for turn in range(1, final):
        values = {"r3": r3[turn - 1]}
        if turn in sends:
            values["sent3"] = sent3[sends[turn]]
        if turn in fetches:
            values["wide"] = wide[fetches[turn]]
        if turn in arrivals:
            values["moved"] = moved[arrivals[turn]]
        if turn >= 2:
            values["r4"] = r4[turn - 2]
        if turn == 6:
            values["sum"] = sums[0]
        summed = {4: 0, 6: 1}.get(turn)
        if summed is not None:
            values["five"] = fives[summed][1]
        values = dict(zip(values, lax.optimization_barrier(tuple(values.values()))))
        r3[turn - 1] = values["r3"]
        if turn in sends:
            r3[sends[turn]] = swap(values["sent3"], "node", Z1)
        if turn in arrivals:
            moved[arrivals[turn]] = values["moved"]
        if turn in fetches:
            moved[fetches[turn]] = swap(values["wide"], "node", Z1, moves)
        if turn >= 2:
            r4[turn - 2] = values["r4"]
        if turn == 6:
            sums[0] = values["sum"]
        fourth(turn - 1)
        if turn in (3, 5, 7):
            node = (turn - 3) // 2
            fives[node] = fifth(node, [turn - 3, turn - 2])
        if summed is not None:
            column_sum(summed, [(fives[summed][0], values["five"])])

    r3[final - 1], sums[1] = lax.optimization_barrier((r3[final - 1], sums[1]))
    fourth(final - 1)
    ends = [fifth(count - 1, [final - 2]), fifth(count - 1, [final - 1])]
    for node, terms in ((count - 2, [fives[count - 2]]), (count - 1, ends)):
        column_sum(node, terms)
    return jnp.concatenate([homeward(sums[: count - 1]), homeward(sums[count - 1 :])])


def solution(mesh):
    placed = (
        P("col", "node", None, None),
        P("col", None, "node", None, None),
        P("col", None, "node", None, None),
        P("col", "node"),
    )
    return jax.shard_map(
        shards, mesh=mesh, in_specs=placed, out_specs=P("node", None, "col"), check_vma=False
    )
```

time: 581 us -> 418 us (0.72)
  waiting for transfers between devices: 452 us -> 227 us
  Pallas kernels: 0 us -> 107 us
  starting transfers between devices: 11.4 us -> 74.3 us
  blocking collectives: 51.9 us -> 0 us
  matrix products: 46.3 us -> 0 us
  local copies, waits for them, and re-layouts: 14.9 us -> 1.73 us
    ppermute x4 -> x30, waiting for transfers between devices: 452 us -> 193 us  [swap(): return lax.ppermute(value, axis, pairs)]
    pallas_call x0 -> x31, Pallas kernels: none -> 107 us  [the longest x13 47.7 us: moved_level(): pl.pallas_call(lambda *refs: moved_kernel(node, count, *refs), grid_spec=...]
    all_to_all x1 -> x0, blocking collectives: 51.9 us -> none  [sum_at_owner(): lax.all_to_all(cut_along(array, dim, count), axis, 0, 0, tiled=True)]
    dot_general x12 -> x0, matrix products: 46.3 us -> none  [apply_mats(): jnp.einsum('nrk,nki->nri', weights.astype(jnp.float32), coeffs, precision...]
    ppermute x4 -> x30, starting transfers between devices: 11.4 us -> 52.1 us  [swap(): return lax.ppermute(value, axis, pairs)]
    all_to_all x0 -> x4, waiting for transfers between devices: none -> 33.5 us  [column_sum(): lax.all_to_all(blocks, 'col', 0, 0, tiled=True)]
    all_to_all x0 -> x4, starting transfers between devices: none -> 22.1 us  [column_sum(): lax.all_to_all(blocks, 'col', 0, 0, tiled=True)]
    rev x2 -> x0, local copies, waits for them, and re-layouts: 9.45 us -> none  [partner_view(): return shaped[:, ::-1].reshape(values.shape)]
  transfers between devices with their start and end apart: 4 -> 34, of which waited for: 4 -> 20; matrix products, arithmetic and copies ran while one was open for 1% -> 1% of each run, Pallas kernels for 0% -> 23%
where the time goes in v2:
time: 418 us; the launch traced here: 416 us
  waiting for transfers between devices  227 us (54%)
  Pallas kernels  107 us (26%)
  starting transfers between devices  74.3 us (18%)
  other arithmetic  6.4 us (2%)
    ppermute x30, waiting for transfers between devices, swap(): return lax.ppermute(value, axis, pairs)  193 us
    ppermute x30, starting transfers between devices, swap(): return lax.ppermute(value, axis, pairs)  52.1 us
    pallas_call x13, Pallas kernels, moved_level(): pl.pallas_call(lambda *refs: moved_kernel(node, count, *refs), grid_spec=...  47.7 us
    all_to_all x4, waiting for transfers between devices, column_sum(): lax.all_to_all(blocks, 'col', 0, 0, tiled=True)  33.5 us
    pallas_call x8, Pallas kernels, level3(): pl.pallas_call(lambda *refs: level3_kernel(node, count, *refs), grid_spec...  25 us
    all_to_all x4, starting transfers between devices, column_sum(): lax.all_to_all(blocks, 'col', 0, 0, tiled=True)  22.1 us
    pallas_call x2, Pallas kernels, local_levels(): pl.pallas_call(local_kernel, grid_spec=pltpu.PrefetchScalarGridSpec(num_s...  16.4 us
    pallas_call x4, Pallas kernels, total(): pl.pallas_call(lambda *refs: total_kernel(node, count, *refs), grid_spec=...  9.14 us
  transfers between devices with their start and end apart: 34, of which 20 were waited for; matrix products, arithmetic and copies ran while one was open for 1% of the time, Pallas kernels for 23%

profile of v2, /device:TPU:2, one launch (start us, length us, event | category | flops | bytes accessed | tf_op | source)
XLA Modules:
  0.0 416.3 jit_solution(5997079740962186114)
XLA Ops:
  2.1 8.1 %local_part0.1 = (f32[4,256,512]{2,1,0:T(8,128)}, f32[4,256,512]{2,1,0:T(8,128)}) custom-call(s32[4]{0:T(128)} %bitcast.ranks, f32[1,4,256,1024]{3,2,1,0:T(8,128)} %state.3, bf16[1,6,4,256,256]{4,3,2,1,0:T(8,128)(2,1)} %refs_3_.35, bf16[1,6,4,256,256]{4,3,2,1,0:T(8,128)(2,1)} %refs_4_.35), custom_call_target="tpu_custom_call" | custom-call | flops 99999997952 | bytes 1000000000 | tf_op jit(solution)/shard_map/local_part0/pallas_call | solution.py:63
  10.2 5.2 %collective-permute-start.5 = (f32[2,2,256,256]{3,2,1,0:T(8,128)}, f32[2,2,256,256]{3,2,1,0:T(8,128)}, u32[]{:S(2)}, u32[]{:S(2)}) collective-permute-start(f32[2,2,256,256]{3,2,1,0:T(8,128)} %widen_0.1), channel_id=1, source_target_pairs={{0,16},{16,0},{40,56},{56,40},{64,80},{80,64},{104,120},{120,104},... | collective-permute-start | bytes 3145736 | tf_op jit(solution)/shard_map/ppermute | solution.py:250
  28.8 3.2 collective-permute-start.3
  32.1 8.2 %local_part1.1 = (f32[4,256,512]{2,1,0:T(8,128)}, f32[4,256,512]{2,1,0:T(8,128)}) custom-call(s32[4]{0:T(128)} %bitcast.ranks, f32[1,4,256,1024]{3,2,1,0:T(8,128)} %state.3, bf16[1,6,4,256,256]{4,3,2,1,0:T(8,128)(2,1)} %refs_3_.35, bf16[1,6,4,256,256]{4,3,2,1,0:T(8,128)(2,1)} %refs_4_.35), custom_call_target="tpu_custom_call" | custom-call | flops 99999997952 | bytes 1000000000 | tf_op jit(solution)/shard_map/local_part1/pallas_call | solution.py:63
  46.5 15.6 %collective-permute-done.3 = s32[4]{0:T(128)} collective-permute-done((s32[4]{0:T(128)}, s32[4]{0:T(128)}, u32[]{:S(2)}, u32[]{:S(2)}) %collective-permute-start.3) | collective-permute-done | bytes 48 | tf_op jit(solution)/shard_map/ppermute | solution.py:250
  63.0 3.4 level4_0.2
  66.5 3.2 level3_0.3
  74.7 3.2 level3_1.2
  77.9 15.9 %collective-permute-done.6.refs_2_ = f32[256,512]{1,0:T(8,128)} collective-permute-done((f32[256,512]{1,0:T(8,128)}, f32[256,512]{1,0:T(8,128)}, u32[]{:S(2)}, u32[]{:S(2)}) %collective-permute-start.6) | collective-permute-done | bytes 524320 | tf_op jit(solution)/shard_map/ppermute | solution.py:250
  93.8 32.4 %collective-permute-done.2.refs_2_ = f32[256,512]{1,0:T(8,128)S(1)} collective-permute-done((f32[256,512]{1,0:T(8,128)}, f32[256,512]{1,0:T(8,128)S(1)}, u32[]{:S(2)}, u32[]{:S(2)}) %collective-permute-start.2) | collective-permute-done | bytes 524320 | tf_op jit(solution)/shard_map/ppermute | solution.py:250
  126.1 3.3 level4_0.3
  133.7 3.3 collective-permute-start.7
  137.0 23.1 %collective-permute-done.10.refs_4_ = f32[256,512]{1,0:T(8,128)S(1)} collective-permute-done((f32[256,512]{1,0:T(8,128)}, f32[256,512]{1,0:T(8,128)S(1)}, u32[]{:S(2)}, u32[]{:S(2)}) %collective-permute-start.10) | collective-permute-done | bytes 524320 | tf_op jit(solution)/shard_map/ppermute | solution.py:250
  160.1 3.4 level4_1.2
  163.6 4.6 %level5_0.1 = (f32[256,1024]{1,0:T(8,128)}, f32[256,1024]{1,0:T(8,128)}) custom-call(s32[5]{0:T(128)S(1)} %copy-done.1, f32[256,512]{1,0:T(8,128)S(1)} %copy-done.25, f32[256,512]{1,0:T(8,128)} %collective-permute-done.6.refs_2_, f32[256,512]{1,0:T(8,128)S(1)} %copy-done.28, f32[256,512]{1,0:T(8,128)S(1)} %collective-permute-done.10.refs_4_, ...), custom_call_target="tpu_custom_call" | custom-call | flops 99999997952 | bytes 1000000000 | tf_op jit(solution)/shard_map/level5_0/pallas_call | solution.py:190
  171.9 4.5 %collective-permute-start.15 = (f32[2,2,256,256]{3,2,1,0:T(8,128)}, f32[2,2,256,256]{3,2,1,0:T(8,128)}, u32[]{:S(2)}, u32[]{:S(2)}) collective-permute-start(f32[2,2,256,256]{3,2,1,0:T(8,128)} %widen_2.1), channel_id=1, source_target_pairs={{0,16},{16,0},{40,56},{56,40},{64,80},{80,64},{104,120},{120,104},... | collective-permute-start | bytes 3145736 | tf_op jit(solution)/shard_map/ppermute | solution.py:250
  176.8 14.2 %collective-permute-done.11.refs_2_ = f32[256,512]{1,0:T(8,128)} collective-permute-done((f32[256,512]{1,0:T(8,128)}, f32[256,512]{1,0:T(8,128)}, u32[]{:S(2)}, u32[]{:S(2)}) %collective-permute-start.11) | collective-permute-done | bytes 524320 | tf_op jit(solution)/shard_map/ppermute | solution.py:250
  193.6 3.4 level4_1.3
  197.0 3.8 collective-permute-start.16
  202.7 4.6 %all-to-all-start = ((f32[8,256,128]{2,1,0:T(8,128)}), f32[8,256,128]{2,1,0:T(8,128)}, u32[]{:S(2)}, u32[]{:S(2)}) async-start(f32[8,256,128]{2,1,0:T(8,128)} %total_0.1), calls=%async_computation | async-start | bytes 2097152 | tf_op jit(solution)/shard_map/all_to_all | solution.py:319
  208.0 14.2 %collective-permute-done.15.refs_5_.refs_7_ = f32[2,2,256,256]{3,2,1,0:T(8,128)} collective-permute-done((f32[2,2,256,256]{3,2,1,0:T(8,128)}, f32[2,2,256,256]{3,2,1,0:T(8,128)}, u32[]{:S(2)}, u32[]{:S(2)}) %collective-permute-start.15) | collective-permute-done | bytes 1048608 | tf_op jit(solution)/shard_map/ppermute | solution.py:250
  222.2 5.6 %collective-permute-done.14.refs_2_ = f32[256,512]{1,0:T(8,128)} collective-permute-done((f32[256,512]{1,0:T(8,128)}, f32[256,512]{1,0:T(8,128)}, u32[]{:S(2)}, u32[]{:S(2)}) %collective-permute-start.14) | collective-permute-done | bytes 524320 | tf_op jit(solution)/shard_map/ppermute | solution.py:250
  227.8 7.2 %collective-permute-done.16.refs_4_ = f32[256,512]{1,0:T(8,128)S(1)} collective-permute-done((f32[256,512]{1,0:T(8,128)}, f32[256,512]{1,0:T(8,128)S(1)}, u32[]{:S(2)}, u32[]{:S(2)}) %collective-permute-start.16) | collective-permute-done | bytes 524320 | tf_op jit(solution)/shard_map/ppermute | solution.py:250
  235.0 3.4 level4_2.2
  238.4 4.7 %level5_1.1 = (f32[256,1024]{1,0:T(8,128)}, f32[256,1024]{1,0:T(8,128)}) custom-call(s32[5]{0:T(128)S(1)} %copy-done.1, f32[256,512]{1,0:T(8,128)S(1)} %copy-done.24, f32[256,512]{1,0:T(8,128)} %collective-permute-done.11.refs_2_, f32[256,512]{1,0:T(8,128)S(1)} %copy-done.27, f32[256,512]{1,0:T(8,128)S(1)} %collective-permute-done.16.refs_4_, ...), custom_call_target="tpu_custom_call" | custom-call | flops 99999997952 | bytes 1000000000 | tf_op jit(solution)/shard_map/level5_1/pallas_call | solution.py:190
  243.4 3.2 level3_3.3
  246.6 6.3 %collective-permute-start.20 = (f32[2,2,256,256]{3,2,1,0:T(8,128)}, f32[2,2,256,256]{3,2,1,0:T(8,128)}, u32[]{:S(2)}, u32[]{:S(2)}) collective-permute-start(f32[2,2,256,256]{3,2,1,0:T(8,128)} %widen_3.1), channel_id=1, source_target_pairs={{0,16},{16,0},{40,56},{56,40},{64,80},{80,64},{104,120},{120,104},... | collective-permute-start | bytes 3145736 | tf_op jit(solution)/shard_map/ppermute | solution.py:250
  254.9 5.4 %collective-permute-done.17.refs_2_ = f32[256,512]{1,0:T(8,128)} collective-permute-done((f32[256,512]{1,0:T(8,128)}, f32[256,512]{1,0:T(8,128)}, u32[]{:S(2)}, u32[]{:S(2)}) %collective-permute-start.17) | collective-permute-done | bytes 524320 | tf_op jit(solution)/shard_map/ppermute | solution.py:250
  261.8 3.4 level4_2.3
  265.6 3.2 collective-permute-start.19
  270.7 5.7 %all-to-all-start.1 = ((f32[8,256,128]{2,1,0:T(8,128)}), f32[8,256,128]{2,1,0:T(8,128)}, u32[]{:S(2)}, u32[]{:S(2)}) async-start(f32[8,256,128]{2,1,0:T(8,128)} %total_1.1), calls=%async_computation.1 | async-start | bytes 2097152 | tf_op jit(solution)/shard_map/all_to_all | solution.py:319
  276.4 16.4 %collective-permute-done.20.refs_5_ = f32[2,2,256,256]{3,2,1,0:T(8,128)} collective-permute-done((f32[2,2,256,256]{3,2,1,0:T(8,128)}, f32[2,2,256,256]{3,2,1,0:T(8,128)}, u32[]{:S(2)}, u32[]{:S(2)}) %collective-permute-start.20) | collective-permute-done | bytes 1048608 | tf_op jit(solution)/shard_map/ppermute | solution.py:250
  292.8 7.0 %collective-permute-done.19.refs_2_ = f32[256,512]{1,0:T(8,128)S(1)} collective-permute-done((f32[256,512]{1,0:T(8,128)S(1)}, f32[256,512]{1,0:T(8,128)S(1)}, u32[]{:S(2)}, u32[]{:S(2)}) %collective-permute-start.19) | collective-permute-done | bytes 524320 | tf_op jit(solution)/shard_map/ppermute | solution.py:250
  299.8 3.3 level4_3.2
  303.2 4.7 %level5_2.1 = (f32[256,1024]{1,0:T(8,128)}, f32[256,1024]{1,0:T(8,128)}) custom-call(s32[5]{0:T(128)S(1)} %copy-done.1, f32[256,512]{1,0:T(8,128)S(1)} %copy-done.23, f32[256,512]{1,0:T(8,128)} %collective-permute-done.17.refs_2_, f32[256,512]{1,0:T(8,128)S(1)} %copy-done.26, f32[256,512]{1,0:T(8,128)S(1)} %collective-permute-done.21.refs_4_, ...), custom_call_target="tpu_custom_call" | custom-call | flops 99999997952 | bytes 1000000000 | tf_op jit(solution)/shard_map/level5_2/pallas_call | solution.py:190
  307.9 5.2 %collective-permute-start.23 = (f32[256,1024]{1,0:T(8,128)}, f32[256,1024]{1,0:T(8,128)}, u32[]{:S(2)}, u32[]{:S(2)}) collective-permute-start(f32[256,1024]{1,0:T(8,128)} %get-tuple-element.149), channel_id=1, source_target_pairs={{0,64},{8,72},{16,80},{24,88},{32,96},{40,104},{48,112},{56,120},{... | collective-permute-start | bytes 3145736 | tf_op jit(solution)/shard_map/ppermute | solution.py:250
  313.1 9.7 %all-to-all-done.1 = f32[8,256,128]{2,1,0:T(8,128)} async-done(((f32[8,256,128]{2,1,0:T(8,128)}), f32[8,256,128]{2,1,0:T(8,128)}, u32[]{:S(2)}, u32[]{:S(2)}) %all-to-all-start.1) | async-done | bytes 1048608 | tf_op jit(solution)/shard_map/all_to_all | solution.py:319
  324.7 4.3 %collective-permute-done.22.refs_2_ = f32[256,512]{1,0:T(8,128)S(1)} collective-permute-done((f32[256,512]{1,0:T(8,128)S(1)}, f32[256,512]{1,0:T(8,128)S(1)}, u32[]{:S(2)}, u32[]{:S(2)}) %collective-permute-start.22) | collective-permute-done | bytes 524320 | tf_op jit(solution)/shard_map/ppermute | solution.py:250
  329.0 3.4 level4_3.3
  333.9 3.3 level5_3.2
  337.2 19.0 %collective-permute-done.27.refs_2_ = f32[256,512]{1,0:T(8,128)S(1)} collective-permute-done((f32[256,512]{1,0:T(8,128)}, f32[256,512]{1,0:T(8,128)S(1)}, u32[]{:S(2)}, u32[]{:S(2)}) %collective-permute-start.27) | collective-permute-done | bytes 524320 | tf_op jit(solution)/shard_map/ppermute | solution.py:250
  356.2 3.4 level5_3.3
  362.4 8.2 %all-to-all-start.2 = ((f32[8,256,128]{2,1,0:T(8,128)}), f32[8,256,128]{2,1,0:T(8,128)S(1)}, u32[]{:S(2)}, u32[]{:S(2)}) async-start(f32[8,256,128]{2,1,0:T(8,128)} %total_2.1), calls=%async_computation.2 | async-start | bytes 2097152 | tf_op jit(solution)/shard_map/all_to_all | solution.py:319
  376.3 8.9 %all-to-all-done.2 = f32[8,256,128]{2,1,0:T(8,128)S(1)} async-done(((f32[8,256,128]{2,1,0:T(8,128)}), f32[8,256,128]{2,1,0:T(8,128)S(1)}, u32[]{:S(2)}, u32[]{:S(2)}) %all-to-all-start.2) | async-done | bytes 1048608 | tf_op jit(solution)/shard_map/all_to_all | solution.py:319
  385.2 3.6 all-to-all-start.3
  389.0 3.5 collective-permute-start.24
  392.5 14.9 %all-to-all-done.3 = f32[8,256,128]{2,1,0:T(8,128)S(1)} async-done(((f32[8,256,128]{2,1,0:T(8,128)}), f32[8,256,128]{2,1,0:T(8,128)S(1)}, u32[]{:S(2)}, u32[]{:S(2)}) %all-to-all-start.3) | async-done | bytes 1048608 | tf_op jit(solution)/shard_map/all_to_all | solution.py:319
  409.5 5.9 %collective-permute-done.29 = f32[1,256,128]{2,1,0:T(8,128)S(1)} collective-permute-done((f32[1,256,128]{2,1,0:T(8,128)S(1)}, f32[1,256,128]{2,1,0:T(8,128)S(1)}, u32[]{:S(2)}, u32[]{:S(2)}) %collective-permute-start.29) | collective-permute-done | bytes 131104 | tf_op jit(solution)/shard_map/ppermute | solution.py:250
  (136 shorter events, 62.3 us)
Async XLA Ops:
  10.2 5.9 %collective-permute-start = (f32[4,256,512]{2,1,0:T(8,128)}, f32[4,256,512]{2,1,0:T(8,128)S(1)}, u32[]{:S(2)}, u32[]{:S(2)}) collective-permute-start(f32[4,256,512]{2,1,0:T(8,128)} %get-tuple-element.86), channel_id=1, source_target_pairs={{0,8},{8,0},{16,24},{24,16},{32,40},{40,32},{48,56},{56,48},{64,72... | collective-permute-start | bytes 6291464 | tf_op jit(solution)/shard_map/ppermute | solution.py:250
  10.2 52.7 %collective-permute-start.5 = (f32[2,2,256,256]{3,2,1,0:T(8,128)}, f32[2,2,256,256]{3,2,1,0:T(8,128)}, u32[]{:S(2)}, u32[]{:S(2)}) collective-permute-start(f32[2,2,256,256]{3,2,1,0:T(8,128)} %widen_0.1), channel_id=1, source_target_pairs={{0,16},{16,0},{40,56},{56,40},{64,80},{80,64},{104,120},{120,104},... | collective-permute-start | bytes 3145736 | tf_op jit(solution)/shard_map/ppermute | solution.py:250
  16.1 27.3 %copy-start.2 = (s32[5]{0:T(128)}, s32[5]{0:T(128)S(1)}, u32[]{:S(2)}) copy-start(s32[5]{0:T(128)S(1)} %pad_add_fusion.refs_0_) | copy-start | bytes 64
  20.8 42.1 %collective-permute-start.4 = (f32[256,512]{1,0:T(8,128)}, f32[256,512]{1,0:T(8,128)}, u32[]{:S(2)}, u32[]{:S(2)}) collective-permute-start(f32[256,512]{1,0:T(8,128)} %get-tuple-element.87), channel_id=1, source_target_pairs={{0,16},{8,24},{16,0},{24,8},{32,48},{40,56},{48,32},{56,40},{64,80... | collective-permute-start | bytes 1572872 | tf_op jit(solution)/shard_map/ppermute | solution.py:250
  28.8 11.5 %copy-start.10 = (f32[4,256,512]{2,1,0:T(8,128)S(1)}, f32[4,256,512]{2,1,0:T(8,128)}, u32[]{:S(2)}) copy-start(f32[4,256,512]{2,1,0:T(8,128)} %get-tuple-element.85.refs_1_) | copy-start | bytes 6291460
  28.8 33.3 %collective-permute-start.3 = (s32[4]{0:T(128)}, s32[4]{0:T(128)}, u32[]{:S(2)}, u32[]{:S(2)}) collective-permute-start(s32[4]{0:T(128)} %bitcast.ranks), channel_id=1, source_target_pairs={{0,16},{16,0},{40,56},{56,40},{64,80},{80,64},{104,120},{120,104},... | collective-permute-start | bytes 56 | tf_op jit(solution)/shard_map/ppermute | solution.py:250
  40.3 26.2 %collective-permute-start.1 = (f32[4,256,512]{2,1,0:T(8,128)}, f32[4,256,512]{2,1,0:T(8,128)}, u32[]{:S(2)}, u32[]{:S(2)}) collective-permute-start(f32[4,256,512]{2,1,0:T(8,128)} %get-tuple-element.90), channel_id=1, source_target_pairs={{0,8},{8,0},{16,24},{24,16},{32,40},{40,32},{48,56},{56,48},{64,72... | collective-permute-start | bytes 6291464 | tf_op jit(solution)/shard_map/ppermute | solution.py:250
  43.4 19.5 %copy-start.21 = (f32[256,512]{1,0:T(8,128)S(1)}, f32[256,512]{1,0:T(8,128)}, u32[]{:S(2)}) copy-start(f32[256,512]{1,0:T(8,128)} %get-tuple-element.94.refs_1_) | copy-start | bytes 1572868
  66.4 27.4 %collective-permute-start.6 = (f32[256,512]{1,0:T(8,128)}, f32[256,512]{1,0:T(8,128)}, u32[]{:S(2)}, u32[]{:S(2)}) collective-permute-start(f32[256,512]{1,0:T(8,128)} %get-tuple-element.97), channel_id=1, source_target_pairs={{0,48},{8,56},{16,32},{24,40},{32,16},{40,24},{48,0},{56,8},{64,11... | collective-permute-start | bytes 1572872 | tf_op jit(solution)/shard_map/ppermute | solution.py:250
  66.4 70.6 %collective-permute-start.8 = (f32[256,512]{1,0:T(8,128)}, f32[256,512]{1,0:T(8,128)}, u32[]{:S(2)}, u32[]{:S(2)}) collective-permute-start(f32[256,512]{1,0:T(8,128)} %get-tuple-element.101), channel_id=1, source_target_pairs={{0,16},{8,24},{16,0},{24,8},{32,48},{40,56},{48,32},{56,40},{64,80... | collective-permute-start | bytes 1572872 | tf_op jit(solution)/shard_map/ppermute | solution.py:250
  69.7 56.4 %copy-start.1 = (s32[5]{0:T(128)S(1)}, s32[5]{0:T(128)}, u32[]{:S(2)}) copy-start(s32[5]{0:T(128)} %copy-done) | copy-start | bytes 64
  69.7 56.4 %copy-start.22 = (f32[256,512]{1,0:T(8,128)S(1)}, f32[256,512]{1,0:T(8,128)}, u32[]{:S(2)}) copy-start(f32[256,512]{1,0:T(8,128)} %get-tuple-element.104.refs_1_) | copy-start | bytes 1572868
  69.7 56.4 %collective-permute-start.2 = (f32[256,512]{1,0:T(8,128)}, f32[256,512]{1,0:T(8,128)S(1)}, u32[]{:S(2)}, u32[]{:S(2)}) collective-permute-start(f32[256,512]{1,0:T(8,128)} %get-tuple-element.91), channel_id=1, source_target_pairs={{0,16},{8,24},{16,0},{24,8},{32,48},{40,56},{48,32},{56,40},{64,80... | collective-permute-start | bytes 1572872 | tf_op jit(solution)/shard_map/ppermute | solution.py:250
  72.7 87.4 %collective-permute-start.9 = (f32[2,2,256,256]{3,2,1,0:T(8,128)}, f32[2,2,256,256]{3,2,1,0:T(8,128)}, u32[]{:S(2)}, u32[]{:S(2)}) collective-permute-start(f32[2,2,256,256]{3,2,1,0:T(8,128)} %widen_1.1), channel_id=1, source_target_pairs={{0,16},{16,0},{40,56},{56,40},{64,80},{80,64},{104,120},{120,104},... | collective-permute-start | bytes 3145736 | tf_op jit(solution)/shard_map/ppermute | solution.py:250
  129.5 30.6 %copy-start.19 = (f32[256,512]{1,0:T(8,128)S(1)}, f32[256,512]{1,0:T(8,128)}, u32[]{:S(2)}) copy-start(f32[256,512]{1,0:T(8,128)} %get-tuple-element.100.refs_1_) | copy-start | bytes 1572868
  129.5 30.6 %collective-permute-start.10 = (f32[256,512]{1,0:T(8,128)}, f32[256,512]{1,0:T(8,128)S(1)}, u32[]{:S(2)}, u32[]{:S(2)}) collective-permute-start(f32[256,512]{1,0:T(8,128)} %get-tuple-element.106), channel_id=1, source_target_pairs={{0,48},{8,56},{16,32},{24,40},{32,16},{40,24},{48,0},{56,8},{64,11... | collective-permute-start | bytes 1572872 | tf_op jit(solution)/shard_map/ppermute | solution.py:250
  133.7 43.1 %collective-permute-start.7 = (f32[256,512]{1,0:T(8,128)}, f32[256,512]{1,0:T(8,128)}, u32[]{:S(2)}, u32[]{:S(2)}) collective-permute-start(f32[256,512]{1,0:T(8,128)} %get-tuple-element.98), channel_id=1, source_target_pairs={{0,16},{8,24},{16,0},{24,8},{32,48},{40,56},{48,32},{56,40},{64,80... | collective-permute-start | bytes 1572872 | tf_op jit(solution)/shard_map/ppermute | solution.py:250
  163.5 27.5 %collective-permute-start.11 = (f32[256,512]{1,0:T(8,128)}, f32[256,512]{1,0:T(8,128)}, u32[]{:S(2)}, u32[]{:S(2)}) collective-permute-start(f32[256,512]{1,0:T(8,128)} %get-tuple-element.109), channel_id=1, source_target_pairs={{0,48},{8,56},{16,32},{24,40},{32,16},{40,24},{48,0},{56,8},{64,11... | collective-permute-start | bytes 1572872 | tf_op jit(solution)/shard_map/ppermute | solution.py:250
  168.2 25.4 %copy-start.20 = (f32[256,512]{1,0:T(8,128)S(1)}, f32[256,512]{1,0:T(8,128)}, u32[]{:S(2)}) copy-start(f32[256,512]{1,0:T(8,128)} %get-tuple-element.120.refs_1_) | copy-start | bytes 1572868
  168.2 25.4 %collective-permute-start.12 = (f32[256,1024]{1,0:T(8,128)}, f32[256,1024]{1,0:T(8,128)S(1)}, u32[]{:S(2)}, u32[]{:S(2)}) collective-permute-start(f32[256,1024]{1,0:T(8,128)} %get-tuple-element.114), channel_id=1, source_target_pairs={{0,64},{8,72},{16,80},{24,88},{32,96},{40,104},{48,112},{56,120},{... | collective-permute-start | bytes 3145736 | tf_op jit(solution)/shard_map/ppermute | solution.py:250
  171.9 50.3 %collective-permute-start.15 = (f32[2,2,256,256]{3,2,1,0:T(8,128)}, f32[2,2,256,256]{3,2,1,0:T(8,128)}, u32[]{:S(2)}, u32[]{:S(2)}) collective-permute-start(f32[2,2,256,256]{3,2,1,0:T(8,128)} %widen_2.1), channel_id=1, source_target_pairs={{0,16},{16,0},{40,56},{56,40},{64,80},{80,64},{104,120},{120,104},... | collective-permute-start | bytes 3145736 | tf_op jit(solution)/shard_map/ppermute | solution.py:250
  176.4 51.4 %collective-permute-start.14 = (f32[256,512]{1,0:T(8,128)}, f32[256,512]{1,0:T(8,128)}, u32[]{:S(2)}, u32[]{:S(2)}) collective-permute-start(f32[256,512]{1,0:T(8,128)} %get-tuple-element.118), channel_id=1, source_target_pairs={{0,16},{8,24},{16,0},{24,8},{32,48},{40,56},{48,32},{56,40},{64,80... | collective-permute-start | bytes 1572872 | tf_op jit(solution)/shard_map/ppermute | solution.py:250
  197.0 38.0 %collective-permute-start.16 = (f32[256,512]{1,0:T(8,128)}, f32[256,512]{1,0:T(8,128)S(1)}, u32[]{:S(2)}, u32[]{:S(2)}) collective-permute-start(f32[256,512]{1,0:T(8,128)} %get-tuple-element.122), channel_id=1, source_target_pairs={{0,48},{8,56},{16,32},{24,40},{32,16},{40,24},{48,0},{56,8},{64,11... | collective-permute-start | bytes 1572872 | tf_op jit(solution)/shard_map/ppermute | solution.py:250
  202.7 32.3 %copy-start.17 = (f32[256,512]{1,0:T(8,128)S(1)}, f32[256,512]{1,0:T(8,128)}, u32[]{:S(2)}) copy-start(f32[256,512]{1,0:T(8,128)} %get-tuple-element.117.refs_1_) | copy-start | bytes 1572868
  202.7 50.3 %all-to-all-start = ((f32[8,256,128]{2,1,0:T(8,128)}), f32[8,256,128]{2,1,0:T(8,128)}, u32[]{:S(2)}, u32[]{:S(2)}) async-start(f32[8,256,128]{2,1,0:T(8,128)} %total_0.1), calls=%async_computation | async-start | bytes 2097152 | tf_op jit(solution)/shard_map/all_to_all | solution.py:319
  207.3 47.6 %collective-permute-start.13 = (f32[256,512]{1,0:T(8,128)}, f32[256,512]{1,0:T(8,128)}, u32[]{:S(2)}, u32[]{:S(2)}) collective-permute-start(f32[256,512]{1,0:T(8,128)} %get-tuple-element.115), channel_id=1, source_target_pairs={{0,16},{8,24},{16,0},{24,8},{32,48},{40,56},{48,32},{56,40},{64,80... | collective-permute-start | bytes 1572872 | tf_op jit(solution)/shard_map/ppermute | solution.py:250
  238.4 21.9 %collective-permute-start.17 = (f32[256,512]{1,0:T(8,128)}, f32[256,512]{1,0:T(8,128)}, u32[]{:S(2)}, u32[]{:S(2)}) collective-permute-start(f32[256,512]{1,0:T(8,128)} %get-tuple-element.125), channel_id=1, source_target_pairs={{0,48},{8,56},{16,32},{24,40},{32,16},{40,24},{48,0},{56,8},{64,11... | collective-permute-start | bytes 1572872 | tf_op jit(solution)/shard_map/ppermute | solution.py:250
  243.1 18.8 %copy-start.16 = (f32[256,512]{1,0:T(8,128)S(1)}, f32[256,512]{1,0:T(8,128)}, u32[]{:S(2)}) copy-start(f32[256,512]{1,0:T(8,128)} %get-tuple-element.137.refs_1_) | copy-start | bytes 1572868
  243.1 18.8 %collective-permute-start.18 = (f32[256,1024]{1,0:T(8,128)}, f32[256,1024]{1,0:T(8,128)S(1)}, u32[]{:S(2)}, u32[]{:S(2)}) collective-permute-start(f32[256,1024]{1,0:T(8,128)} %get-tuple-element.132), channel_id=1, source_target_pairs={{0,64},{8,72},{16,80},{24,88},{32,96},{40,104},{48,112},{56,120},{... | collective-permute-start | bytes 3145736 | tf_op jit(solution)/shard_map/ppermute | solution.py:250
  246.6 46.2 %collective-permute-start.20 = (f32[2,2,256,256]{3,2,1,0:T(8,128)}, f32[2,2,256,256]{3,2,1,0:T(8,128)}, u32[]{:S(2)}, u32[]{:S(2)}) collective-permute-start(f32[2,2,256,256]{3,2,1,0:T(8,128)} %widen_3.1), channel_id=1, source_target_pairs={{0,16},{16,0},{40,56},{56,40},{64,80},{80,64},{104,120},{120,104},... | collective-permute-start | bytes 3145736 | tf_op jit(solution)/shard_map/ppermute | solution.py:250
  265.2 27.6 %collective-permute-start.21 = (f32[256,512]{1,0:T(8,128)}, f32[256,512]{1,0:T(8,128)S(1)}, u32[]{:S(2)}, u32[]{:S(2)}) collective-permute-start(f32[256,512]{1,0:T(8,128)} %get-tuple-element.139), channel_id=1, source_target_pairs={{0,48},{8,56},{16,32},{24,40},{32,16},{40,24},{48,0},{56,8},{64,11... | collective-permute-start | bytes 1572872 | tf_op jit(solution)/shard_map/ppermute | solution.py:250
  265.6 34.2 %collective-permute-start.19 = (f32[256,512]{1,0:T(8,128)S(1)}, f32[256,512]{1,0:T(8,128)S(1)}, u32[]{:S(2)}, u32[]{:S(2)}) collective-permute-start(f32[256,512]{1,0:T(8,128)S(1)} %copy-done.35), channel_id=1, source_target_pairs={{0,16},{8,24},{16,0},{24,8},{32,48},{40,56},{48,32},{56,40},{64,80... | collective-permute-start | bytes 1572872 | tf_op jit(solution)/shard_map/ppermute | solution.py:250
  270.7 29.1 %copy-start.15 = (f32[256,512]{1,0:T(8,128)S(1)}, f32[256,512]{1,0:T(8,128)}, u32[]{:S(2)}) copy-start(f32[256,512]{1,0:T(8,128)} %get-tuple-element.150.refs_1_) | copy-start | bytes 1572868
  270.7 52.1 %all-to-all-start.1 = ((f32[8,256,128]{2,1,0:T(8,128)}), f32[8,256,128]{2,1,0:T(8,128)}, u32[]{:S(2)}, u32[]{:S(2)}) async-start(f32[8,256,128]{2,1,0:T(8,128)} %total_1.1), calls=%async_computation.1 | async-start | bytes 2097152 | tf_op jit(solution)/shard_map/all_to_all | solution.py:319
  303.1 30.8 %collective-permute-start.25 = (f32[256,512]{1,0:T(8,128)}, f32[256,512]{1,0:T(8,128)}, u32[]{:S(2)}, u32[]{:S(2)}) collective-permute-start(f32[256,512]{1,0:T(8,128)} %get-tuple-element.154), channel_id=1, source_target_pairs={{0,48},{8,56},{16,32},{24,40},{32,16},{40,24},{48,0},{56,8},{64,11... | collective-permute-start | bytes 1572872 | tf_op jit(solution)/shard_map/ppermute | solution.py:250
  303.1 25.9 %collective-permute-start.22 = (f32[256,512]{1,0:T(8,128)S(1)}, f32[256,512]{1,0:T(8,128)S(1)}, u32[]{:S(2)}, u32[]{:S(2)}) collective-permute-start(f32[256,512]{1,0:T(8,128)S(1)} %copy-done.36), channel_id=1, source_target_pairs={{0,16},{8,24},{16,0},{24,8},{32,48},{40,56},{48,32},{56,40},{64,80... | collective-permute-start | bytes 1572872 | tf_op jit(solution)/shard_map/ppermute | solution.py:250
  303.2 25.8 %copy-start.18 = (f32[256,512]{1,0:T(8,128)S(1)}, f32[256,512]{1,0:T(8,128)}, u32[]{:S(2)}) copy-start(f32[256,512]{1,0:T(8,128)} %get-tuple-element.157.refs_1_) | copy-start | bytes 1572868
  307.9 51.7 %collective-permute-start.23 = (f32[256,1024]{1,0:T(8,128)}, f32[256,1024]{1,0:T(8,128)}, u32[]{:S(2)}, u32[]{:S(2)}) collective-permute-start(f32[256,1024]{1,0:T(8,128)} %get-tuple-element.149), channel_id=1, source_target_pairs={{0,64},{8,72},{16,80},{24,88},{32,96},{40,104},{48,112},{56,120},{... | collective-permute-start | bytes 3145736 | tf_op jit(solution)/shard_map/ppermute | solution.py:250
  332.4 23.9 %collective-permute-start.27 = (f32[256,512]{1,0:T(8,128)}, f32[256,512]{1,0:T(8,128)S(1)}, u32[]{:S(2)}, u32[]{:S(2)}) collective-permute-start(f32[256,512]{1,0:T(8,128)} %get-tuple-element.160), channel_id=1, source_target_pairs={{0,48},{8,56},{16,32},{24,40},{32,16},{40,24},{48,0},{56,8},{64,11... | collective-permute-start | bytes 1572872 | tf_op jit(solution)/shard_map/ppermute | solution.py:250
  333.9 22.4 %copy-start.32 = (f32[256,512]{1,0:T(8,128)S(1)}, f32[256,512]{1,0:T(8,128)}, u32[]{:S(2)}) copy-start(f32[256,512]{1,0:T(8,128)} %get-tuple-element.159.refs_1_) | copy-start | bytes 1572868
  337.2 33.3 %collective-permute-start.26 = (f32[256,512]{1,0:T(8,128)}, f32[256,512]{1,0:T(8,128)}, u32[]{:S(2)}, u32[]{:S(2)}) collective-permute-start(f32[256,512]{1,0:T(8,128)} %get-tuple-element.156), channel_id=1, source_target_pairs={{0,64},{8,72},{16,80},{24,88},{32,96},{40,104},{48,112},{56,120},{... | collective-permute-start | bytes 1572872 | tf_op jit(solution)/shard_map/ppermute | solution.py:250
  359.6 14.1 %collective-permute-start.28 = (f32[256,512]{1,0:T(8,128)}, f32[256,512]{1,0:T(8,128)S(1)}, u32[]{:S(2)}, u32[]{:S(2)}) collective-permute-start(f32[256,512]{1,0:T(8,128)} %get-tuple-element.162), channel_id=1, source_target_pairs={{0,64},{8,72},{16,80},{24,88},{32,96},{40,104},{48,112},{56,120},{... | collective-permute-start | bytes 1572872 | tf_op jit(solution)/shard_map/ppermute | solution.py:250
  362.4 22.9 %all-to-all-start.2 = ((f32[8,256,128]{2,1,0:T(8,128)}), f32[8,256,128]{2,1,0:T(8,128)S(1)}, u32[]{:S(2)}, u32[]{:S(2)}) async-start(f32[8,256,128]{2,1,0:T(8,128)} %total_2.1), calls=%async_computation.2 | async-start | bytes 2097152 | tf_op jit(solution)/shard_map/all_to_all | solution.py:319
  376.3 12.6 %copy-start.33 = (f32[256,128]{1,0:T(8,128)S(1)}, f32[256,128]{1,0:T(8,128)}, u32[]{:S(2)}) copy-start(f32[256,128]{1,0:T(8,128)} %reduce_sum.36) | copy-start | bytes 393220
  376.3 12.6 %copy-start.34 = (f32[256,128]{1,0:T(8,128)S(1)}, f32[256,128]{1,0:T(8,128)}, u32[]{:S(2)}) copy-start(f32[256,128]{1,0:T(8,128)} %reduce_sum.37) | copy-start | bytes 393220
  385.2 22.2 %all-to-all-start.3 = ((f32[8,256,128]{2,1,0:T(8,128)}), f32[8,256,128]{2,1,0:T(8,128)S(1)}, u32[]{:S(2)}, u32[]{:S(2)}) async-start(f32[8,256,128]{2,1,0:T(8,128)} %total_3.1), calls=%async_computation.3 | async-start | bytes 2097152 | tf_op jit(solution)/shard_map/all_to_all | solution.py:319
  389.0 20.4 %collective-permute-start.24 = (f32[3,256,128]{2,1,0:T(8,128)S(1)}, f32[3,256,128]{2,1,0:T(8,128)S(1)}, u32[]{:S(2)}, u32[]{:S(2)}) collective-permute-start(f32[3,256,128]{2,1,0:T(8,128)S(1)} %pad_maximum_fusion.1), channel_id=1, source_target_pairs={{0,16},{16,0},{40,56},{56,40},{64,80},{80,64},{104,120},{120,104},... | collective-permute-start | bytes 1179656 | tf_op jit(solution)/shard_map/ppermute | solution.py:250
  407.5 7.9 %collective-permute-start.29 = (f32[1,256,128]{2,1,0:T(8,128)S(1)}, f32[1,256,128]{2,1,0:T(8,128)S(1)}, u32[]{:S(2)}, u32[]{:S(2)}) collective-permute-start(f32[1,256,128]{2,1,0:T(8,128)S(1)} %bitcast.14), channel_id=1, source_target_pairs={{0,16},{16,0},{40,56},{56,40},{64,80},{80,64},{104,120},{120,104},... | collective-permute-start | bytes 393224 | tf_op jit(solution)/shard_map/ppermute | solution.py:250
  (23 other events, 109.7 us)

commit v3 on v2

--- a/solution.py
+++ b/solution.py
@@ -39,7 +39,7 @@
     return [pltpu.with_memory_space_constraint(array, pltpu.HBM) for array in arrays]
 
 
-def local_kernel(ranks, state, self_w, cross_w, keep_out, send_out):
+def local_kernel(ranks, state, self_w, cross_w, keep_out, *send_outs):
     count = state.shape[1]
     nodes = [state[0, n] for n in range(count)]
     for level in range(2):
@@ -50,10 +50,14 @@
     for n in range(count):
         parts = split(nodes[n])
         keep_out[n] = times(self_w[0, 2, n], parts)
-        send_out[n] = times(cross_w[0, 2, n], parts)
-
-
-def local_levels(part, parts, coefficients, self_weights, cross_weights, ranks):
+        sent = times(cross_w[0, 2, n], parts)
+        if len(send_outs) == 1:
+            send_outs[0][n] = sent
+        else:
+            send_outs[n][0] = sent
+
+
+def local_levels(part, parts, arrays, coefficients, self_weights, cross_weights, ranks):
     _, count, rank, illum = coefficients.shape
     width = illum // parts
     block = 256
@@ -70,9 +74,10 @@
                 mats,
                 mats,
             ],
-            out_specs=[out, out],
+            out_specs=[out]
+            + [pl.BlockSpec((count // arrays, rank, block), lambda i, r: (0, 0, i))] * arrays,
         ),
-        out_shape=[hbm(count, rank, width)] * 2,
+        out_shape=[hbm(count, rank, width)] + [hbm(count // arrays, rank, width)] * arrays,
         compiler_params=params(),
         cost_estimate=COST,
         name=f"local_part{part}",
@@ -128,7 +133,10 @@
         def at(i):
             return jnp.clip(i - c * steps, 0, steps - 1)
 
-        return [pl.BlockSpec((1, rank, block), lambda i, r: (node, 0, at(i)))] * 2
+        return [
+            pl.BlockSpec((1, rank, block), lambda i, r, n=n: (n, 0, at(i)))
+            for n in (node, node if pairs[c][1].shape[0] > 1 else 0)
+        ]
 
     mat = pl.BlockSpec((1, 1, 1, rank, rank), lambda i, r: (0, 3, node, 0, 0))
     out = pl.BlockSpec((rank, block), lambda i, r: (0, i))
@@ -245,6 +253,33 @@
     )(info, *[v for pair in pairs for v in pair])
 
 
+def halve_kernel(node, spot, info, kept_a, recv_a, kept_b, recv_b, keep_out, send_out):
+    for kept, recv, out in ((kept_a, recv_a, keep_out), (kept_b, recv_b, send_out)):
+        total = kept[...] + recv[...]
+        out[...] = total if node is None else masked(info[node], total)
+
+
+def halve(node, spot, info, kept, recv, groups=1):
+    rank, width = kept.shape
+    block = width // (2 * groups)
+    mine = pl.BlockSpec((rank, block), lambda i, s, r: (0, 2 * i + s[0]))
+    theirs = pl.BlockSpec((rank, block), lambda i, s, r: (0, 2 * i + s[1]))
+    out = pl.BlockSpec((rank, block), lambda i, s, r: (0, i))
+    return pl.pallas_call(
+        lambda *refs: halve_kernel(node, *refs),
+        grid_spec=pltpu.PrefetchScalarGridSpec(
+            num_scalar_prefetch=2,
+            grid=(groups,),
+            in_specs=[mine, mine, theirs, theirs],
+            out_specs=[out, out],
+        ),
+        out_shape=[hbm(rank, groups * block)] * 2,
+        compiler_params=params(),
+        cost_estimate=COST,
+        name="halve",
+    )(spot, info, kept, recv, kept, recv)
+
+
 def swap(value, axis, mask, chosen=lambda index: True):
     pairs = [(i, i ^ mask) for i in range(lax.axis_size(axis)) if chosen(i)]
     return lax.ppermute(value, axis, pairs)
@@ -265,58 +300,72 @@
 def shards(coefficients, self_weights, cross_weights, true_ranks):
     ranks = true_ranks[0]
     count = ranks.shape[0]
-    cols = lax.axis_size("col")
+    nodes, cols = lax.axis_size("node"), lax.axis_size("col")
+    col = lax.axis_index("col")
+    y0, y1, z0 = col & 1, (col >> 1) & 1, (col >> 2) & 1
+    home, across = [], []
+    for d in range(nodes):
+        to = d ^ Z1 if moves(d) else d
+        for c in range(cols):
+            across.append((d * cols + c, to * cols + (c ^ 4)))
+            if moves(d):
+                home.append((d * cols + c, to * cols + c))
     flag = moves(lax.axis_index("node")).astype(jnp.int32)
     weights = (self_weights, cross_weights)
 
     wide = [widen(0, 1, *weights)[0]]
     moved = {0: swap(wide[0], "node", Z1, moves)}
-    fetches, arrivals = {0: 1, 2: 2, 5: 3}, {3: 1, 5: 2, 7: 3}
-    sends = {1: 2, 2: 3, 3: 4, 4: 5, 6: 6, 7: 7}
-    pieces = [(node, part) for node in range(count) for part in range(PARTS)]
+    pieces = [(0, (0,)), (0, (1,)), (1, (0,)), (1, (1,)), (2, (0,)), (2, (1,)), (3, (0,)), (3, (1,))]
     final = len(pieces)
+    sends, fetches, arrivals = {1: 1, 2: 2, 3: 3, 4: 4, 5: 5, 6: 6, 7: 7}, {0: 1, 2: 2, 4: 3}, {3: 1, 5: 2, 7: 3}
+    fifths, summing = {4: (0, [0, 1]), 6: (1, [2, 3]), 7: (2, [4, 5])}, {5: 0, 7: 1}
 
     own_info = jnp.concatenate([ranks, flag[None]])
-    kept3, sent3 = {}, {}
-    first = []
+    kept3, sent3, first = {}, {}, []
+
+    def third(turn):
+        node, held_parts = pieces[turn]
+        kept3[turn], sent3[turn] = level3(node, own_info, [first[p] for p in held_parts], *weights)
+
     for part in range(PARTS):
         start = tie(ranks, sent3[0] if part else wide[0])
-        k, sent = local_levels(part, PARTS, coefficients, *weights, start)
+        k, sent = local_levels(part, PARTS, 1, coefficients, *weights, start)
         first.append((k, swap(sent, "node", CORE)))
-        kept3[part], sent3[part] = level3(0, own_info, [first[part]], *weights)
+        if part == pieces[0][1][-1]:
+            third(0)
     later_ranks, later_weights = tie(ranks, sent3[0]), tie(self_weights, sent3[0])
     wide += [widen(node, 1, later_weights, cross_weights)[0] for node in range(1, count)]
     other_ranks = swap(later_ranks, "node", Z1, moves)
     held = jnp.where(flag == 1, other_ranks, ranks)
     held_info = jnp.concatenate([held, flag[None]])
-
-    def third(turn):
-        node, part = pieces[turn]
-        return level3(node, own_info, [first[part]], *weights)
+    for turn in range(1, final):
+        third(turn)
+    r3 = {turn: swap(sent3[turn], "node", Z1) for turn in (0,)}
+    if 0 in fetches:
+        moved[fetches[0]] = swap(tie(wide[fetches[0]], sent3[0]), "node", Z1, moves)
+    kept4, sent4, r4, fives, sums, blocks_of = {}, {}, {}, {}, [], []
 
     def fourth(turn):
         node = pieces[turn][0]
         k, s = moved_level(4, node, held_info, [(kept3[turn], r3[turn])], *weights, moved[node])
-        kept4[turn], r4[turn] = k, swap(s, "node", Z1 | Z2)
-
-    def fifth(node, turns):
+        if 0 and 0 <= turn < final - 1:
+            s = tie(s, r4[turn - 0])
+        kept4[turn], sent4[turn], r4[turn] = k, s, swap(s, "node", Z1 | Z2)
+
+    def fifth(node, turns, *before):
         state = [(kept4[t], r4[t]) for t in turns]
+        if before:
+            state[0] = (tie(state[0][0], *before), state[0][1])
         k, s = moved_level(5, node, held_info, state, *weights, moved[node])
         return k, swap(s, "node", X0)
 
-    def homeward(group):
-        mine = jnp.stack(group)
-        return jnp.where(flag == 1, swap(mine, "node", Z1, moves), mine)
-
-    for turn in range(PARTS, final):
-        kept3[turn], sent3[turn] = third(turn)
-    r3 = {turn: swap(sent3[turn], "node", Z1) for turn in (0, 1)}
-    moved[1] = swap(tie(wide[1], sent3[1]), "node", Z1, moves)
-    kept4, r4, fives, sums = {}, {}, {}, []
-
     def column_sum(node, terms):
         blocks = total(node, held_info, terms, cols)
+        blocks_of.append(blocks)
         sums.append(jnp.sum(lax.all_to_all(blocks, "col", 0, 0, tiled=True), axis=0))
+
+    def homeward(mine):
+        return jnp.where(flag == 1, swap(mine, "node", Z1, moves), mine)
 
     for turn in range(1, final):
         values = {"r3": r3[turn - 1]}
@@ -326,11 +375,11 @@
             values["wide"] = wide[fetches[turn]]
         if turn in arrivals:
             values["moved"] = moved[arrivals[turn]]
-        if turn >= 2:
-            values["r4"] = r4[turn - 2]
-        if turn == 6:
+        if 3 and turn >= 3:
+            values["r4"] = r4[turn - 3]
+        if turn == 7:
             values["sum"] = sums[0]
-        summed = {4: 0, 6: 1}.get(turn)
+        summed = summing.get(turn)
         if summed is not None:
             values["five"] = fives[summed][1]
         values = dict(zip(values, lax.optimization_barrier(tuple(values.values()))))
@@ -341,23 +390,43 @@
             moved[arrivals[turn]] = values["moved"]
         if turn in fetches:
             moved[fetches[turn]] = swap(values["wide"], "node", Z1, moves)
-        if turn >= 2:
-            r4[turn - 2] = values["r4"]
-        if turn == 6:
+        if "r4" in values:
+            r4[turn - 3] = values["r4"]
+        if "sum" in values:
             sums[0] = values["sum"]
         fourth(turn - 1)
-        if turn in (3, 5, 7):
-            node = (turn - 3) // 2
-            fives[node] = fifth(node, [turn - 3, turn - 2])
+        if turn in fifths:
+            node, turns = fifths[turn]
+            fives[node] = fifth(node, turns, *([sent4[turn - 1]] if False else []))
         if summed is not None:
             column_sum(summed, [(fives[summed][0], values["five"])])
 
     r3[final - 1], sums[1] = lax.optimization_barrier((r3[final - 1], sums[1]))
     fourth(final - 1)
-    ends = [fifth(count - 1, [final - 2]), fifth(count - 1, [final - 1])]
-    for node, terms in ((count - 2, [fives[count - 2]]), (count - 1, ends)):
-        column_sum(node, terms)
-    return jnp.concatenate([homeward(sums[: count - 1]), homeward(sums[count - 1 :])])
+    ends = [fifth(count - 1, [final - 2], *([sent4[final - 1]] if False else []))]
+    column_sum(count - 2, [fives[count - 2]])
+    kept4[final - 1] = tie(kept4[final - 1], blocks_of[-1])
+    ends.append(fifth(count - 1, [final - 1]))
+    early = jnp.stack(sums)
+
+    def spot(bit):
+        return jnp.stack([bit, 1 - bit]).astype(jnp.int32)
+
+    quarters, before = [], [early] if False else []
+    for k, r in ends:
+        if quarters and before:
+            k = tie(k, *before)
+        k, s = halve(count - 1, spot(y1), held_info, k, r)
+        k, s = halve(None, spot(y0), held_info, k, swap(s, "col", 2))
+        if False:
+            before.append(s)
+        quarters.append(k + swap(s, "col", 1))
+    mine = jnp.where(z0 == 1, quarters[1], quarters[0])
+    theirs = jnp.where(z0 == 1, quarters[0], quarters[1])
+    away = lax.ppermute(mine, ("node", "col"), home)
+    other = lax.ppermute(theirs, ("node", "col"), across)
+    end = jnp.where(flag == 1, away, mine) + other
+    return jnp.concatenate([homeward(early), end[None]])
 
 
 def solution(mesh):

time: 418 us -> 410 us (0.981)
  waiting for transfers between devices: 227 us -> 182 us
  starting transfers between devices: 74.3 us -> 104 us
    all_to_all x4 -> x3, waiting for transfers between devices: 33.5 us -> 0.01 us  [column_sum(): lax.all_to_all(blocks, 'col', 0, 0, tiled=True)]
    ppermute x30 -> x33, starting transfers between devices: 52.1 us -> 78 us  [swap(): return lax.ppermute(value, axis, pairs)]
    ppermute x30 -> x33, waiting for transfers between devices: 193 us -> 176 us  [swap(): return lax.ppermute(value, axis, pairs)]
    pallas_call x0 -> x4, Pallas kernels: none -> 6.45 us  [halve(): pl.pallas_call(lambda *refs: halve_kernel(node, *refs), grid_spec=pltpu.P...]
    ppermute x0 -> x2, waiting for transfers between devices: none -> 5.77 us  [the longest x1 4.53 us: shards(): away = lax.ppermute(mine, ('node', 'col'), home)]
    ppermute x0 -> x2, starting transfers between devices: none -> 5.54 us  [the longest x1 3.63 us: shards(): other = lax.ppermute(theirs, ('node', 'col'), across)]
    pallas_call x4 -> x3, Pallas kernels: 9.14 us -> 6.36 us  [total(): pl.pallas_call(lambda *refs: total_kernel(node, count, *refs), grid_spec=...]
    all_to_all x4 -> x3, starting transfers between devices: 22.1 us -> 20.5 us  [column_sum(): lax.all_to_all(blocks, 'col', 0, 0, tiled=True)]
  transfers between devices with their start and end apart: 34 -> 38, of which waited for: 20 -> 17; matrix products, arithmetic and copies ran while one was open for 1% -> 2% of each run, Pallas kernels for 23% -> 25%
where the time goes in v3:
time: 410 us; the launch traced here: 409 us
  waiting for transfers between devices  182 us (44%)
  Pallas kernels  111 us (27%)
  starting transfers between devices  104 us (25%)
  other arithmetic  8.66 us (2%)
    ppermute x33, waiting for transfers between devices, swap(): return lax.ppermute(value, axis, pairs)  176 us
    ppermute x33, starting transfers between devices, swap(): return lax.ppermute(value, axis, pairs)  78 us
    pallas_call x13, Pallas kernels, moved_level(): pl.pallas_call(lambda *refs: moved_kernel(node, count, *refs), grid_spec=...  48.6 us
    pallas_call x8, Pallas kernels, level3(): pl.pallas_call(lambda *refs: level3_kernel(node, count, *refs), grid_spec...  25.1 us
    all_to_all x3, starting transfers between devices, column_sum(): lax.all_to_all(blocks, 'col', 0, 0, tiled=True)  20.5 us
    pallas_call x2, Pallas kernels, local_levels(): pl.pallas_call(local_kernel, grid_spec=pltpu.PrefetchScalarGridSpec(num_s...  16.3 us
    pallas_call x4, Pallas kernels, widen(): pl.pallas_call(widen_kernel, grid=(1,), in_specs=[mats, mats], out_specs=...  8.39 us
  transfers between devices with their start and end apart: 38, of which 17 were waited for; matrix products, arithmetic and copies ran while one was open for 2% of the time, Pallas kernels for 25%

profile of v3, /device:TPU:2, one launch (start us, length us, event | category | flops | bytes accessed | tf_op | source)
XLA Modules:
  0.0 408.9 jit_solution(1649694355076047231)
XLA Ops:
  2.1 8.1 %local_part0.1 = (f32[4,256,512]{2,1,0:T(8,128)}, f32[4,256,512]{2,1,0:T(8,128)}) custom-call(s32[4]{0:T(128)} %bitcast.ranks, f32[1,4,256,1024]{3,2,1,0:T(8,128)} %state.3, bf16[1,6,4,256,256]{4,3,2,1,0:T(8,128)(2,1)} %refs_3_.35, bf16[1,6,4,256,256]{4,3,2,1,0:T(8,128)(2,1)} %refs_4_.35), custom_call_target="tpu_custom_call" | custom-call | flops 99999997952 | bytes 1000000000 | tf_op jit(solution)/shard_map/local_part0/pallas_call | solution.py:67
  10.3 5.2 %collective-permute-start.7 = (f32[2,2,256,256]{3,2,1,0:T(8,128)}, f32[2,2,256,256]{3,2,1,0:T(8,128)}, u32[]{:S(2)}, u32[]{:S(2)}) collective-permute-start(f32[2,2,256,256]{3,2,1,0:T(8,128)} %widen_0.1), channel_id=1, source_target_pairs={{0,16},{16,0},{40,56},{56,40},{64,80},{80,64},{104,120},{120,104},... | collective-permute-start | bytes 3145736 | tf_op jit(solution)/shard_map/ppermute | solution.py:285
  17.9 3.1 level3_0.2
  28.9 3.4 collective-permute-start.6
  32.3 8.2 %local_part1.1 = (f32[4,256,512]{2,1,0:T(8,128)}, f32[4,256,512]{2,1,0:T(8,128)}) custom-call(s32[4]{0:T(128)} %bitcast.ranks, f32[1,4,256,1024]{3,2,1,0:T(8,128)} %state.3, bf16[1,6,4,256,256]{4,3,2,1,0:T(8,128)(2,1)} %refs_3_.35, bf16[1,6,4,256,256]{4,3,2,1,0:T(8,128)(2,1)} %refs_4_.35), custom_call_target="tpu_custom_call" | custom-call | flops 99999997952 | bytes 1000000000 | tf_op jit(solution)/shard_map/local_part1/pallas_call | solution.py:67
  40.5 3.5 collective-permute-start.5
  50.3 3.1 level3_1.2
  53.4 20.1 %collective-permute-done.6 = s32[4]{0:T(128)} collective-permute-done((s32[4]{0:T(128)}, s32[4]{0:T(128)}, u32[]{:S(2)}, u32[]{:S(2)}) %collective-permute-start.6) | collective-permute-done | bytes 48 | tf_op jit(solution)/shard_map/ppermute | solution.py:285
  74.9 3.2 level3_0.3
  78.1 3.4 level4_0.2
  81.5 3.1 level3_3.3
  84.7 3.2 level3_2.3
  87.9 3.2 level3_1.3
  91.1 6.3 %collective-permute-done.3.refs_2_ = f32[256,512]{1,0:T(8,128)} collective-permute-done((f32[256,512]{1,0:T(8,128)}, f32[256,512]{1,0:T(8,128)}, u32[]{:S(2)}, u32[]{:S(2)}) %collective-permute-start.3) | collective-permute-done | bytes 524320 | tf_op jit(solution)/shard_map/ppermute | solution.py:285
  98.6 3.4 level4_0.3
  102.0 13.5 %collective-permute-start.10 = (f32[256,512]{1,0:T(8,128)}, f32[256,512]{1,0:T(8,128)S(1)}, u32[]{:S(2)}, u32[]{:S(2)}) collective-permute-start(f32[256,512]{1,0:T(8,128)} %get-tuple-element.114), channel_id=1, source_target_pairs={{0,48},{8,56},{16,32},{24,40},{32,16},{40,24},{48,0},{56,8},{64,11... | collective-permute-start | bytes 1572872 | tf_op jit(solution)/shard_map/ppermute | solution.py:285
  115.5 4.8 %collective-permute-start.12 = (f32[2,2,256,256]{3,2,1,0:T(8,128)}, f32[2,2,256,256]{3,2,1,0:T(8,128)}, u32[]{:S(2)}, u32[]{:S(2)}) collective-permute-start(f32[2,2,256,256]{3,2,1,0:T(8,128)} %widen_2.1), channel_id=1, source_target_pairs={{0,16},{16,0},{40,56},{56,40},{64,80},{80,64},{104,120},{120,104},... | collective-permute-start | bytes 3145736 | tf_op jit(solution)/shard_map/ppermute | solution.py:285
  120.5 3.4 level4_1.2
  123.9 13.9 %collective-permute-start.13 = (f32[256,512]{1,0:T(8,128)}, f32[256,512]{1,0:T(8,128)}, u32[]{:S(2)}, u32[]{:S(2)}) collective-permute-start(f32[256,512]{1,0:T(8,128)} %get-tuple-element.121), channel_id=1, source_target_pairs={{0,48},{8,56},{16,32},{24,40},{32,16},{40,24},{48,0},{56,8},{64,11... | collective-permute-start | bytes 1572872 | tf_op jit(solution)/shard_map/ppermute | solution.py:285
  137.8 51.8 %collective-permute-done.9.refs_2_ = f32[256,512]{1,0:T(8,128)S(1)} collective-permute-done((f32[256,512]{1,0:T(8,128)S(1)}, f32[256,512]{1,0:T(8,128)S(1)}, u32[]{:S(2)}, u32[]{:S(2)}) %collective-permute-start.9) | collective-permute-done | bytes 524320 | tf_op jit(solution)/shard_map/ppermute | solution.py:285
  189.6 4.6 %level5_0.1 = (f32[256,1024]{1,0:T(8,128)}, f32[256,1024]{1,0:T(8,128)}) custom-call(s32[5]{0:T(128)S(1)} %pad_add_fusion.1.refs_0_.refs_1_, f32[256,512]{1,0:T(8,128)S(1)} %copy-done.20, f32[256,512]{1,0:T(8,128)} %collective-permute-done.8.refs_2_, f32[256,512]{1,0:T(8,128)S(1)} %copy-done.23, f32[256,512]{1,0:T(8,128)S(1)} %collective-permute-done.10.refs_4_, ...), custom_call_target="tpu_custom_call" | custom-call | flops 99999997952 | bytes 1000000000 | tf_op jit(solution)/shard_map/level5_0/pallas_call | solution.py:198
  194.2 3.4 level4_1.3
  197.6 4.8 %collective-permute-start.18 = (f32[2,2,256,256]{3,2,1,0:T(8,128)}, f32[2,2,256,256]{3,2,1,0:T(8,128)}, u32[]{:S(2)}, u32[]{:S(2)}) collective-permute-start(f32[2,2,256,256]{3,2,1,0:T(8,128)} %widen_3.1), channel_id=1, source_target_pairs={{0,16},{16,0},{40,56},{56,40},{64,80},{80,64},{104,120},{120,104},... | collective-permute-start | bytes 3145736 | tf_op jit(solution)/shard_map/ppermute | solution.py:285
  205.5 3.7 collective-permute-done.14.refs_2_
  211.1 7.3 %all-to-all-start = ((f32[8,256,128]{2,1,0:T(8,128)}), f32[8,256,128]{2,1,0:T(8,128)}, u32[]{:S(2)}, u32[]{:S(2)}) async-start(f32[8,256,128]{2,1,0:T(8,128)} %total_0.1), calls=%async_computation | async-start | bytes 2097152 | tf_op jit(solution)/shard_map/all_to_all | solution.py:365
  218.7 3.4 level4_2.2
  222.1 13.2 %collective-permute-done.16.refs_4_ = f32[256,512]{1,0:T(8,128)} collective-permute-done((f32[256,512]{1,0:T(8,128)}, f32[256,512]{1,0:T(8,128)}, u32[]{:S(2)}, u32[]{:S(2)}) %collective-permute-start.16) | collective-permute-done | bytes 524320 | tf_op jit(solution)/shard_map/ppermute | solution.py:285
  235.2 28.6 %collective-permute-done.15.refs_2_ = f32[256,512]{1,0:T(8,128)S(1)} collective-permute-done((f32[256,512]{1,0:T(8,128)S(1)}, f32[256,512]{1,0:T(8,128)S(1)}, u32[]{:S(2)}, u32[]{:S(2)}) %collective-permute-start.15) | collective-permute-done | bytes 524320 | tf_op jit(solution)/shard_map/ppermute | solution.py:285
  263.8 3.4 collective-permute-start.17
  267.2 5.2 %level5_1.1 = (f32[256,1024]{1,0:T(8,128)}, f32[256,1024]{1,0:T(8,128)}) custom-call(s32[5]{0:T(128)S(1)} %copy-done.1, f32[256,512]{1,0:T(8,128)S(1)} %copy-done.18, f32[256,512]{1,0:T(8,128)} %collective-permute-done.13.refs_2_, f32[256,512]{1,0:T(8,128)S(1)} %copy-done.21, f32[256,512]{1,0:T(8,128)} %collective-permute-done.16.refs_4_, ...), custom_call_target="tpu_custom_call" | custom-call | flops 99999997952 | bytes 1000000000 | tf_op jit(solution)/shard_map/level5_1/pallas_call | solution.py:198
  273.8 3.3 level4_2.3
  280.4 7.0 %collective-permute-done.20.refs_2_ = f32[256,1024]{1,0:T(8,128)S(1)} collective-permute-done((f32[256,1024]{1,0:T(8,128)}, f32[256,1024]{1,0:T(8,128)S(1)}, u32[]{:S(2)}, u32[]{:S(2)}) %collective-permute-start.20) | collective-permute-done | bytes 1048608 | tf_op jit(solution)/shard_map/ppermute | solution.py:285
  289.2 4.5 %all-to-all-start.1 = ((f32[8,256,128]{2,1,0:T(8,128)}), f32[8,256,128]{2,1,0:T(8,128)}, u32[]{:S(2)}, u32[]{:S(2)}) async-start(f32[8,256,128]{2,1,0:T(8,128)} %total_1.1), calls=%async_computation.1 | async-start | bytes 2097152 | tf_op jit(solution)/shard_map/all_to_all | solution.py:365
  293.8 3.3 level4_3.3
  301.5 5.2 %level5_2.1 = (f32[256,1024]{1,0:T(8,128)}, f32[256,1024]{1,0:T(8,128)}) custom-call(s32[5]{0:T(128)S(1)} %copy-done.1, f32[256,512]{1,0:T(8,128)S(1)} %copy-done.19, f32[256,512]{1,0:T(8,128)} %collective-permute-done.19.refs_2_, f32[256,512]{1,0:T(8,128)S(1)} %copy-done.22, f32[256,512]{1,0:T(8,128)} %collective-permute-done.22.refs_4_, ...), custom_call_target="tpu_custom_call" | custom-call | flops 99999997952 | bytes 1000000000 | tf_op jit(solution)/shard_map/level5_2/pallas_call | solution.py:198
  307.2 17.1 %collective-permute-done.29.refs_2_ = f32[256,512]{1,0:T(8,128)S(1)} collective-permute-done((f32[256,512]{1,0:T(8,128)}, f32[256,512]{1,0:T(8,128)S(1)}, u32[]{:S(2)}, u32[]{:S(2)}) %collective-permute-start.29) | collective-permute-done | bytes 524320 | tf_op jit(solution)/shard_map/ppermute | solution.py:285
  324.3 3.3 level5_3.3
  332.4 3.4 level4_3.2
  339.3 8.7 %all-to-all-start.2 = ((f32[8,256,128]{2,1,0:T(8,128)}), f32[8,256,128]{2,1,0:T(8,128)}, u32[]{:S(2)}, u32[]{:S(2)}) async-start(f32[8,256,128]{2,1,0:T(8,128)} %total_2.1), calls=%async_computation.2 | async-start | bytes 2097152 | tf_op jit(solution)/shard_map/all_to_all | solution.py:365
  348.0 10.5 %collective-permute-done.25.refs_2_ = f32[256,512]{1,0:T(8,128)S(1)} collective-permute-done((f32[256,512]{1,0:T(8,128)}, f32[256,512]{1,0:T(8,128)S(1)}, u32[]{:S(2)}, u32[]{:S(2)}) %collective-permute-start.25) | collective-permute-done | bytes 524320 | tf_op jit(solution)/shard_map/ppermute | solution.py:285
  358.5 3.3 level5_3.2
  364.6 4.0 collective-permute-start.31
  368.6 7.1 %collective-permute-done.26.refs_3_.refs_5_ = f32[256,512]{1,0:T(8,128)S(1)} collective-permute-done((f32[256,512]{1,0:T(8,128)}, f32[256,512]{1,0:T(8,128)S(1)}, u32[]{:S(2)}, u32[]{:S(2)}) %collective-permute-start.26) | collective-permute-done | bytes 524320 | tf_op jit(solution)/shard_map/ppermute | solution.py:285
  377.1 4.7 %collective-permute-start.27 = (f32[256,256]{1,0:T(8,128)}, f32[256,256]{1,0:T(8,128)S(1)}, u32[]{:S(2)}, u32[]{:S(2)}) collective-permute-start(f32[256,256]{1,0:T(8,128)} %get-tuple-element.168), channel_id=1, source_target_pairs={{0,2},{1,3},{2,0},{3,1},{4,6},{5,7},{6,4},{7,5},{8,10},{9,11},{10,... | collective-permute-start | bytes 786440 | tf_op jit(solution)/shard_map/ppermute | solution.py:285
  385.3 3.4 collective-permute-start.24
  392.3 3.4 collective-permute-done.28
  396.6 3.6 collective-permute-start.34
  403.5 4.5 %collective-permute-done.33 = f32[256,128]{1,0:T(8,128)S(1)} collective-permute-done((f32[256,128]{1,0:T(8,128)S(1)}, f32[256,128]{1,0:T(8,128)S(1)}, u32[]{:S(2)}, u32[]{:S(2)}) %collective-permute-start.33) | collective-permute-done | bytes 131104 | tf_op jit(solution)/shard_map/ppermute | solution.py:426
  (147 shorter events, 62.6 us)
Async XLA Ops:
  10.3 6.1 %collective-permute-start = (f32[4,256,512]{2,1,0:T(8,128)}, f32[4,256,512]{2,1,0:T(8,128)S(1)}, u32[]{:S(2)}, u32[]{:S(2)}) collective-permute-start(f32[4,256,512]{2,1,0:T(8,128)} %get-tuple-element.95), channel_id=1, source_target_pairs={{0,8},{8,0},{16,24},{24,16},{32,40},{40,32},{48,56},{56,48},{64,72... | collective-permute-start | bytes 6291464 | tf_op jit(solution)/shard_map/ppermute | solution.py:285
  10.3 67.8 %collective-permute-start.7 = (f32[2,2,256,256]{3,2,1,0:T(8,128)}, f32[2,2,256,256]{3,2,1,0:T(8,128)}, u32[]{:S(2)}, u32[]{:S(2)}) collective-permute-start(f32[2,2,256,256]{3,2,1,0:T(8,128)} %widen_0.1), channel_id=1, source_target_pairs={{0,16},{16,0},{40,56},{56,40},{64,80},{80,64},{104,120},{120,104},... | collective-permute-start | bytes 3145736 | tf_op jit(solution)/shard_map/ppermute | solution.py:285
  16.2 34.1 %copy-start.2 = (s32[5]{0:T(128)}, s32[5]{0:T(128)S(1)}, u32[]{:S(2)}) copy-start(s32[5]{0:T(128)S(1)} %pad_add_fusion.refs_0_) | copy-start | bytes 64
  21.1 57.0 %collective-permute-start.1 = (f32[256,512]{1,0:T(8,128)}, f32[256,512]{1,0:T(8,128)}, u32[]{:S(2)}, u32[]{:S(2)}) collective-permute-start(f32[256,512]{1,0:T(8,128)} %get-tuple-element.96), channel_id=1, source_target_pairs={{0,16},{8,24},{16,0},{24,8},{32,48},{40,56},{48,32},{56,40},{64,80... | collective-permute-start | bytes 1572872 | tf_op jit(solution)/shard_map/ppermute | solution.py:285
  28.9 44.6 %collective-permute-start.6 = (s32[4]{0:T(128)}, s32[4]{0:T(128)}, u32[]{:S(2)}, u32[]{:S(2)}) collective-permute-start(s32[4]{0:T(128)} %bitcast.ranks), channel_id=1, source_target_pairs={{0,16},{16,0},{40,56},{56,40},{64,80},{80,64},{104,120},{120,104},... | collective-permute-start | bytes 56 | tf_op jit(solution)/shard_map/ppermute | solution.py:285
  40.5 79.8 %collective-permute-start.5 = (f32[2,2,256,256]{3,2,1,0:T(8,128)}, f32[2,2,256,256]{3,2,1,0:T(8,128)}, u32[]{:S(2)}, u32[]{:S(2)}) collective-permute-start(f32[2,2,256,256]{3,2,1,0:T(8,128)} %widen_1.1), channel_id=1, source_target_pairs={{0,16},{16,0},{40,56},{56,40},{64,80},{80,64},{104,120},{120,104},... | collective-permute-start | bytes 3145736 | tf_op jit(solution)/shard_map/ppermute | solution.py:285
  44.0 30.3 %collective-permute-start.2 = (f32[4,256,512]{2,1,0:T(8,128)}, f32[4,256,512]{2,1,0:T(8,128)}, u32[]{:S(2)}, u32[]{:S(2)}) collective-permute-start(f32[4,256,512]{2,1,0:T(8,128)} %get-tuple-element.99), channel_id=1, source_target_pairs={{0,8},{8,0},{16,24},{24,16},{32,40},{40,32},{48,56},{56,48},{64,72... | collective-permute-start | bytes 6291464 | tf_op jit(solution)/shard_map/ppermute | solution.py:285
  50.3 24.0 %copy-start.6 = (f32[4,256,512]{2,1,0:T(8,128)S(1)}, f32[4,256,512]{2,1,0:T(8,128)}, u32[]{:S(2)}) copy-start(f32[4,256,512]{2,1,0:T(8,128)} %get-tuple-element.98.refs_1_) | copy-start | bytes 6291460
  74.3 135.0 %copy-start = (s32[5]{0:T(128)}, s32[5]{0:T(128)S(1)}, u32[]{:S(2)}) copy-start(s32[5]{0:T(128)S(1)} %pad_add_fusion.1.refs_0_.refs_1_) | copy-start | bytes 64
  81.5 38.8 %collective-permute-start.8 = (f32[256,512]{1,0:T(8,128)}, f32[256,512]{1,0:T(8,128)}, u32[]{:S(2)}, u32[]{:S(2)}) collective-permute-start(f32[256,512]{1,0:T(8,128)} %get-tuple-element.109), channel_id=1, source_target_pairs={{0,48},{8,56},{16,32},{24,40},{32,16},{40,24},{48,0},{56,8},{64,11... | collective-permute-start | bytes 1572872 | tf_op jit(solution)/shard_map/ppermute | solution.py:285
  81.5 15.9 %collective-permute-start.3 = (f32[256,512]{1,0:T(8,128)}, f32[256,512]{1,0:T(8,128)}, u32[]{:S(2)}, u32[]{:S(2)}) collective-permute-start(f32[256,512]{1,0:T(8,128)} %get-tuple-element.101), channel_id=1, source_target_pairs={{0,16},{8,24},{16,0},{24,8},{32,48},{40,56},{48,32},{56,40},{64,80... | collective-permute-start | bytes 1572872 | tf_op jit(solution)/shard_map/ppermute | solution.py:285
  97.4 22.9 %collective-permute-start.4 = (f32[256,512]{1,0:T(8,128)S(1)}, f32[256,512]{1,0:T(8,128)S(1)}, u32[]{:S(2)}, u32[]{:S(2)}) collective-permute-start(f32[256,512]{1,0:T(8,128)S(1)} %copy-done.34), channel_id=1, source_target_pairs={{0,16},{8,24},{16,0},{24,8},{32,48},{40,56},{48,32},{56,40},{64,80... | collective-permute-start | bytes 1572872 | tf_op jit(solution)/shard_map/ppermute | solution.py:285
  98.6 21.7 %copy-start.35 = (f32[256,512]{1,0:T(8,128)S(1)}, f32[256,512]{1,0:T(8,128)}, u32[]{:S(2)}) copy-start(f32[256,512]{1,0:T(8,128)} %get-tuple-element.110) | copy-start | bytes 1572868
  98.6 21.8 %copy-start.14 = (f32[256,512]{1,0:T(8,128)S(1)}, f32[256,512]{1,0:T(8,128)}, u32[]{:S(2)}) copy-start(f32[256,512]{1,0:T(8,128)} %get-tuple-element.118.refs_1_) | copy-start | bytes 1572868
  102.0 35.8 %collective-permute-start.10 = (f32[256,512]{1,0:T(8,128)}, f32[256,512]{1,0:T(8,128)S(1)}, u32[]{:S(2)}, u32[]{:S(2)}) collective-permute-start(f32[256,512]{1,0:T(8,128)} %get-tuple-element.114), channel_id=1, source_target_pairs={{0,48},{8,56},{16,32},{24,40},{32,16},{40,24},{48,0},{56,8},{64,11... | collective-permute-start | bytes 1572872 | tf_op jit(solution)/shard_map/ppermute | solution.py:285
  115.5 86.9 %collective-permute-start.12 = (f32[2,2,256,256]{3,2,1,0:T(8,128)}, f32[2,2,256,256]{3,2,1,0:T(8,128)}, u32[]{:S(2)}, u32[]{:S(2)}) collective-permute-start(f32[2,2,256,256]{3,2,1,0:T(8,128)} %widen_2.1), channel_id=1, source_target_pairs={{0,16},{16,0},{40,56},{56,40},{64,80},{80,64},{104,120},{120,104},... | collective-permute-start | bytes 3145736 | tf_op jit(solution)/shard_map/ppermute | solution.py:285
  120.3 69.2 %collective-permute-start.9 = (f32[256,512]{1,0:T(8,128)S(1)}, f32[256,512]{1,0:T(8,128)S(1)}, u32[]{:S(2)}, u32[]{:S(2)}) collective-permute-start(f32[256,512]{1,0:T(8,128)S(1)} %copy-done.35), channel_id=1, source_target_pairs={{0,16},{8,24},{16,0},{24,8},{32,48},{40,56},{48,32},{56,40},{64,80... | collective-permute-start | bytes 1572872 | tf_op jit(solution)/shard_map/ppermute | solution.py:285
  120.5 69.1 %copy-start.20 = (f32[256,512]{1,0:T(8,128)S(1)}, f32[256,512]{1,0:T(8,128)}, u32[]{:S(2)}) copy-start(f32[256,512]{1,0:T(8,128)} %get-tuple-element.122.refs_1_) | copy-start | bytes 1572868
  120.5 69.1 %copy-start.23 = (f32[256,512]{1,0:T(8,128)S(1)}, f32[256,512]{1,0:T(8,128)}, u32[]{:S(2)}) copy-start(f32[256,512]{1,0:T(8,128)} %get-tuple-element.124.refs_3_) | copy-start | bytes 1572868
  123.9 73.7 %collective-permute-start.13 = (f32[256,512]{1,0:T(8,128)}, f32[256,512]{1,0:T(8,128)}, u32[]{:S(2)}, u32[]{:S(2)}) collective-permute-start(f32[256,512]{1,0:T(8,128)} %get-tuple-element.121), channel_id=1, source_target_pairs={{0,48},{8,56},{16,32},{24,40},{32,16},{40,24},{48,0},{56,8},{64,11... | collective-permute-start | bytes 1572872 | tf_op jit(solution)/shard_map/ppermute | solution.py:285
  189.6 15.9 %collective-permute-start.11 = (f32[256,512]{1,0:T(8,128)}, f32[256,512]{1,0:T(8,128)}, u32[]{:S(2)}, u32[]{:S(2)}) collective-permute-start(f32[256,512]{1,0:T(8,128)} %get-tuple-element.115), channel_id=1, source_target_pairs={{0,16},{8,24},{16,0},{24,8},{32,48},{40,56},{48,32},{56,40},{64,80... | collective-permute-start | bytes 1572872 | tf_op jit(solution)/shard_map/ppermute | solution.py:285
  194.2 15.0 %collective-permute-start.14 = (f32[256,1024]{1,0:T(8,128)}, f32[256,1024]{1,0:T(8,128)S(1)}, u32[]{:S(2)}, u32[]{:S(2)}) collective-permute-start(f32[256,1024]{1,0:T(8,128)} %get-tuple-element.126), channel_id=1, source_target_pairs={{0,64},{8,72},{16,80},{24,88},{32,96},{40,104},{48,112},{56,120},{... | collective-permute-start | bytes 3145736 | tf_op jit(solution)/shard_map/ppermute | solution.py:285
  197.6 37.6 %collective-permute-start.16 = (f32[256,512]{1,0:T(8,128)}, f32[256,512]{1,0:T(8,128)}, u32[]{:S(2)}, u32[]{:S(2)}) collective-permute-start(f32[256,512]{1,0:T(8,128)} %get-tuple-element.131), channel_id=1, source_target_pairs={{0,48},{8,56},{16,32},{24,40},{32,16},{40,24},{48,0},{56,8},{64,11... | collective-permute-start | bytes 1572872 | tf_op jit(solution)/shard_map/ppermute | solution.py:285
  197.6 81.5 %collective-permute-start.18 = (f32[2,2,256,256]{3,2,1,0:T(8,128)}, f32[2,2,256,256]{3,2,1,0:T(8,128)}, u32[]{:S(2)}, u32[]{:S(2)}) collective-permute-start(f32[2,2,256,256]{3,2,1,0:T(8,128)} %widen_3.1), channel_id=1, source_target_pairs={{0,16},{16,0},{40,56},{56,40},{64,80},{80,64},{104,120},{120,104},... | collective-permute-start | bytes 3145736 | tf_op jit(solution)/shard_map/ppermute | solution.py:285
  211.1 66.1 %all-to-all-start = ((f32[8,256,128]{2,1,0:T(8,128)}), f32[8,256,128]{2,1,0:T(8,128)}, u32[]{:S(2)}, u32[]{:S(2)}) async-start(f32[8,256,128]{2,1,0:T(8,128)} %total_0.1), calls=%async_computation | async-start | bytes 2097152 | tf_op jit(solution)/shard_map/all_to_all | solution.py:365
  218.4 45.4 %collective-permute-start.15 = (f32[256,512]{1,0:T(8,128)S(1)}, f32[256,512]{1,0:T(8,128)S(1)}, u32[]{:S(2)}, u32[]{:S(2)}) collective-permute-start(f32[256,512]{1,0:T(8,128)S(1)} %copy-done.33), channel_id=1, source_target_pairs={{0,16},{8,24},{16,0},{24,8},{32,48},{40,56},{48,32},{56,40},{64,80... | collective-permute-start | bytes 1572872 | tf_op jit(solution)/shard_map/ppermute | solution.py:285
  218.7 48.6 %copy-start.18 = (f32[256,512]{1,0:T(8,128)S(1)}, f32[256,512]{1,0:T(8,128)}, u32[]{:S(2)}) copy-start(f32[256,512]{1,0:T(8,128)} %get-tuple-element.141.refs_1_) | copy-start | bytes 1572868
  218.7 48.6 %copy-start.21 = (f32[256,512]{1,0:T(8,128)S(1)}, f32[256,512]{1,0:T(8,128)}, u32[]{:S(2)}) copy-start(f32[256,512]{1,0:T(8,128)} %get-tuple-element.143.refs_3_) | copy-start | bytes 1572868
  222.1 57.0 %collective-permute-start.19 = (f32[256,512]{1,0:T(8,128)}, f32[256,512]{1,0:T(8,128)}, u32[]{:S(2)}, u32[]{:S(2)}) collective-permute-start(f32[256,512]{1,0:T(8,128)} %get-tuple-element.138), channel_id=1, source_target_pairs={{0,48},{8,56},{16,32},{24,40},{32,16},{40,24},{48,0},{56,8},{64,11... | collective-permute-start | bytes 1572872 | tf_op jit(solution)/shard_map/ppermute | solution.py:285
  263.8 16.6 %collective-permute-start.17 = (f32[256,512]{1,0:T(8,128)}, f32[256,512]{1,0:T(8,128)}, u32[]{:S(2)}, u32[]{:S(2)}) collective-permute-start(f32[256,512]{1,0:T(8,128)} %get-tuple-element.132), channel_id=1, source_target_pairs={{0,16},{8,24},{16,0},{24,8},{32,48},{40,56},{48,32},{56,40},{64,80... | collective-permute-start | bytes 1572872 | tf_op jit(solution)/shard_map/ppermute | solution.py:285
  272.4 15.0 %collective-permute-start.20 = (f32[256,1024]{1,0:T(8,128)}, f32[256,1024]{1,0:T(8,128)S(1)}, u32[]{:S(2)}, u32[]{:S(2)}) collective-permute-start(f32[256,1024]{1,0:T(8,128)} %get-tuple-element.145), channel_id=1, source_target_pairs={{0,64},{8,72},{16,80},{24,88},{32,96},{40,104},{48,112},{56,120},{... | collective-permute-start | bytes 3145736 | tf_op jit(solution)/shard_map/ppermute | solution.py:285
  277.1 24.3 %collective-permute-start.22 = (f32[256,512]{1,0:T(8,128)}, f32[256,512]{1,0:T(8,128)}, u32[]{:S(2)}, u32[]{:S(2)}) collective-permute-start(f32[256,512]{1,0:T(8,128)} %get-tuple-element.156), channel_id=1, source_target_pairs={{0,48},{8,56},{16,32},{24,40},{32,16},{40,24},{48,0},{56,8},{64,11... | collective-permute-start | bytes 1572872 | tf_op jit(solution)/shard_map/ppermute | solution.py:285
  289.2 41.3 %all-to-all-start.1 = ((f32[8,256,128]{2,1,0:T(8,128)}), f32[8,256,128]{2,1,0:T(8,128)}, u32[]{:S(2)}, u32[]{:S(2)}) async-start(f32[8,256,128]{2,1,0:T(8,128)} %total_1.1), calls=%async_computation.1 | async-start | bytes 2097152 | tf_op jit(solution)/shard_map/all_to_all | solution.py:365
  297.1 27.2 %collective-permute-start.29 = (f32[256,512]{1,0:T(8,128)}, f32[256,512]{1,0:T(8,128)S(1)}, u32[]{:S(2)}, u32[]{:S(2)}) collective-permute-start(f32[256,512]{1,0:T(8,128)} %get-tuple-element.174), channel_id=1, source_target_pairs={{0,48},{8,56},{16,32},{24,40},{32,16},{40,24},{48,0},{56,8},{64,11... | collective-permute-start | bytes 1572872 | tf_op jit(solution)/shard_map/ppermute | solution.py:285
  297.1 35.3 %collective-permute-start.21 = (f32[256,512]{1,0:T(8,128)}, f32[256,512]{1,0:T(8,128)}, u32[]{:S(2)}, u32[]{:S(2)}) collective-permute-start(f32[256,512]{1,0:T(8,128)} %get-tuple-element.147), channel_id=1, source_target_pairs={{0,16},{8,24},{16,0},{24,8},{32,48},{40,56},{48,32},{56,40},{64,80... | collective-permute-start | bytes 1572872 | tf_op jit(solution)/shard_map/ppermute | solution.py:285
  301.5 22.9 %copy-start.25 = (f32[256,512]{1,0:T(8,128)S(1)}, f32[256,512]{1,0:T(8,128)}, u32[]{:S(2)}) copy-start(f32[256,512]{1,0:T(8,128)} %get-tuple-element.173.refs_1_) | copy-start | bytes 1572868
  306.7 29.9 %collective-permute-start.23 = (f32[256,1024]{1,0:T(8,128)}, f32[256,1024]{1,0:T(8,128)}, u32[]{:S(2)}, u32[]{:S(2)}) collective-permute-start(f32[256,1024]{1,0:T(8,128)} %get-tuple-element.158), channel_id=1, source_target_pairs={{0,64},{8,72},{16,80},{24,88},{32,96},{40,104},{48,112},{56,120},{... | collective-permute-start | bytes 3145736 | tf_op jit(solution)/shard_map/ppermute | solution.py:285
  327.6 34.5 %collective-permute-start.30 = (f32[256,512]{1,0:T(8,128)}, f32[256,512]{1,0:T(8,128)}, u32[]{:S(2)}, u32[]{:S(2)}) collective-permute-start(f32[256,512]{1,0:T(8,128)} %get-tuple-element.176), channel_id=1, source_target_pairs={{0,64},{8,72},{16,80},{24,88},{32,96},{40,104},{48,112},{56,120},{... | collective-permute-start | bytes 1572872 | tf_op jit(solution)/shard_map/ppermute | solution.py:285
  335.8 22.7 %collective-permute-start.25 = (f32[256,512]{1,0:T(8,128)}, f32[256,512]{1,0:T(8,128)S(1)}, u32[]{:S(2)}, u32[]{:S(2)}) collective-permute-start(f32[256,512]{1,0:T(8,128)} %get-tuple-element.164), channel_id=1, source_target_pairs={{0,48},{8,56},{16,32},{24,40},{32,16},{40,24},{48,0},{56,8},{64,11... | collective-permute-start | bytes 1572872 | tf_op jit(solution)/shard_map/ppermute | solution.py:285
  339.3 44.6 %all-to-all-start.2 = ((f32[8,256,128]{2,1,0:T(8,128)}), f32[8,256,128]{2,1,0:T(8,128)}, u32[]{:S(2)}, u32[]{:S(2)}) async-start(f32[8,256,128]{2,1,0:T(8,128)} %total_2.1), calls=%async_computation.2 | async-start | bytes 2097152 | tf_op jit(solution)/shard_map/all_to_all | solution.py:365
  361.8 13.9 %collective-permute-start.26 = (f32[256,512]{1,0:T(8,128)}, f32[256,512]{1,0:T(8,128)S(1)}, u32[]{:S(2)}, u32[]{:S(2)}) collective-permute-start(f32[256,512]{1,0:T(8,128)} %get-tuple-element.166), channel_id=1, source_target_pairs={{0,64},{8,72},{16,80},{24,88},{32,96},{40,104},{48,112},{56,120},{... | collective-permute-start | bytes 1572872 | tf_op jit(solution)/shard_map/ppermute | solution.py:285
  364.6 17.2 %collective-permute-start.31 = (f32[256,256]{1,0:T(8,128)}, f32[256,256]{1,0:T(8,128)S(1)}, u32[]{:S(2)}, u32[]{:S(2)}) collective-permute-start(f32[256,256]{1,0:T(8,128)} %get-tuple-element.178), channel_id=1, source_target_pairs={{0,2},{1,3},{2,0},{3,1},{4,6},{5,7},{6,4},{7,5},{8,10},{9,11},{10,... | collective-permute-start | bytes 786440 | tf_op jit(solution)/shard_map/ppermute | solution.py:285
  377.1 12.1 %collective-permute-start.27 = (f32[256,256]{1,0:T(8,128)}, f32[256,256]{1,0:T(8,128)S(1)}, u32[]{:S(2)}, u32[]{:S(2)}) collective-permute-start(f32[256,256]{1,0:T(8,128)} %get-tuple-element.168), channel_id=1, source_target_pairs={{0,2},{1,3},{2,0},{3,1},{4,6},{5,7},{6,4},{7,5},{8,10},{9,11},{10,... | collective-permute-start | bytes 786440 | tf_op jit(solution)/shard_map/ppermute | solution.py:285
  383.1 9.2 %collective-permute-start.32 = (f32[256,128]{1,0:T(8,128)}, f32[256,128]{1,0:T(8,128)S(1)}, u32[]{:S(2)}, u32[]{:S(2)}) collective-permute-start(f32[256,128]{1,0:T(8,128)} %get-tuple-element.180), channel_id=1, source_target_pairs={{0,1},{1,0},{2,3},{3,2},{4,5},{5,4},{6,7},{7,6},{8,9},{9,8},{10,11... | collective-permute-start | bytes 393224 | tf_op jit(solution)/shard_map/ppermute | solution.py:285
  385.3 16.9 %collective-permute-start.24 = (f32[3,256,128]{2,1,0:T(8,128)S(1)}, f32[3,256,128]{2,1,0:T(8,128)S(1)}, u32[]{:S(2)}, u32[]{:S(2)}) collective-permute-start(f32[3,256,128]{2,1,0:T(8,128)S(1)} %pad_maximum_fusion.1), channel_id=1, source_target_pairs={{0,16},{16,0},{40,56},{56,40},{64,80},{80,64},{104,120},{120,104},... | collective-permute-start | bytes 1179656 | tf_op jit(solution)/shard_map/ppermute | solution.py:285
  390.5 5.2 %collective-permute-start.28 = (f32[256,128]{1,0:T(8,128)}, f32[256,128]{1,0:T(8,128)S(1)}, u32[]{:S(2)}, u32[]{:S(2)}) collective-permute-start(f32[256,128]{1,0:T(8,128)} %get-tuple-element.170), channel_id=1, source_target_pairs={{0,1},{1,0},{2,3},{3,2},{4,5},{5,4},{6,7},{7,6},{8,9},{9,8},{10,11... | collective-permute-start | bytes 393224 | tf_op jit(solution)/shard_map/ppermute | solution.py:285
  396.6 6.9 %collective-permute-start.34 = (f32[256,128]{1,0:T(8,128)S(1)}, f32[256,128]{1,0:T(8,128)S(1)}, u32[]{:S(2)}, u32[]{:S(2)}) collective-permute-start(f32[256,128]{1,0:T(8,128)S(1)} %get-tuple-element.182), channel_id=1, source_target_pairs={{0,20},{1,21},{2,22},{3,23},{4,16},{5,17},{6,18},{7,19},{8,12},{9,... | collective-permute-start | bytes 393224 | tf_op jit(solution)/shard_map/ppermute | solution.py:427
  400.3 7.7 %collective-permute-start.33 = (f32[256,128]{1,0:T(8,128)S(1)}, f32[256,128]{1,0:T(8,128)S(1)}, u32[]{:S(2)}, u32[]{:S(2)}) collective-permute-start(f32[256,128]{1,0:T(8,128)S(1)} %get-tuple-element.181), channel_id=1, source_target_pairs={{0,16},{1,17},{2,18},{3,19},{4,20},{5,21},{6,22},{7,23},{16,0},{17... | collective-permute-start | bytes 393224 | tf_op jit(solution)/shard_map/ppermute | solution.py:426
  (26 other events, 209.1 us)

commit v4 on v3

--- a/solution.py
+++ b/solution.py
@@ -313,11 +313,13 @@
     flag = moves(lax.axis_index("node")).astype(jnp.int32)
     weights = (self_weights, cross_weights)
 
-    wide = [widen(0, 1, *weights)[0]]
-    moved = {0: swap(wide[0], "node", Z1, moves)}
+    wide = {}
+    wide[4, 0] = wide[5, 0] = widen(0, 1, *weights)[0]
+    moved = {}
+    moved[4, 0] = moved[5, 0] = swap(wide[4, 0], "node", Z1, moves)
     pieces = [(0, (0,)), (0, (1,)), (1, (0,)), (1, (1,)), (2, (0,)), (2, (1,)), (3, (0,)), (3, (1,))]
     final = len(pieces)
-    sends, fetches, arrivals = {1: 1, 2: 2, 3: 3, 4: 4, 5: 5, 6: 6, 7: 7}, {0: 1, 2: 2, 4: 3}, {3: 1, 5: 2, 7: 3}
+    sends, fetches, arrivals = {1: 1, 2: 2, 3: 3, 4: 4, 5: 5, 6: 6, 7: 7}, {1: (4, 1), 2: (5, 1), 3: (4, 2), 4: (5, 2), 5: (4, 3), 6: (5, 3)}, {3: (4, 1), 4: (5, 1), 5: (4, 2), 6: (5, 2), 7: (4, 3)}
     fifths, summing = {4: (0, [0, 1]), 6: (1, [2, 3]), 7: (2, [4, 5])}, {5: 0, 7: 1}
 
     own_info = jnp.concatenate([ranks, flag[None]])
@@ -328,13 +330,14 @@
         kept3[turn], sent3[turn] = level3(node, own_info, [first[p] for p in held_parts], *weights)
 
     for part in range(PARTS):
-        start = tie(ranks, sent3[0] if part else wide[0])
+        start = tie(ranks, sent3[0] if part else wide[4, 0])
         k, sent = local_levels(part, PARTS, 1, coefficients, *weights, start)
         first.append((k, swap(sent, "node", CORE)))
         if part == pieces[0][1][-1]:
             third(0)
     later_ranks, later_weights = tie(ranks, sent3[0]), tie(self_weights, sent3[0])
-    wide += [widen(node, 1, later_weights, cross_weights)[0] for node in range(1, count)]
+    for node in range(1, count):
+        wide[4, node], wide[5, node] = widen(node, 2, later_weights, cross_weights)
     other_ranks = swap(later_ranks, "node", Z1, moves)
     held = jnp.where(flag == 1, other_ranks, ranks)
     held_info = jnp.concatenate([held, flag[None]])
@@ -347,7 +350,7 @@
 
     def fourth(turn):
         node = pieces[turn][0]
-        k, s = moved_level(4, node, held_info, [(kept3[turn], r3[turn])], *weights, moved[node])
+        k, s = moved_level(4, node, held_info, [(kept3[turn], r3[turn])], *weights, moved[4, node])
         if 0 and 0 <= turn < final - 1:
             s = tie(s, r4[turn - 0])
         kept4[turn], sent4[turn], r4[turn] = k, s, swap(s, "node", Z1 | Z2)
@@ -356,7 +359,7 @@
         state = [(kept4[t], r4[t]) for t in turns]
         if before:
             state[0] = (tie(state[0][0], *before), state[0][1])
-        k, s = moved_level(5, node, held_info, state, *weights, moved[node])
+        k, s = moved_level(5, node, held_info, state, *weights, moved[5, node])
         return k, swap(s, "node", X0)
 
     def column_sum(node, terms):
@@ -412,7 +415,7 @@
     def spot(bit):
         return jnp.stack([bit, 1 - bit]).astype(jnp.int32)
 
-    quarters, before = [], [early] if False else []
+    quarters, before = [], [early] if True else []
     for k, r in ends:
         if quarters and before:
             k = tie(k, *before)

time: 410 us -> 406 us (level)
  waiting for transfers between devices: 182 us -> 168 us
  starting transfers between devices: 104 us -> 111 us
    ppermute x33 -> x36, waiting for transfers between devices: 176 us -> 165 us  [swap(): return lax.ppermute(value, axis, pairs)]
    ppermute x1, starting transfers between devices: 1.91 us -> 6.18 us  [shards(): away = lax.ppermute(mine, ('node', 'col'), home)]
    ppermute x33 -> x36, starting transfers between devices: 78 us -> 81.4 us  [swap(): return lax.ppermute(value, axis, pairs)]
  transfers between devices with their start and end apart: 38 -> 41, of which waited for: 17 -> 17; matrix products, arithmetic and copies ran while one was open for 2% -> 2% of each run, Pallas kernels for 25% -> 24%
where the time goes in v4:
time: 406 us; the launch traced here: 403 us
  waiting for transfers between devices  168 us (41%)
  Pallas kernels  111 us (27%)
  starting transfers between devices  111 us (27%)
  other arithmetic  9.42 us (2%)
    ppermute x36, waiting for transfers between devices, swap(): return lax.ppermute(value, axis, pairs)  165 us
    ppermute x36, starting transfers between devices, swap(): return lax.ppermute(value, axis, pairs)  81.4 us
    pallas_call x13, Pallas kernels, moved_level(): pl.pallas_call(lambda *refs: moved_kernel(node, count, *refs), grid_spec=...  48.3 us
    pallas_call x8, Pallas kernels, level3(): pl.pallas_call(lambda *refs: level3_kernel(node, count, *refs), grid_spec...  25 us
    all_to_all x3, starting transfers between devices, column_sum(): lax.all_to_all(blocks, 'col', 0, 0, tiled=True)  22.7 us
    pallas_call x2, Pallas kernels, local_levels(): pl.pallas_call(local_kernel, grid_spec=pltpu.PrefetchScalarGridSpec(num_s...  16.3 us
    pallas_call x4, Pallas kernels, widen(): pl.pallas_call(widen_kernel, grid=(1,), in_specs=[mats, mats], out_specs=...  8.25 us
  transfers between devices with their start and end apart: 41, of which 17 were waited for; matrix products, arithmetic and copies ran while one was open for 2% of the time, Pallas kernels for 24%

profile of v4, /device:TPU:2, one launch (start us, length us, event | category | flops | bytes accessed | tf_op | source)
XLA Modules:
  0.0 402.8 jit_solution(3772316919444684804)
XLA Ops:
  2.1 8.1 %local_part0.1 = (f32[4,256,512]{2,1,0:T(8,128)}, f32[4,256,512]{2,1,0:T(8,128)}) custom-call(s32[4]{0:T(128)} %bitcast.ranks, f32[1,4,256,1024]{3,2,1,0:T(8,128)} %state.3, bf16[1,6,4,256,256]{4,3,2,1,0:T(8,128)(2,1)} %refs_3_.35, bf16[1,6,4,256,256]{4,3,2,1,0:T(8,128)(2,1)} %refs_4_.35), custom_call_target="tpu_custom_call" | custom-call | flops 99999997952 | bytes 1000000000 | tf_op jit(solution)/shard_map/local_part0/pallas_call | solution.py:67
  10.2 5.2 %collective-permute-start.7 = (f32[2,2,256,256]{3,2,1,0:T(8,128)}, f32[2,2,256,256]{3,2,1,0:T(8,128)}, u32[]{:S(2)}, u32[]{:S(2)}) collective-permute-start(f32[2,2,256,256]{3,2,1,0:T(8,128)} %widen_0.1), channel_id=1, source_target_pairs={{0,16},{16,0},{40,56},{56,40},{64,80},{80,64},{104,120},{120,104},... | collective-permute-start | bytes 3145736 | tf_op jit(solution)/shard_map/ppermute | solution.py:285
  28.8 3.4 collective-permute-start.6
  32.2 8.2 %local_part1.1 = (f32[4,256,512]{2,1,0:T(8,128)}, f32[4,256,512]{2,1,0:T(8,128)}) custom-call(s32[4]{0:T(128)} %bitcast.ranks, f32[1,4,256,1024]{3,2,1,0:T(8,128)} %state.3, bf16[1,6,4,256,256]{4,3,2,1,0:T(8,128)(2,1)} %refs_3_.35, bf16[1,6,4,256,256]{4,3,2,1,0:T(8,128)(2,1)} %refs_4_.35), custom_call_target="tpu_custom_call" | custom-call | flops 99999997952 | bytes 1000000000 | tf_op jit(solution)/shard_map/local_part1/pallas_call | solution.py:67
  49.7 12.5 %collective-permute-done.6 = s32[4]{0:T(128)} collective-permute-done((s32[4]{0:T(128)}, s32[4]{0:T(128)}, u32[]{:S(2)}, u32[]{:S(2)}) %collective-permute-start.6) | collective-permute-done | bytes 48 | tf_op jit(solution)/shard_map/ppermute | solution.py:285
  63.5 3.2 level3_0.3
  66.8 3.4 level4_0.2
  70.2 4.8 %collective-permute-start.5 = (f32[1,2,256,256]{3,2,1,0:T(8,128)}, f32[1,2,256,256]{3,2,1,0:T(8,128)}, u32[]{:S(2)}, u32[]{:S(2)}) collective-permute-start(f32[1,2,256,256]{3,2,1,0:T(8,128)} %get-tuple-element.121), channel_id=1, source_target_pairs={{0,16},{16,0},{40,56},{56,40},{64,80},{80,64},{104,120},{120,104},... | collective-permute-start | bytes 1572872 | tf_op jit(solution)/shard_map/ppermute | solution.py:285
  78.1 3.2 level3_2.3
  81.3 3.1 level3_1.3
  84.4 10.0 %collective-permute-done.3.refs_2_ = f32[256,512]{1,0:T(8,128)} collective-permute-done((f32[256,512]{1,0:T(8,128)}, f32[256,512]{1,0:T(8,128)}, u32[]{:S(2)}, u32[]{:S(2)}) %collective-permute-start.3) | collective-permute-done | bytes 524320 | tf_op jit(solution)/shard_map/ppermute | solution.py:285
  94.5 3.4 level4_0.3
  97.9 7.1 %collective-permute-start.11 = (f32[256,512]{1,0:T(8,128)}, f32[256,512]{1,0:T(8,128)S(1)}, u32[]{:S(2)}, u32[]{:S(2)}) collective-permute-start(f32[256,512]{1,0:T(8,128)} %get-tuple-element.131), channel_id=1, source_target_pairs={{0,48},{8,56},{16,32},{24,40},{32,16},{40,24},{48,0},{56,8},{64,11... | collective-permute-start | bytes 1572872 | tf_op jit(solution)/shard_map/ppermute | solution.py:285
  105.0 4.8 %collective-permute-start.10 = (f32[1,2,256,256]{3,2,1,0:T(8,128)S(1)}, f32[1,2,256,256]{3,2,1,0:T(8,128)S(1)}, u32[]{:S(2)}, u32[]{:S(2)}) collective-permute-start(f32[1,2,256,256]{3,2,1,0:T(8,128)S(1)} %copy-done.41), channel_id=1, source_target_pairs={{0,16},{16,0},{40,56},{56,40},{64,80},{80,64},{104,120},{120,104},... | collective-permute-start | bytes 1572872 | tf_op jit(solution)/shard_map/ppermute | solution.py:285
  109.8 21.9 %collective-permute-done.5.refs_5_ = f32[1,2,256,256]{3,2,1,0:T(8,128)} collective-permute-done((f32[1,2,256,256]{3,2,1,0:T(8,128)}, f32[1,2,256,256]{3,2,1,0:T(8,128)}, u32[]{:S(2)}, u32[]{:S(2)}) %collective-permute-start.5) | collective-permute-done | bytes 524320 | tf_op jit(solution)/shard_map/ppermute | solution.py:285
  131.7 16.4 %collective-permute-done.4.refs_2_ = f32[256,512]{1,0:T(8,128)S(1)} collective-permute-done((f32[256,512]{1,0:T(8,128)S(1)}, f32[256,512]{1,0:T(8,128)S(1)}, u32[]{:S(2)}, u32[]{:S(2)}) %collective-permute-start.4) | collective-permute-done | bytes 524320 | tf_op jit(solution)/shard_map/ppermute | solution.py:285
  148.2 3.3 level4_1.2
  151.5 4.8 %collective-permute-start.13 = (f32[1,2,256,256]{3,2,1,0:T(8,128)}, f32[1,2,256,256]{3,2,1,0:T(8,128)}, u32[]{:S(2)}, u32[]{:S(2)}) collective-permute-start(f32[1,2,256,256]{3,2,1,0:T(8,128)} %get-tuple-element.135), channel_id=1, source_target_pairs={{0,16},{16,0},{40,56},{56,40},{64,80},{80,64},{104,120},{120,104},... | collective-permute-start | bytes 1572872 | tf_op jit(solution)/shard_map/ppermute | solution.py:285
  156.3 13.9 %collective-permute-done.10.refs_7_ = f32[1,2,256,256]{3,2,1,0:T(8,128)S(1)} collective-permute-done((f32[1,2,256,256]{3,2,1,0:T(8,128)S(1)}, f32[1,2,256,256]{3,2,1,0:T(8,128)S(1)}, u32[]{:S(2)}, u32[]{:S(2)}) %collective-permute-start.10) | collective-permute-done | bytes 524320 | tf_op jit(solution)/shard_map/ppermute | solution.py:285
  171.0 13.6 %collective-permute-done.9.refs_2_ = f32[256,512]{1,0:T(8,128)S(1)} collective-permute-done((f32[256,512]{1,0:T(8,128)S(1)}, f32[256,512]{1,0:T(8,128)S(1)}, u32[]{:S(2)}, u32[]{:S(2)}) %collective-permute-start.9) | collective-permute-done | bytes 524320 | tf_op jit(solution)/shard_map/ppermute | solution.py:285
  184.6 4.6 %level5_0.1 = (f32[256,1024]{1,0:T(8,128)}, f32[256,1024]{1,0:T(8,128)}) custom-call(s32[5]{0:T(128)S(1)} %pad_add_fusion.1.refs_0_.refs_1_, f32[256,512]{1,0:T(8,128)S(1)} %copy-done.20, f32[256,512]{1,0:T(8,128)} %collective-permute-done.8.refs_2_, f32[256,512]{1,0:T(8,128)S(1)} %copy-done.21, f32[256,512]{1,0:T(8,128)S(1)} %collective-permute-done.11.refs_4_, ...), custom_call_target="tpu_custom_call" | custom-call | flops 99999997952 | bytes 1000000000 | tf_op jit(solution)/shard_map/level5_0/pallas_call | solution.py:198
  189.2 3.3 level4_1.3
  192.6 4.8 %collective-permute-start.17 = (f32[1,2,256,256]{3,2,1,0:T(8,128)}, f32[1,2,256,256]{3,2,1,0:T(8,128)}, u32[]{:S(2)}, u32[]{:S(2)}) collective-permute-start(f32[1,2,256,256]{3,2,1,0:T(8,128)} %get-tuple-element.148), channel_id=1, source_target_pairs={{0,16},{16,0},{40,56},{56,40},{64,80},{80,64},{104,120},{120,104},... | collective-permute-start | bytes 1572872 | tf_op jit(solution)/shard_map/ppermute | solution.py:285
  197.4 5.5 %collective-permute-done.12.refs_2_ = f32[256,512]{1,0:T(8,128)} collective-permute-done((f32[256,512]{1,0:T(8,128)}, f32[256,512]{1,0:T(8,128)}, u32[]{:S(2)}, u32[]{:S(2)}) %collective-permute-start.12) | collective-permute-done | bytes 524320 | tf_op jit(solution)/shard_map/ppermute | solution.py:285
  206.0 10.3 %all-to-all-start = ((f32[8,256,128]{2,1,0:T(8,128)}), f32[8,256,128]{2,1,0:T(8,128)}, u32[]{:S(2)}, u32[]{:S(2)}) async-start(f32[8,256,128]{2,1,0:T(8,128)} %total_0.1), calls=%async_computation | async-start | bytes 2097152 | tf_op jit(solution)/shard_map/all_to_all | solution.py:368
  219.4 3.4 level4_2.2
  224.7 10.6 %collective-permute-done.18.refs_4_ = f32[256,512]{1,0:T(8,128)} collective-permute-done((f32[256,512]{1,0:T(8,128)}, f32[256,512]{1,0:T(8,128)}, u32[]{:S(2)}, u32[]{:S(2)}) %collective-permute-start.18) | collective-permute-done | bytes 524320 | tf_op jit(solution)/shard_map/ppermute | solution.py:285
  235.2 12.4 %collective-permute-done.16.refs_2_ = f32[256,512]{1,0:T(8,128)S(1)} collective-permute-done((f32[256,512]{1,0:T(8,128)S(1)}, f32[256,512]{1,0:T(8,128)S(1)}, u32[]{:S(2)}, u32[]{:S(2)}) %collective-permute-start.16) | collective-permute-done | bytes 524320 | tf_op jit(solution)/shard_map/ppermute | solution.py:285
  247.7 3.4 collective-permute-start.19
  251.1 5.0 %level5_1.1 = (f32[256,1024]{1,0:T(8,128)}, f32[256,1024]{1,0:T(8,128)}) custom-call(s32[5]{0:T(128)S(1)} %copy-done.3, f32[256,512]{1,0:T(8,128)S(1)} %copy-done.22, f32[256,512]{1,0:T(8,128)} %collective-permute-done.14.refs_2_, f32[256,512]{1,0:T(8,128)S(1)} %copy-done.24, f32[256,512]{1,0:T(8,128)} %collective-permute-done.18.refs_4_, ...), custom_call_target="tpu_custom_call" | custom-call | flops 99999997952 | bytes 1000000000 | tf_op jit(solution)/shard_map/level5_1/pallas_call | solution.py:198
  256.2 3.3 level4_2.3
  261.5 4.4 %collective-permute-start.28 = (f32[1,2,256,256]{3,2,1,0:T(8,128)}, f32[1,2,256,256]{3,2,1,0:T(8,128)}, u32[]{:S(2)}, u32[]{:S(2)}) collective-permute-start(f32[1,2,256,256]{3,2,1,0:T(8,128)} %get-tuple-element.187), channel_id=1, source_target_pairs={{0,16},{16,0},{40,56},{56,40},{64,80},{80,64},{104,120},{120,104},... | collective-permute-start | bytes 1572872 | tf_op jit(solution)/shard_map/ppermute | solution.py:285
  265.9 6.3 %collective-permute-done.19.refs_2_ = f32[256,512]{1,0:T(8,128)} collective-permute-done((f32[256,512]{1,0:T(8,128)}, f32[256,512]{1,0:T(8,128)}, u32[]{:S(2)}, u32[]{:S(2)}) %collective-permute-start.19) | collective-permute-done | bytes 524320 | tf_op jit(solution)/shard_map/ppermute | solution.py:285
  274.1 4.4 %all-to-all-start.1 = ((f32[8,256,128]{2,1,0:T(8,128)}), f32[8,256,128]{2,1,0:T(8,128)}, u32[]{:S(2)}, u32[]{:S(2)}) async-start(f32[8,256,128]{2,1,0:T(8,128)} %total_1.1), calls=%async_computation.1 | async-start | bytes 2097152 | tf_op jit(solution)/shard_map/all_to_all | solution.py:368
  278.5 3.4 level4_3.3
  281.9 8.4 %collective-permute-start.32 = (f32[256,512]{1,0:T(8,128)}, f32[256,512]{1,0:T(8,128)S(1)}, u32[]{:S(2)}, u32[]{:S(2)}) collective-permute-start(f32[256,512]{1,0:T(8,128)} %get-tuple-element.198), channel_id=1, source_target_pairs={{0,48},{8,56},{16,32},{24,40},{32,16},{40,24},{48,0},{56,8},{64,11... | collective-permute-start | bytes 1572872 | tf_op jit(solution)/shard_map/ppermute | solution.py:285
  290.2 4.0 %collective-permute-start.23 = (f32[256,512]{1,0:T(8,128)}, f32[256,512]{1,0:T(8,128)}, u32[]{:S(2)}, u32[]{:S(2)}) collective-permute-start(f32[256,512]{1,0:T(8,128)} %get-tuple-element.168), channel_id=1, source_target_pairs={{0,16},{8,24},{16,0},{24,8},{32,48},{40,56},{48,32},{56,40},{64,80... | collective-permute-start | bytes 1572872 | tf_op jit(solution)/shard_map/ppermute | solution.py:285
  294.3 5.2 %level5_2.1 = (f32[256,1024]{1,0:T(8,128)}, f32[256,1024]{1,0:T(8,128)}) custom-call(s32[5]{0:T(128)S(1)} %copy-done.3, f32[256,512]{1,0:T(8,128)S(1)} %copy-done.23, f32[256,512]{1,0:T(8,128)} %collective-permute-done.21.refs_2_, f32[256,512]{1,0:T(8,128)S(1)} %copy-done.25, f32[256,512]{1,0:T(8,128)} %collective-permute-done.24.refs_4_, ...), custom_call_target="tpu_custom_call" | custom-call | flops 99999997952 | bytes 1000000000 | tf_op jit(solution)/shard_map/level5_2/pallas_call | solution.py:198
  299.5 22.3 %collective-permute-done.32.refs_2_ = f32[256,512]{1,0:T(8,128)S(1)} collective-permute-done((f32[256,512]{1,0:T(8,128)}, f32[256,512]{1,0:T(8,128)S(1)}, u32[]{:S(2)}, u32[]{:S(2)}) %collective-permute-start.32) | collective-permute-done | bytes 524320 | tf_op jit(solution)/shard_map/ppermute | solution.py:285
  321.8 3.3 level5_3.3
  327.5 3.4 level4_3.2
  333.6 8.0 %all-to-all-start.2 = ((f32[8,256,128]{2,1,0:T(8,128)}), f32[8,256,128]{2,1,0:T(8,128)}, u32[]{:S(2)}, u32[]{:S(2)}) async-start(f32[8,256,128]{2,1,0:T(8,128)} %total_2.1), calls=%async_computation.2 | async-start | bytes 2097152 | tf_op jit(solution)/shard_map/all_to_all | solution.py:368
  341.6 11.6 %collective-permute-done.27.refs_2_ = f32[256,512]{1,0:T(8,128)S(1)} collective-permute-done((f32[256,512]{1,0:T(8,128)}, f32[256,512]{1,0:T(8,128)S(1)}, u32[]{:S(2)}, u32[]{:S(2)}) %collective-permute-start.27) | collective-permute-done | bytes 524320 | tf_op jit(solution)/shard_map/ppermute | solution.py:285
  353.2 3.3 level5_3.2
  365.7 3.4 collective-permute-done.29.refs_3_.refs_5_
  376.3 8.5 %collective-permute-start.26 = (f32[3,256,128]{2,1,0:T(8,128)S(1)}, f32[3,256,128]{2,1,0:T(8,128)S(1)}, u32[]{:S(2)}, u32[]{:S(2)}) collective-permute-start(f32[3,256,128]{2,1,0:T(8,128)S(1)} %copy-done.38), channel_id=1, source_target_pairs={{0,16},{16,0},{40,56},{56,40},{64,80},{80,64},{104,120},{120,104},... | collective-permute-start | bytes 1179656 | tf_op jit(solution)/shard_map/ppermute | solution.py:285
  387.8 3.5 collective-permute-done.31
  392.8 6.2 %collective-permute-start.36 = (f32[256,128]{1,0:T(8,128)S(1)}, f32[256,128]{1,0:T(8,128)S(1)}, u32[]{:S(2)}, u32[]{:S(2)}) collective-permute-start(f32[256,128]{1,0:T(8,128)S(1)} %get-tuple-element.205), channel_id=1, source_target_pairs={{0,16},{1,17},{2,18},{3,19},{4,20},{5,21},{6,22},{7,23},{16,0},{17... | collective-permute-start | bytes 393224 | tf_op jit(solution)/shard_map/ppermute | solution.py:429
  (169 shorter events, 71.7 us)
Async XLA Ops:
  10.2 6.1 %collective-permute-start = (f32[4,256,512]{2,1,0:T(8,128)}, f32[4,256,512]{2,1,0:T(8,128)S(1)}, u32[]{:S(2)}, u32[]{:S(2)}) collective-permute-start(f32[4,256,512]{2,1,0:T(8,128)} %get-tuple-element.107), channel_id=1, source_target_pairs={{0,8},{8,0},{16,24},{24,16},{32,40},{40,32},{48,56},{56,48},{64,72... | collective-permute-start | bytes 6291464 | tf_op jit(solution)/shard_map/ppermute | solution.py:285
  10.2 56.5 %collective-permute-start.7 = (f32[2,2,256,256]{3,2,1,0:T(8,128)}, f32[2,2,256,256]{3,2,1,0:T(8,128)}, u32[]{:S(2)}, u32[]{:S(2)}) collective-permute-start(f32[2,2,256,256]{3,2,1,0:T(8,128)} %widen_0.1), channel_id=1, source_target_pairs={{0,16},{16,0},{40,56},{56,40},{64,80},{80,64},{104,120},{120,104},... | collective-permute-start | bytes 3145736 | tf_op jit(solution)/shard_map/ppermute | solution.py:285
  21.0 45.7 %collective-permute-start.1 = (f32[256,512]{1,0:T(8,128)}, f32[256,512]{1,0:T(8,128)}, u32[]{:S(2)}, u32[]{:S(2)}) collective-permute-start(f32[256,512]{1,0:T(8,128)} %get-tuple-element.108), channel_id=1, source_target_pairs={{0,16},{8,24},{16,0},{24,8},{32,48},{40,56},{48,32},{56,40},{64,80... | collective-permute-start | bytes 1572872 | tf_op jit(solution)/shard_map/ppermute | solution.py:285
  28.8 33.4 %collective-permute-start.6 = (s32[4]{0:T(128)}, s32[4]{0:T(128)}, u32[]{:S(2)}, u32[]{:S(2)}) collective-permute-start(s32[4]{0:T(128)} %bitcast.ranks), channel_id=1, source_target_pairs={{0,16},{16,0},{40,56},{56,40},{64,80},{80,64},{104,120},{120,104},... | collective-permute-start | bytes 56 | tf_op jit(solution)/shard_map/ppermute | solution.py:285
  40.4 22.6 %collective-permute-start.2 = (f32[4,256,512]{2,1,0:T(8,128)}, f32[4,256,512]{2,1,0:T(8,128)}, u32[]{:S(2)}, u32[]{:S(2)}) collective-permute-start(f32[4,256,512]{2,1,0:T(8,128)} %get-tuple-element.111), channel_id=1, source_target_pairs={{0,8},{8,0},{16,24},{24,16},{32,40},{40,32},{48,56},{56,48},{64,72... | collective-permute-start | bytes 6291464 | tf_op jit(solution)/shard_map/ppermute | solution.py:285
  62.9 141.3 %copy-start.2 = (s32[5]{0:T(128)}, s32[5]{0:T(128)S(1)}, u32[]{:S(2)}) copy-start(s32[5]{0:T(128)S(1)} %pad_add_fusion.1.refs_0_.refs_1_) | copy-start | bytes 64
  70.2 39.6 %collective-permute-start.8 = (f32[256,512]{1,0:T(8,128)}, f32[256,512]{1,0:T(8,128)}, u32[]{:S(2)}, u32[]{:S(2)}) collective-permute-start(f32[256,512]{1,0:T(8,128)} %get-tuple-element.124), channel_id=1, source_target_pairs={{0,48},{8,56},{16,32},{24,40},{32,16},{40,24},{48,0},{56,8},{64,11... | collective-permute-start | bytes 1572872 | tf_op jit(solution)/shard_map/ppermute | solution.py:285
  70.2 24.3 %collective-permute-start.3 = (f32[256,512]{1,0:T(8,128)}, f32[256,512]{1,0:T(8,128)}, u32[]{:S(2)}, u32[]{:S(2)}) collective-permute-start(f32[256,512]{1,0:T(8,128)} %get-tuple-element.115), channel_id=1, source_target_pairs={{0,16},{8,24},{16,0},{24,8},{32,48},{40,56},{48,32},{56,40},{64,80... | collective-permute-start | bytes 1572872 | tf_op jit(solution)/shard_map/ppermute | solution.py:285
  70.2 61.5 %collective-permute-start.5 = (f32[1,2,256,256]{3,2,1,0:T(8,128)}, f32[1,2,256,256]{3,2,1,0:T(8,128)}, u32[]{:S(2)}, u32[]{:S(2)}) collective-permute-start(f32[1,2,256,256]{3,2,1,0:T(8,128)} %get-tuple-element.121), channel_id=1, source_target_pairs={{0,16},{16,0},{40,56},{56,40},{64,80},{80,64},{104,120},{120,104},... | collective-permute-start | bytes 1572872 | tf_op jit(solution)/shard_map/ppermute | solution.py:285
  94.4 53.7 %collective-permute-start.4 = (f32[256,512]{1,0:T(8,128)S(1)}, f32[256,512]{1,0:T(8,128)S(1)}, u32[]{:S(2)}, u32[]{:S(2)}) collective-permute-start(f32[256,512]{1,0:T(8,128)S(1)} %copy-done.42), channel_id=1, source_target_pairs={{0,16},{8,24},{16,0},{24,8},{32,48},{40,56},{48,32},{56,40},{64,80... | collective-permute-start | bytes 1572872 | tf_op jit(solution)/shard_map/ppermute | solution.py:285
  94.5 53.7 %copy-start.43 = (f32[256,512]{1,0:T(8,128)S(1)}, f32[256,512]{1,0:T(8,128)}, u32[]{:S(2)}) copy-start(f32[256,512]{1,0:T(8,128)} %get-tuple-element.125) | copy-start | bytes 1572868
  94.5 53.7 %copy-start.16 = (f32[256,512]{1,0:T(8,128)S(1)}, f32[256,512]{1,0:T(8,128)}, u32[]{:S(2)}) copy-start(f32[256,512]{1,0:T(8,128)} %get-tuple-element.136.refs_1_) | copy-start | bytes 1572868
  97.9 58.4 %collective-permute-start.11 = (f32[256,512]{1,0:T(8,128)}, f32[256,512]{1,0:T(8,128)S(1)}, u32[]{:S(2)}, u32[]{:S(2)}) collective-permute-start(f32[256,512]{1,0:T(8,128)} %get-tuple-element.131), channel_id=1, source_target_pairs={{0,48},{8,56},{16,32},{24,40},{32,16},{40,24},{48,0},{56,8},{64,11... | collective-permute-start | bytes 1572872 | tf_op jit(solution)/shard_map/ppermute | solution.py:285
  105.0 65.2 %collective-permute-start.10 = (f32[1,2,256,256]{3,2,1,0:T(8,128)S(1)}, f32[1,2,256,256]{3,2,1,0:T(8,128)S(1)}, u32[]{:S(2)}, u32[]{:S(2)}) collective-permute-start(f32[1,2,256,256]{3,2,1,0:T(8,128)S(1)} %copy-done.41), channel_id=1, source_target_pairs={{0,16},{16,0},{40,56},{56,40},{64,80},{80,64},{104,120},{120,104},... | collective-permute-start | bytes 1572872 | tf_op jit(solution)/shard_map/ppermute | solution.py:285
  148.2 36.4 %collective-permute-start.9 = (f32[256,512]{1,0:T(8,128)S(1)}, f32[256,512]{1,0:T(8,128)S(1)}, u32[]{:S(2)}, u32[]{:S(2)}) collective-permute-start(f32[256,512]{1,0:T(8,128)S(1)} %copy-done.43), channel_id=1, source_target_pairs={{0,16},{8,24},{16,0},{24,8},{32,48},{40,56},{48,32},{56,40},{64,80... | collective-permute-start | bytes 1572872 | tf_op jit(solution)/shard_map/ppermute | solution.py:285
  148.2 36.4 %copy-start.20 = (f32[256,512]{1,0:T(8,128)S(1)}, f32[256,512]{1,0:T(8,128)}, u32[]{:S(2)}) copy-start(f32[256,512]{1,0:T(8,128)} %get-tuple-element.140.refs_1_) | copy-start | bytes 1572868
  148.2 36.4 %copy-start.21 = (f32[256,512]{1,0:T(8,128)S(1)}, f32[256,512]{1,0:T(8,128)}, u32[]{:S(2)}) copy-start(f32[256,512]{1,0:T(8,128)} %get-tuple-element.142.refs_3_) | copy-start | bytes 1572868
  151.5 41.1 %collective-permute-start.14 = (f32[256,512]{1,0:T(8,128)}, f32[256,512]{1,0:T(8,128)}, u32[]{:S(2)}, u32[]{:S(2)}) collective-permute-start(f32[256,512]{1,0:T(8,128)} %get-tuple-element.139), channel_id=1, source_target_pairs={{0,48},{8,56},{16,32},{24,40},{32,16},{40,24},{48,0},{56,8},{64,11... | collective-permute-start | bytes 1572872 | tf_op jit(solution)/shard_map/ppermute | solution.py:285
  151.5 45.9 %collective-permute-start.13 = (f32[1,2,256,256]{3,2,1,0:T(8,128)}, f32[1,2,256,256]{3,2,1,0:T(8,128)}, u32[]{:S(2)}, u32[]{:S(2)}) collective-permute-start(f32[1,2,256,256]{3,2,1,0:T(8,128)} %get-tuple-element.135), channel_id=1, source_target_pairs={{0,16},{16,0},{40,56},{56,40},{64,80},{80,64},{104,120},{120,104},... | collective-permute-start | bytes 1572872 | tf_op jit(solution)/shard_map/ppermute | solution.py:285
  184.5 18.3 %collective-permute-start.12 = (f32[256,512]{1,0:T(8,128)}, f32[256,512]{1,0:T(8,128)}, u32[]{:S(2)}, u32[]{:S(2)}) collective-permute-start(f32[256,512]{1,0:T(8,128)} %get-tuple-element.132), channel_id=1, source_target_pairs={{0,16},{8,24},{16,0},{24,8},{32,48},{40,56},{48,32},{56,40},{64,80... | collective-permute-start | bytes 1572872 | tf_op jit(solution)/shard_map/ppermute | solution.py:285
  189.2 15.0 %collective-permute-start.15 = (f32[256,1024]{1,0:T(8,128)}, f32[256,1024]{1,0:T(8,128)S(1)}, u32[]{:S(2)}, u32[]{:S(2)}) collective-permute-start(f32[256,1024]{1,0:T(8,128)} %get-tuple-element.144), channel_id=1, source_target_pairs={{0,64},{8,72},{16,80},{24,88},{32,96},{40,104},{48,112},{56,120},{... | collective-permute-start | bytes 3145736 | tf_op jit(solution)/shard_map/ppermute | solution.py:285
  192.5 42.7 %collective-permute-start.18 = (f32[256,512]{1,0:T(8,128)}, f32[256,512]{1,0:T(8,128)}, u32[]{:S(2)}, u32[]{:S(2)}) collective-permute-start(f32[256,512]{1,0:T(8,128)} %get-tuple-element.151), channel_id=1, source_target_pairs={{0,48},{8,56},{16,32},{24,40},{32,16},{40,24},{48,0},{56,8},{64,11... | collective-permute-start | bytes 1572872 | tf_op jit(solution)/shard_map/ppermute | solution.py:285
  192.6 42.7 %collective-permute-start.17 = (f32[1,2,256,256]{3,2,1,0:T(8,128)}, f32[1,2,256,256]{3,2,1,0:T(8,128)}, u32[]{:S(2)}, u32[]{:S(2)}) collective-permute-start(f32[1,2,256,256]{3,2,1,0:T(8,128)} %get-tuple-element.148), channel_id=1, source_target_pairs={{0,16},{16,0},{40,56},{56,40},{64,80},{80,64},{104,120},{120,104},... | collective-permute-start | bytes 1572872 | tf_op jit(solution)/shard_map/ppermute | solution.py:285
  206.0 53.5 %all-to-all-start = ((f32[8,256,128]{2,1,0:T(8,128)}), f32[8,256,128]{2,1,0:T(8,128)}, u32[]{:S(2)}, u32[]{:S(2)}) async-start(f32[8,256,128]{2,1,0:T(8,128)} %total_0.1), calls=%async_computation | async-start | bytes 2097152 | tf_op jit(solution)/shard_map/all_to_all | solution.py:368
  216.3 31.3 %collective-permute-start.16 = (f32[256,512]{1,0:T(8,128)S(1)}, f32[256,512]{1,0:T(8,128)S(1)}, u32[]{:S(2)}, u32[]{:S(2)}) collective-permute-start(f32[256,512]{1,0:T(8,128)S(1)} %copy-done.40), channel_id=1, source_target_pairs={{0,16},{8,24},{16,0},{24,8},{32,48},{40,56},{48,32},{56,40},{64,80... | collective-permute-start | bytes 1572872 | tf_op jit(solution)/shard_map/ppermute | solution.py:285
  219.3 31.8 %copy-start.1 = (f32[1,2,256,256]{3,2,1,0:T(8,128)S(1)}, f32[1,2,256,256]{3,2,1,0:T(8,128)}, u32[]{:S(2)}) copy-start(f32[1,2,256,256]{3,2,1,0:T(8,128)} %copy-done) | copy-start | bytes 1572868
  219.3 31.8 %copy-start.22 = (f32[256,512]{1,0:T(8,128)S(1)}, f32[256,512]{1,0:T(8,128)}, u32[]{:S(2)}) copy-start(f32[256,512]{1,0:T(8,128)} %get-tuple-element.161.refs_1_) | copy-start | bytes 1572868
  222.7 38.7 %collective-permute-start.21 = (f32[256,512]{1,0:T(8,128)}, f32[256,512]{1,0:T(8,128)}, u32[]{:S(2)}, u32[]{:S(2)}) collective-permute-start(f32[256,512]{1,0:T(8,128)} %get-tuple-element.158), channel_id=1, source_target_pairs={{0,48},{8,56},{16,32},{24,40},{32,16},{40,24},{48,0},{56,8},{64,11... | collective-permute-start | bytes 1572872 | tf_op jit(solution)/shard_map/ppermute | solution.py:285
  222.7 43.2 %collective-permute-start.20 = (f32[1,2,256,256]{3,2,1,0:T(8,128)}, f32[1,2,256,256]{3,2,1,0:T(8,128)}, u32[]{:S(2)}, u32[]{:S(2)}) collective-permute-start(f32[1,2,256,256]{3,2,1,0:T(8,128)} %get-tuple-element.154), channel_id=1, source_target_pairs={{0,16},{16,0},{40,56},{56,40},{64,80},{80,64},{104,120},{120,104},... | collective-permute-start | bytes 1572872 | tf_op jit(solution)/shard_map/ppermute | solution.py:285
  247.7 24.6 %collective-permute-start.19 = (f32[256,512]{1,0:T(8,128)}, f32[256,512]{1,0:T(8,128)}, u32[]{:S(2)}, u32[]{:S(2)}) collective-permute-start(f32[256,512]{1,0:T(8,128)} %get-tuple-element.152), channel_id=1, source_target_pairs={{0,16},{8,24},{16,0},{24,8},{32,48},{40,56},{48,32},{56,40},{64,80... | collective-permute-start | bytes 1572872 | tf_op jit(solution)/shard_map/ppermute | solution.py:285
  256.1 16.1 %collective-permute-start.22 = (f32[256,1024]{1,0:T(8,128)}, f32[256,1024]{1,0:T(8,128)S(1)}, u32[]{:S(2)}, u32[]{:S(2)}) collective-permute-start(f32[256,1024]{1,0:T(8,128)} %get-tuple-element.166), channel_id=1, source_target_pairs={{0,64},{8,72},{16,80},{24,88},{32,96},{40,104},{48,112},{56,120},{... | collective-permute-start | bytes 3145736 | tf_op jit(solution)/shard_map/ppermute | solution.py:285
  259.5 34.8 %collective-permute-start.24 = (f32[256,512]{1,0:T(8,128)}, f32[256,512]{1,0:T(8,128)}, u32[]{:S(2)}, u32[]{:S(2)}) collective-permute-start(f32[256,512]{1,0:T(8,128)} %get-tuple-element.177), channel_id=1, source_target_pairs={{0,48},{8,56},{16,32},{24,40},{32,16},{40,24},{48,0},{56,8},{64,11... | collective-permute-start | bytes 1572872 | tf_op jit(solution)/shard_map/ppermute | solution.py:285
  261.5 38.0 %collective-permute-start.28 = (f32[1,2,256,256]{3,2,1,0:T(8,128)}, f32[1,2,256,256]{3,2,1,0:T(8,128)}, u32[]{:S(2)}, u32[]{:S(2)}) collective-permute-start(f32[1,2,256,256]{3,2,1,0:T(8,128)} %get-tuple-element.187), channel_id=1, source_target_pairs={{0,16},{16,0},{40,56},{56,40},{64,80},{80,64},{104,120},{120,104},... | collective-permute-start | bytes 1572872 | tf_op jit(solution)/shard_map/ppermute | solution.py:285
  274.1 51.4 %all-to-all-start.1 = ((f32[8,256,128]{2,1,0:T(8,128)}), f32[8,256,128]{2,1,0:T(8,128)}, u32[]{:S(2)}, u32[]{:S(2)}) async-start(f32[8,256,128]{2,1,0:T(8,128)} %total_1.1), calls=%async_computation.1 | async-start | bytes 2097152 | tf_op jit(solution)/shard_map/all_to_all | solution.py:368
  281.9 39.9 %collective-permute-start.32 = (f32[256,512]{1,0:T(8,128)}, f32[256,512]{1,0:T(8,128)S(1)}, u32[]{:S(2)}, u32[]{:S(2)}) collective-permute-start(f32[256,512]{1,0:T(8,128)} %get-tuple-element.198), channel_id=1, source_target_pairs={{0,48},{8,56},{16,32},{24,40},{32,16},{40,24},{48,0},{56,8},{64,11... | collective-permute-start | bytes 1572872 | tf_op jit(solution)/shard_map/ppermute | solution.py:285
  290.2 37.2 %collective-permute-start.23 = (f32[256,512]{1,0:T(8,128)}, f32[256,512]{1,0:T(8,128)}, u32[]{:S(2)}, u32[]{:S(2)}) collective-permute-start(f32[256,512]{1,0:T(8,128)} %get-tuple-element.168), channel_id=1, source_target_pairs={{0,16},{8,24},{16,0},{24,8},{32,48},{40,56},{48,32},{56,40},{64,80... | collective-permute-start | bytes 1572872 | tf_op jit(solution)/shard_map/ppermute | solution.py:285
  299.5 31.3 %collective-permute-start.25 = (f32[256,1024]{1,0:T(8,128)}, f32[256,1024]{1,0:T(8,128)}, u32[]{:S(2)}, u32[]{:S(2)}) collective-permute-start(f32[256,1024]{1,0:T(8,128)} %get-tuple-element.180), channel_id=1, source_target_pairs={{0,64},{8,72},{16,80},{24,88},{32,96},{40,104},{48,112},{56,120},{... | collective-permute-start | bytes 3145736 | tf_op jit(solution)/shard_map/ppermute | solution.py:285
  325.2 33.1 %collective-permute-start.33 = (f32[256,512]{1,0:T(8,128)}, f32[256,512]{1,0:T(8,128)}, u32[]{:S(2)}, u32[]{:S(2)}) collective-permute-start(f32[256,512]{1,0:T(8,128)} %get-tuple-element.200), channel_id=1, source_target_pairs={{0,64},{8,72},{16,80},{24,88},{32,96},{40,104},{48,112},{56,120},{... | collective-permute-start | bytes 1572872 | tf_op jit(solution)/shard_map/ppermute | solution.py:285
  330.8 22.4 %collective-permute-start.27 = (f32[256,512]{1,0:T(8,128)}, f32[256,512]{1,0:T(8,128)S(1)}, u32[]{:S(2)}, u32[]{:S(2)}) collective-permute-start(f32[256,512]{1,0:T(8,128)} %get-tuple-element.186), channel_id=1, source_target_pairs={{0,48},{8,56},{16,32},{24,40},{32,16},{40,24},{48,0},{56,8},{64,11... | collective-permute-start | bytes 1572872 | tf_op jit(solution)/shard_map/ppermute | solution.py:285
  333.6 30.1 %all-to-all-start.2 = ((f32[8,256,128]{2,1,0:T(8,128)}), f32[8,256,128]{2,1,0:T(8,128)}, u32[]{:S(2)}, u32[]{:S(2)}) async-start(f32[8,256,128]{2,1,0:T(8,128)} %total_2.1), calls=%async_computation.2 | async-start | bytes 2097152 | tf_op jit(solution)/shard_map/all_to_all | solution.py:368
  356.5 12.6 %collective-permute-start.29 = (f32[256,512]{1,0:T(8,128)}, f32[256,512]{1,0:T(8,128)S(1)}, u32[]{:S(2)}, u32[]{:S(2)}) collective-permute-start(f32[256,512]{1,0:T(8,128)} %get-tuple-element.190), channel_id=1, source_target_pairs={{0,64},{8,72},{16,80},{24,88},{32,96},{40,104},{48,112},{56,120},{... | collective-permute-start | bytes 1572872 | tf_op jit(solution)/shard_map/ppermute | solution.py:285
  360.7 12.6 %collective-permute-start.34 = (f32[256,256]{1,0:T(8,128)}, f32[256,256]{1,0:T(8,128)S(1)}, u32[]{:S(2)}, u32[]{:S(2)}) collective-permute-start(f32[256,256]{1,0:T(8,128)} %get-tuple-element.202), channel_id=1, source_target_pairs={{0,2},{1,3},{2,0},{3,1},{4,6},{5,7},{6,4},{7,5},{8,10},{9,11},{10,... | collective-permute-start | bytes 786440 | tf_op jit(solution)/shard_map/ppermute | solution.py:285
  370.5 14.3 %collective-permute-start.30 = (f32[256,256]{1,0:T(8,128)}, f32[256,256]{1,0:T(8,128)S(1)}, u32[]{:S(2)}, u32[]{:S(2)}) collective-permute-start(f32[256,256]{1,0:T(8,128)} %get-tuple-element.192), channel_id=1, source_target_pairs={{0,2},{1,3},{2,0},{3,1},{4,6},{5,7},{6,4},{7,5},{8,10},{9,11},{10,... | collective-permute-start | bytes 786440 | tf_op jit(solution)/shard_map/ppermute | solution.py:285
  374.6 13.3 %collective-permute-start.35 = (f32[256,128]{1,0:T(8,128)}, f32[256,128]{1,0:T(8,128)S(1)}, u32[]{:S(2)}, u32[]{:S(2)}) collective-permute-start(f32[256,128]{1,0:T(8,128)} %get-tuple-element.204), channel_id=1, source_target_pairs={{0,1},{1,0},{2,3},{3,2},{4,5},{5,4},{6,7},{7,6},{8,9},{9,8},{10,11... | collective-permute-start | bytes 393224 | tf_op jit(solution)/shard_map/ppermute | solution.py:285
  376.3 22.6 %collective-permute-start.26 = (f32[3,256,128]{2,1,0:T(8,128)S(1)}, f32[3,256,128]{2,1,0:T(8,128)S(1)}, u32[]{:S(2)}, u32[]{:S(2)}) collective-permute-start(f32[3,256,128]{2,1,0:T(8,128)S(1)} %copy-done.38), channel_id=1, source_target_pairs={{0,16},{16,0},{40,56},{56,40},{64,80},{80,64},{104,120},{120,104},... | collective-permute-start | bytes 1179656 | tf_op jit(solution)/shard_map/ppermute | solution.py:285
  386.1 5.2 %collective-permute-start.31 = (f32[256,128]{1,0:T(8,128)}, f32[256,128]{1,0:T(8,128)S(1)}, u32[]{:S(2)}, u32[]{:S(2)}) collective-permute-start(f32[256,128]{1,0:T(8,128)} %get-tuple-element.194), channel_id=1, source_target_pairs={{0,1},{1,0},{2,3},{3,2},{4,5},{5,4},{6,7},{7,6},{8,9},{9,8},{10,11... | collective-permute-start | bytes 393224 | tf_op jit(solution)/shard_map/ppermute | solution.py:285
  392.3 6.9 %collective-permute-start.37 = (f32[256,128]{1,0:T(8,128)S(1)}, f32[256,128]{1,0:T(8,128)S(1)}, u32[]{:S(2)}, u32[]{:S(2)}) collective-permute-start(f32[256,128]{1,0:T(8,128)S(1)} %get-tuple-element.206), channel_id=1, source_target_pairs={{0,20},{1,21},{2,22},{3,23},{4,16},{5,17},{6,18},{7,19},{8,12},{9,... | collective-permute-start | bytes 393224 | tf_op jit(solution)/shard_map/ppermute | solution.py:430
  392.8 9.1 %collective-permute-start.36 = (f32[256,128]{1,0:T(8,128)S(1)}, f32[256,128]{1,0:T(8,128)S(1)}, u32[]{:S(2)}, u32[]{:S(2)}) collective-permute-start(f32[256,128]{1,0:T(8,128)S(1)} %get-tuple-element.205), channel_id=1, source_target_pairs={{0,16},{1,17},{2,18},{3,19},{4,20},{5,21},{6,22},{7,23},{16,0},{17... | collective-permute-start | bytes 393224 | tf_op jit(solution)/shard_map/ppermute | solution.py:429
  (37 other events, 420.6 us)

commit v5 on v4

--- a/solution.py
+++ b/solution.py
@@ -319,7 +319,7 @@
     moved[4, 0] = moved[5, 0] = swap(wide[4, 0], "node", Z1, moves)
     pieces = [(0, (0,)), (0, (1,)), (1, (0,)), (1, (1,)), (2, (0,)), (2, (1,)), (3, (0,)), (3, (1,))]
     final = len(pieces)
-    sends, fetches, arrivals = {1: 1, 2: 2, 3: 3, 4: 4, 5: 5, 6: 6, 7: 7}, {1: (4, 1), 2: (5, 1), 3: (4, 2), 4: (5, 2), 5: (4, 3), 6: (5, 3)}, {3: (4, 1), 4: (5, 1), 5: (4, 2), 6: (5, 2), 7: (4, 3)}
+    sends, fetches, arrivals = {1: 1, 2: 2, 3: 3, 4: 4, 5: 5, 6: 6, 7: 7}, {0: (4, 1), 2: (5, 1), 3: (4, 2), 4: (5, 2), 5: (4, 3), 6: (5, 3)}, {3: (4, 1), 4: (5, 1), 5: (4, 2), 6: (5, 2), 7: (4, 3)}
     fifths, summing = {4: (0, [0, 1]), 6: (1, [2, 3]), 7: (2, [4, 5])}, {5: 0, 7: 1}
 
     own_info = jnp.concatenate([ranks, flag[None]])

time: 406 us -> 399 us (0.983)
  starting transfers between devices: 111 us -> 87.1 us
  waiting for transfers between devices: 168 us -> 186 us
    ppermute x36, waiting for transfers between devices: 165 us -> 181 us  [swap(): return lax.ppermute(value, axis, pairs)]
    ppermute x36, starting transfers between devices: 81.4 us -> 67.4 us  [swap(): return lax.ppermute(value, axis, pairs)]
    all_to_all x3, starting transfers between devices: 22.7 us -> 15.1 us  [column_sum(): lax.all_to_all(blocks, 'col', 0, 0, tiled=True)]
  transfers between devices with their start and end apart: 41 -> 41, of which waited for: 17 -> 18; matrix products, arithmetic and copies ran while one was open for 2% -> 2% of each run, Pallas kernels for 24% -> 25%
where the time goes in v5:
time: 399 us; the launch traced here: 397 us
  waiting for transfers between devices  186 us (47%)
  Pallas kernels  111 us (28%)
  starting transfers between devices  87.1 us (22%)
  other arithmetic  9.42 us (2%)
    ppermute x36, waiting for transfers between devices, swap(): return lax.ppermute(value, axis, pairs)  181 us
    ppermute x36, starting transfers between devices, swap(): return lax.ppermute(value, axis, pairs)  67.4 us
    pallas_call x13, Pallas kernels, moved_level(): pl.pallas_call(lambda *refs: moved_kernel(node, count, *refs), grid_spec=...  48.3 us
    pallas_call x8, Pallas kernels, level3(): pl.pallas_call(lambda *refs: level3_kernel(node, count, *refs), grid_spec...  25.1 us
    pallas_call x2, Pallas kernels, local_levels(): pl.pallas_call(local_kernel, grid_spec=pltpu.PrefetchScalarGridSpec(num_s...  16.3 us
    all_to_all x3, starting transfers between devices, column_sum(): lax.all_to_all(blocks, 'col', 0, 0, tiled=True)  15.1 us
    pallas_call x4, Pallas kernels, widen(): pl.pallas_call(widen_kernel, grid=(1,), in_specs=[mats, mats], out_specs=...  8.28 us
  transfers between devices with their start and end apart: 41, of which 18 were waited for; matrix products, arithmetic and copies ran while one was open for 2% of the time, Pallas kernels for 25%

profile of v5, /device:TPU:2, one launch (start us, length us, event | category | flops | bytes accessed | tf_op | source)
XLA Modules:
  0.0 397.5 jit_solution(8637818429066481220)
XLA Ops:
  2.1 8.1 %local_part0.1 = (f32[4,256,512]{2,1,0:T(8,128)}, f32[4,256,512]{2,1,0:T(8,128)}) custom-call(s32[4]{0:T(128)} %bitcast.ranks, f32[1,4,256,1024]{3,2,1,0:T(8,128)} %state.3, bf16[1,6,4,256,256]{4,3,2,1,0:T(8,128)(2,1)} %refs_3_.35, bf16[1,6,4,256,256]{4,3,2,1,0:T(8,128)(2,1)} %refs_4_.35), custom_call_target="tpu_custom_call" | custom-call | flops 99999997952 | bytes 1000000000 | tf_op jit(solution)/shard_map/local_part0/pallas_call | solution.py:67
  10.2 5.2 %collective-permute-start.7 = (f32[2,2,256,256]{3,2,1,0:T(8,128)}, f32[2,2,256,256]{3,2,1,0:T(8,128)}, u32[]{:S(2)}, u32[]{:S(2)}) collective-permute-start(f32[2,2,256,256]{3,2,1,0:T(8,128)} %widen_0.1), channel_id=1, source_target_pairs={{0,16},{16,0},{40,56},{56,40},{64,80},{80,64},{104,120},{120,104},... | collective-permute-start | bytes 3145736 | tf_op jit(solution)/shard_map/ppermute | solution.py:285
  28.8 3.4 collective-permute-start.6
  32.2 8.2 %local_part1.1 = (f32[4,256,512]{2,1,0:T(8,128)}, f32[4,256,512]{2,1,0:T(8,128)}) custom-call(s32[4]{0:T(128)} %bitcast.ranks, f32[1,4,256,1024]{3,2,1,0:T(8,128)} %state.3, bf16[1,6,4,256,256]{4,3,2,1,0:T(8,128)(2,1)} %refs_3_.35, bf16[1,6,4,256,256]{4,3,2,1,0:T(8,128)(2,1)} %refs_4_.35), custom_call_target="tpu_custom_call" | custom-call | flops 99999997952 | bytes 1000000000 | tf_op jit(solution)/shard_map/local_part1/pallas_call | solution.py:67
  40.4 3.5 collective-permute-start.5
  50.2 3.2 level3_1.2
  53.3 14.5 %collective-permute-done.6 = s32[4]{0:T(128)} collective-permute-done((s32[4]{0:T(128)}, s32[4]{0:T(128)}, u32[]{:S(2)}, u32[]{:S(2)}) %collective-permute-start.6) | collective-permute-done | bytes 48 | tf_op jit(solution)/shard_map/ppermute | solution.py:285
  69.2 3.2 level3_0.3
  72.4 3.4 level4_0.2
  85.3 14.8 %collective-permute-done.3.refs_2_ = f32[256,512]{1,0:T(8,128)} collective-permute-done((f32[256,512]{1,0:T(8,128)}, f32[256,512]{1,0:T(8,128)}, u32[]{:S(2)}, u32[]{:S(2)}) %collective-permute-start.3) | collective-permute-done | bytes 524320 | tf_op jit(solution)/shard_map/ppermute | solution.py:285
  100.1 3.4 level4_0.3
  103.5 6.2 %collective-permute-start.11 = (f32[256,512]{1,0:T(8,128)}, f32[256,512]{1,0:T(8,128)S(1)}, u32[]{:S(2)}, u32[]{:S(2)}) collective-permute-start(f32[256,512]{1,0:T(8,128)} %get-tuple-element.131), channel_id=1, source_target_pairs={{0,48},{8,56},{16,32},{24,40},{32,16},{40,24},{48,0},{56,8},{64,11... | collective-permute-start | bytes 1572872 | tf_op jit(solution)/shard_map/ppermute | solution.py:285
  109.7 4.8 %collective-permute-start.10 = (f32[1,2,256,256]{3,2,1,0:T(8,128)S(1)}, f32[1,2,256,256]{3,2,1,0:T(8,128)S(1)}, u32[]{:S(2)}, u32[]{:S(2)}) collective-permute-start(f32[1,2,256,256]{3,2,1,0:T(8,128)S(1)} %copy-done.41), channel_id=1, source_target_pairs={{0,16},{16,0},{40,56},{56,40},{64,80},{80,64},{104,120},{120,104},... | collective-permute-start | bytes 1572872 | tf_op jit(solution)/shard_map/ppermute | solution.py:285
  114.6 17.0 %collective-permute-done.4.refs_2_ = f32[256,512]{1,0:T(8,128)S(1)} collective-permute-done((f32[256,512]{1,0:T(8,128)S(1)}, f32[256,512]{1,0:T(8,128)S(1)}, u32[]{:S(2)}, u32[]{:S(2)}) %collective-permute-start.4) | collective-permute-done | bytes 524320 | tf_op jit(solution)/shard_map/ppermute | solution.py:285
  131.6 3.3 level4_1.2
  134.9 5.5 %collective-permute-start.14 = (f32[256,512]{1,0:T(8,128)}, f32[256,512]{1,0:T(8,128)}, u32[]{:S(2)}, u32[]{:S(2)}) collective-permute-start(f32[256,512]{1,0:T(8,128)} %get-tuple-element.139), channel_id=1, source_target_pairs={{0,48},{8,56},{16,32},{24,40},{32,16},{40,24},{48,0},{56,8},{64,11... | collective-permute-start | bytes 1572872 | tf_op jit(solution)/shard_map/ppermute | solution.py:285
  142.3 15.7 %collective-permute-done.10.refs_7_ = f32[1,2,256,256]{3,2,1,0:T(8,128)S(1)} collective-permute-done((f32[1,2,256,256]{3,2,1,0:T(8,128)S(1)}, f32[1,2,256,256]{3,2,1,0:T(8,128)S(1)}, u32[]{:S(2)}, u32[]{:S(2)}) %collective-permute-start.10) | collective-permute-done | bytes 524320 | tf_op jit(solution)/shard_map/ppermute | solution.py:285
  158.9 7.4 %collective-permute-done.9.refs_2_ = f32[256,512]{1,0:T(8,128)S(1)} collective-permute-done((f32[256,512]{1,0:T(8,128)S(1)}, f32[256,512]{1,0:T(8,128)S(1)}, u32[]{:S(2)}, u32[]{:S(2)}) %collective-permute-start.9) | collective-permute-done | bytes 524320 | tf_op jit(solution)/shard_map/ppermute | solution.py:285
  166.3 4.6 %level5_0.1 = (f32[256,1024]{1,0:T(8,128)}, f32[256,1024]{1,0:T(8,128)}) custom-call(s32[5]{0:T(128)S(1)} %pad_add_fusion.1.refs_0_.refs_1_, f32[256,512]{1,0:T(8,128)S(1)} %copy-done.20, f32[256,512]{1,0:T(8,128)} %collective-permute-done.8.refs_2_, f32[256,512]{1,0:T(8,128)S(1)} %copy-done.21, f32[256,512]{1,0:T(8,128)S(1)} %collective-permute-done.11.refs_4_, ...), custom_call_target="tpu_custom_call" | custom-call | flops 99999997952 | bytes 1000000000 | tf_op jit(solution)/shard_map/level5_0/pallas_call | solution.py:198
  173.2 3.3 level4_1.3
  177.6 3.8 collective-permute-start.17
  181.3 7.3 %collective-permute-done.13.refs_5_ = f32[1,2,256,256]{3,2,1,0:T(8,128)} collective-permute-done((f32[1,2,256,256]{3,2,1,0:T(8,128)}, f32[1,2,256,256]{3,2,1,0:T(8,128)}, u32[]{:S(2)}, u32[]{:S(2)}) %collective-permute-start.13) | collective-permute-done | bytes 524320 | tf_op jit(solution)/shard_map/ppermute | solution.py:285
  188.7 11.6 %collective-permute-done.12.refs_2_ = f32[256,512]{1,0:T(8,128)} collective-permute-done((f32[256,512]{1,0:T(8,128)}, f32[256,512]{1,0:T(8,128)}, u32[]{:S(2)}, u32[]{:S(2)}) %collective-permute-start.12) | collective-permute-done | bytes 524320 | tf_op jit(solution)/shard_map/ppermute | solution.py:285
  202.1 4.6 %all-to-all-start = ((f32[8,256,128]{2,1,0:T(8,128)}), f32[8,256,128]{2,1,0:T(8,128)}, u32[]{:S(2)}, u32[]{:S(2)}) async-start(f32[8,256,128]{2,1,0:T(8,128)} %total_0.1), calls=%async_computation | async-start | bytes 2097152 | tf_op jit(solution)/shard_map/all_to_all | solution.py:368
  208.4 3.4 level4_2.2
  211.8 3.2 collective-permute-start.20
  215.0 15.4 %collective-permute-done.18.refs_4_ = f32[256,512]{1,0:T(8,128)} collective-permute-done((f32[256,512]{1,0:T(8,128)}, f32[256,512]{1,0:T(8,128)}, u32[]{:S(2)}, u32[]{:S(2)}) %collective-permute-start.18) | collective-permute-done | bytes 524320 | tf_op jit(solution)/shard_map/ppermute | solution.py:285
  230.4 6.6 %collective-permute-done.16.refs_2_ = f32[256,512]{1,0:T(8,128)S(1)} collective-permute-done((f32[256,512]{1,0:T(8,128)S(1)}, f32[256,512]{1,0:T(8,128)S(1)}, u32[]{:S(2)}, u32[]{:S(2)}) %collective-permute-start.16) | collective-permute-done | bytes 524320 | tf_op jit(solution)/shard_map/ppermute | solution.py:285
  237.0 3.4 collective-permute-start.19
  240.5 5.0 %level5_1.1 = (f32[256,1024]{1,0:T(8,128)}, f32[256,1024]{1,0:T(8,128)}) custom-call(s32[5]{0:T(128)S(1)} %copy-done.3, f32[256,512]{1,0:T(8,128)S(1)} %copy-done.22, f32[256,512]{1,0:T(8,128)} %collective-permute-done.14.refs_2_, f32[256,512]{1,0:T(8,128)S(1)} %copy-done.24, f32[256,512]{1,0:T(8,128)} %collective-permute-done.18.refs_4_, ...), custom_call_target="tpu_custom_call" | custom-call | flops 99999997952 | bytes 1000000000 | tf_op jit(solution)/shard_map/level5_1/pallas_call | solution.py:198
  245.5 3.2 collective-permute-start.22
  248.7 3.3 level4_2.3
  255.9 12.4 %collective-permute-done.19.refs_2_ = f32[256,512]{1,0:T(8,128)} collective-permute-done((f32[256,512]{1,0:T(8,128)}, f32[256,512]{1,0:T(8,128)}, u32[]{:S(2)}, u32[]{:S(2)}) %collective-permute-start.19) | collective-permute-done | bytes 524320 | tf_op jit(solution)/shard_map/ppermute | solution.py:285
  270.2 5.3 %all-to-all-start.1 = ((f32[8,256,128]{2,1,0:T(8,128)}), f32[8,256,128]{2,1,0:T(8,128)}, u32[]{:S(2)}, u32[]{:S(2)}) async-start(f32[8,256,128]{2,1,0:T(8,128)} %total_1.1), calls=%async_computation.1 | async-start | bytes 2097152 | tf_op jit(solution)/shard_map/all_to_all | solution.py:368
  275.5 3.4 level4_3.3
  279.5 3.6 collective-permute-start.23
  283.3 5.2 %level5_2.1 = (f32[256,1024]{1,0:T(8,128)}, f32[256,1024]{1,0:T(8,128)}) custom-call(s32[5]{0:T(128)S(1)} %copy-done.3, f32[256,512]{1,0:T(8,128)S(1)} %copy-done.23, f32[256,512]{1,0:T(8,128)} %collective-permute-done.21.refs_2_, f32[256,512]{1,0:T(8,128)S(1)} %copy-done.25, f32[256,512]{1,0:T(8,128)} %collective-permute-done.24.refs_4_, ...), custom_call_target="tpu_custom_call" | custom-call | flops 99999997952 | bytes 1000000000 | tf_op jit(solution)/shard_map/level5_2/pallas_call | solution.py:198
  288.7 25.9 %collective-permute-done.32.refs_2_ = f32[256,512]{1,0:T(8,128)S(1)} collective-permute-done((f32[256,512]{1,0:T(8,128)}, f32[256,512]{1,0:T(8,128)S(1)}, u32[]{:S(2)}, u32[]{:S(2)}) %collective-permute-start.32) | collective-permute-done | bytes 524320 | tf_op jit(solution)/shard_map/ppermute | solution.py:285
  314.6 3.3 level5_3.3
  317.9 3.8 collective-permute-start.33
  323.7 3.4 level4_3.2
  329.8 5.1 %all-to-all-start.2 = ((f32[8,256,128]{2,1,0:T(8,128)}), f32[8,256,128]{2,1,0:T(8,128)}, u32[]{:S(2)}, u32[]{:S(2)}) async-start(f32[8,256,128]{2,1,0:T(8,128)} %total_2.1), calls=%async_computation.2 | async-start | bytes 2097152 | tf_op jit(solution)/shard_map/all_to_all | solution.py:368
  334.9 15.2 %collective-permute-done.27.refs_2_ = f32[256,512]{1,0:T(8,128)S(1)} collective-permute-done((f32[256,512]{1,0:T(8,128)}, f32[256,512]{1,0:T(8,128)S(1)}, u32[]{:S(2)}, u32[]{:S(2)}) %collective-permute-start.27) | collective-permute-done | bytes 524320 | tf_op jit(solution)/shard_map/ppermute | solution.py:285
  350.1 3.3 level5_3.2
  358.3 8.8 %collective-permute-done.29.refs_3_.refs_5_ = f32[256,512]{1,0:T(8,128)S(1)} collective-permute-done((f32[256,512]{1,0:T(8,128)}, f32[256,512]{1,0:T(8,128)S(1)}, u32[]{:S(2)}, u32[]{:S(2)}) %collective-permute-start.29) | collective-permute-done | bytes 524320 | tf_op jit(solution)/shard_map/ppermute | solution.py:285
  369.8 6.2 %collective-permute-start.26 = (f32[3,256,128]{2,1,0:T(8,128)S(1)}, f32[3,256,128]{2,1,0:T(8,128)S(1)}, u32[]{:S(2)}, u32[]{:S(2)}) collective-permute-start(f32[3,256,128]{2,1,0:T(8,128)S(1)} %copy-done.38), channel_id=1, source_target_pairs={{0,16},{16,0},{40,56},{56,40},{64,80},{80,64},{104,120},{120,104},... | collective-permute-start | bytes 1179656 | tf_op jit(solution)/shard_map/ppermute | solution.py:285
  380.4 5.2 %collective-permute-done.31 = f32[256,128]{1,0:T(8,128)S(1)} collective-permute-done((f32[256,128]{1,0:T(8,128)}, f32[256,128]{1,0:T(8,128)S(1)}, u32[]{:S(2)}, u32[]{:S(2)}) %collective-permute-start.31) | collective-permute-done | bytes 131104 | tf_op jit(solution)/shard_map/ppermute | solution.py:285
  387.5 3.8 collective-permute-start.36
  (169 shorter events, 73.5 us)
Async XLA Ops:
  10.2 6.1 %collective-permute-start = (f32[4,256,512]{2,1,0:T(8,128)}, f32[4,256,512]{2,1,0:T(8,128)S(1)}, u32[]{:S(2)}, u32[]{:S(2)}) collective-permute-start(f32[4,256,512]{2,1,0:T(8,128)} %get-tuple-element.107), channel_id=1, source_target_pairs={{0,8},{8,0},{16,24},{24,16},{32,40},{40,32},{48,56},{56,48},{64,72... | collective-permute-start | bytes 6291464 | tf_op jit(solution)/shard_map/ppermute | solution.py:285
  10.2 62.2 %collective-permute-start.7 = (f32[2,2,256,256]{3,2,1,0:T(8,128)}, f32[2,2,256,256]{3,2,1,0:T(8,128)}, u32[]{:S(2)}, u32[]{:S(2)}) collective-permute-start(f32[2,2,256,256]{3,2,1,0:T(8,128)} %widen_0.1), channel_id=1, source_target_pairs={{0,16},{16,0},{40,56},{56,40},{64,80},{80,64},{104,120},{120,104},... | collective-permute-start | bytes 3145736 | tf_op jit(solution)/shard_map/ppermute | solution.py:285
  16.1 34.0 %copy-start.4 = (s32[5]{0:T(128)}, s32[5]{0:T(128)S(1)}, u32[]{:S(2)}) copy-start(s32[5]{0:T(128)S(1)} %pad_add_fusion.refs_0_) | copy-start | bytes 64
  21.0 51.4 %collective-permute-start.1 = (f32[256,512]{1,0:T(8,128)}, f32[256,512]{1,0:T(8,128)}, u32[]{:S(2)}, u32[]{:S(2)}) collective-permute-start(f32[256,512]{1,0:T(8,128)} %get-tuple-element.108), channel_id=1, source_target_pairs={{0,16},{8,24},{16,0},{24,8},{32,48},{40,56},{48,32},{56,40},{64,80... | collective-permute-start | bytes 1572872 | tf_op jit(solution)/shard_map/ppermute | solution.py:285
  28.8 39.0 %collective-permute-start.6 = (s32[4]{0:T(128)}, s32[4]{0:T(128)}, u32[]{:S(2)}, u32[]{:S(2)}) collective-permute-start(s32[4]{0:T(128)} %bitcast.ranks), channel_id=1, source_target_pairs={{0,16},{16,0},{40,56},{56,40},{64,80},{80,64},{104,120},{120,104},... | collective-permute-start | bytes 56 | tf_op jit(solution)/shard_map/ppermute | solution.py:285
  40.4 74.1 %collective-permute-start.5 = (f32[1,2,256,256]{3,2,1,0:T(8,128)}, f32[1,2,256,256]{3,2,1,0:T(8,128)}, u32[]{:S(2)}, u32[]{:S(2)}) collective-permute-start(f32[1,2,256,256]{3,2,1,0:T(8,128)} %get-tuple-element.121), channel_id=1, source_target_pairs={{0,16},{16,0},{40,56},{56,40},{64,80},{80,64},{104,120},{120,104},... | collective-permute-start | bytes 1572872 | tf_op jit(solution)/shard_map/ppermute | solution.py:285
  43.9 24.7 %collective-permute-start.2 = (f32[4,256,512]{2,1,0:T(8,128)}, f32[4,256,512]{2,1,0:T(8,128)}, u32[]{:S(2)}, u32[]{:S(2)}) collective-permute-start(f32[4,256,512]{2,1,0:T(8,128)} %get-tuple-element.111), channel_id=1, source_target_pairs={{0,8},{8,0},{16,24},{24,16},{32,40},{40,32},{48,56},{56,48},{64,72... | collective-permute-start | bytes 6291464 | tf_op jit(solution)/shard_map/ppermute | solution.py:285
  68.5 131.7 %copy-start.2 = (s32[5]{0:T(128)}, s32[5]{0:T(128)S(1)}, u32[]{:S(2)}) copy-start(s32[5]{0:T(128)S(1)} %pad_add_fusion.1.refs_0_.refs_1_) | copy-start | bytes 64
  75.8 38.8 %collective-permute-start.8 = (f32[256,512]{1,0:T(8,128)}, f32[256,512]{1,0:T(8,128)}, u32[]{:S(2)}, u32[]{:S(2)}) collective-permute-start(f32[256,512]{1,0:T(8,128)} %get-tuple-element.124), channel_id=1, source_target_pairs={{0,48},{8,56},{16,32},{24,40},{32,16},{40,24},{48,0},{56,8},{64,11... | collective-permute-start | bytes 1572872 | tf_op jit(solution)/shard_map/ppermute | solution.py:285
  75.8 24.3 %collective-permute-start.3 = (f32[256,512]{1,0:T(8,128)}, f32[256,512]{1,0:T(8,128)}, u32[]{:S(2)}, u32[]{:S(2)}) collective-permute-start(f32[256,512]{1,0:T(8,128)} %get-tuple-element.113), channel_id=1, source_target_pairs={{0,16},{8,24},{16,0},{24,8},{32,48},{40,56},{48,32},{56,40},{64,80... | collective-permute-start | bytes 1572872 | tf_op jit(solution)/shard_map/ppermute | solution.py:285
  100.1 31.5 %collective-permute-start.4 = (f32[256,512]{1,0:T(8,128)S(1)}, f32[256,512]{1,0:T(8,128)S(1)}, u32[]{:S(2)}, u32[]{:S(2)}) collective-permute-start(f32[256,512]{1,0:T(8,128)S(1)} %copy-done.42), channel_id=1, source_target_pairs={{0,16},{8,24},{16,0},{24,8},{32,48},{40,56},{48,32},{56,40},{64,80... | collective-permute-start | bytes 1572872 | tf_op jit(solution)/shard_map/ppermute | solution.py:285
  103.5 38.8 %collective-permute-start.11 = (f32[256,512]{1,0:T(8,128)}, f32[256,512]{1,0:T(8,128)S(1)}, u32[]{:S(2)}, u32[]{:S(2)}) collective-permute-start(f32[256,512]{1,0:T(8,128)} %get-tuple-element.131), channel_id=1, source_target_pairs={{0,48},{8,56},{16,32},{24,40},{32,16},{40,24},{48,0},{56,8},{64,11... | collective-permute-start | bytes 1572872 | tf_op jit(solution)/shard_map/ppermute | solution.py:285
  109.7 48.3 %collective-permute-start.10 = (f32[1,2,256,256]{3,2,1,0:T(8,128)S(1)}, f32[1,2,256,256]{3,2,1,0:T(8,128)S(1)}, u32[]{:S(2)}, u32[]{:S(2)}) collective-permute-start(f32[1,2,256,256]{3,2,1,0:T(8,128)S(1)} %copy-done.41), channel_id=1, source_target_pairs={{0,16},{16,0},{40,56},{56,40},{64,80},{80,64},{104,120},{120,104},... | collective-permute-start | bytes 1572872 | tf_op jit(solution)/shard_map/ppermute | solution.py:285
  131.6 34.8 %collective-permute-start.9 = (f32[256,512]{1,0:T(8,128)S(1)}, f32[256,512]{1,0:T(8,128)S(1)}, u32[]{:S(2)}, u32[]{:S(2)}) collective-permute-start(f32[256,512]{1,0:T(8,128)S(1)} %copy-done.43), channel_id=1, source_target_pairs={{0,16},{8,24},{16,0},{24,8},{32,48},{40,56},{48,32},{56,40},{64,80... | collective-permute-start | bytes 1572872 | tf_op jit(solution)/shard_map/ppermute | solution.py:285
  131.6 34.7 %copy-start.20 = (f32[256,512]{1,0:T(8,128)S(1)}, f32[256,512]{1,0:T(8,128)}, u32[]{:S(2)}) copy-start(f32[256,512]{1,0:T(8,128)} %get-tuple-element.140.refs_1_) | copy-start | bytes 1572868
  131.6 34.7 %copy-start.21 = (f32[256,512]{1,0:T(8,128)S(1)}, f32[256,512]{1,0:T(8,128)}, u32[]{:S(2)}) copy-start(f32[256,512]{1,0:T(8,128)} %get-tuple-element.142.refs_3_) | copy-start | bytes 1572868
  134.9 42.7 %collective-permute-start.14 = (f32[256,512]{1,0:T(8,128)}, f32[256,512]{1,0:T(8,128)}, u32[]{:S(2)}, u32[]{:S(2)}) collective-permute-start(f32[256,512]{1,0:T(8,128)} %get-tuple-element.139), channel_id=1, source_target_pairs={{0,48},{8,56},{16,32},{24,40},{32,16},{40,24},{48,0},{56,8},{64,11... | collective-permute-start | bytes 1572872 | tf_op jit(solution)/shard_map/ppermute | solution.py:285
  140.4 48.3 %collective-permute-start.13 = (f32[1,2,256,256]{3,2,1,0:T(8,128)}, f32[1,2,256,256]{3,2,1,0:T(8,128)}, u32[]{:S(2)}, u32[]{:S(2)}) collective-permute-start(f32[1,2,256,256]{3,2,1,0:T(8,128)} %get-tuple-element.135), channel_id=1, source_target_pairs={{0,16},{16,0},{40,56},{56,40},{64,80},{80,64},{104,120},{120,104},... | collective-permute-start | bytes 1572872 | tf_op jit(solution)/shard_map/ppermute | solution.py:285
  166.3 34.0 %collective-permute-start.12 = (f32[256,512]{1,0:T(8,128)}, f32[256,512]{1,0:T(8,128)}, u32[]{:S(2)}, u32[]{:S(2)}) collective-permute-start(f32[256,512]{1,0:T(8,128)} %get-tuple-element.132), channel_id=1, source_target_pairs={{0,16},{8,24},{16,0},{24,8},{32,48},{40,56},{48,32},{56,40},{64,80... | collective-permute-start | bytes 1572872 | tf_op jit(solution)/shard_map/ppermute | solution.py:285
  171.0 29.3 %collective-permute-start.15 = (f32[256,1024]{1,0:T(8,128)}, f32[256,1024]{1,0:T(8,128)S(1)}, u32[]{:S(2)}, u32[]{:S(2)}) collective-permute-start(f32[256,1024]{1,0:T(8,128)} %get-tuple-element.144), channel_id=1, source_target_pairs={{0,64},{8,72},{16,80},{24,88},{32,96},{40,104},{48,112},{56,120},{... | collective-permute-start | bytes 3145736 | tf_op jit(solution)/shard_map/ppermute | solution.py:285
  176.5 53.9 %collective-permute-start.18 = (f32[256,512]{1,0:T(8,128)}, f32[256,512]{1,0:T(8,128)}, u32[]{:S(2)}, u32[]{:S(2)}) collective-permute-start(f32[256,512]{1,0:T(8,128)} %get-tuple-element.151), channel_id=1, source_target_pairs={{0,48},{8,56},{16,32},{24,40},{32,16},{40,24},{48,0},{56,8},{64,11... | collective-permute-start | bytes 1572872 | tf_op jit(solution)/shard_map/ppermute | solution.py:285
  177.6 52.9 %collective-permute-start.17 = (f32[1,2,256,256]{3,2,1,0:T(8,128)}, f32[1,2,256,256]{3,2,1,0:T(8,128)}, u32[]{:S(2)}, u32[]{:S(2)}) collective-permute-start(f32[1,2,256,256]{3,2,1,0:T(8,128)} %get-tuple-element.148), channel_id=1, source_target_pairs={{0,16},{16,0},{40,56},{56,40},{64,80},{80,64},{104,120},{120,104},... | collective-permute-start | bytes 1572872 | tf_op jit(solution)/shard_map/ppermute | solution.py:285
  202.1 49.9 %all-to-all-start = ((f32[8,256,128]{2,1,0:T(8,128)}), f32[8,256,128]{2,1,0:T(8,128)}, u32[]{:S(2)}, u32[]{:S(2)}) async-start(f32[8,256,128]{2,1,0:T(8,128)} %total_0.1), calls=%async_computation | async-start | bytes 2097152 | tf_op jit(solution)/shard_map/all_to_all | solution.py:368
  206.7 30.3 %collective-permute-start.16 = (f32[256,512]{1,0:T(8,128)S(1)}, f32[256,512]{1,0:T(8,128)S(1)}, u32[]{:S(2)}, u32[]{:S(2)}) collective-permute-start(f32[256,512]{1,0:T(8,128)S(1)} %copy-done.40), channel_id=1, source_target_pairs={{0,16},{8,24},{16,0},{24,8},{32,48},{40,56},{48,32},{56,40},{64,80... | collective-permute-start | bytes 1572872 | tf_op jit(solution)/shard_map/ppermute | solution.py:285
  208.4 32.1 %copy-start.1 = (f32[1,2,256,256]{3,2,1,0:T(8,128)S(1)}, f32[1,2,256,256]{3,2,1,0:T(8,128)}, u32[]{:S(2)}) copy-start(f32[1,2,256,256]{3,2,1,0:T(8,128)} %copy-done) | copy-start | bytes 1572868
  208.4 32.1 %copy-start.22 = (f32[256,512]{1,0:T(8,128)S(1)}, f32[256,512]{1,0:T(8,128)}, u32[]{:S(2)}) copy-start(f32[256,512]{1,0:T(8,128)} %get-tuple-element.161.refs_1_) | copy-start | bytes 1572868
  208.4 32.1 %copy-start.24 = (f32[256,512]{1,0:T(8,128)S(1)}, f32[256,512]{1,0:T(8,128)}, u32[]{:S(2)}) copy-start(f32[256,512]{1,0:T(8,128)} %get-tuple-element.163.refs_3_) | copy-start | bytes 1572868
  211.8 42.2 %collective-permute-start.21 = (f32[256,512]{1,0:T(8,128)}, f32[256,512]{1,0:T(8,128)}, u32[]{:S(2)}, u32[]{:S(2)}) collective-permute-start(f32[256,512]{1,0:T(8,128)} %get-tuple-element.158), channel_id=1, source_target_pairs={{0,48},{8,56},{16,32},{24,40},{32,16},{40,24},{48,0},{56,8},{64,11... | collective-permute-start | bytes 1572872 | tf_op jit(solution)/shard_map/ppermute | solution.py:285
  211.8 44.1 %collective-permute-start.20 = (f32[1,2,256,256]{3,2,1,0:T(8,128)}, f32[1,2,256,256]{3,2,1,0:T(8,128)}, u32[]{:S(2)}, u32[]{:S(2)}) collective-permute-start(f32[1,2,256,256]{3,2,1,0:T(8,128)} %get-tuple-element.154), channel_id=1, source_target_pairs={{0,16},{16,0},{40,56},{56,40},{64,80},{80,64},{104,120},{120,104},... | collective-permute-start | bytes 1572872 | tf_op jit(solution)/shard_map/ppermute | solution.py:285
  237.0 31.3 %collective-permute-start.19 = (f32[256,512]{1,0:T(8,128)}, f32[256,512]{1,0:T(8,128)}, u32[]{:S(2)}, u32[]{:S(2)}) collective-permute-start(f32[256,512]{1,0:T(8,128)} %get-tuple-element.152), channel_id=1, source_target_pairs={{0,16},{8,24},{16,0},{24,8},{32,48},{40,56},{48,32},{56,40},{64,80... | collective-permute-start | bytes 1572872 | tf_op jit(solution)/shard_map/ppermute | solution.py:285
  245.5 22.8 %collective-permute-start.22 = (f32[256,1024]{1,0:T(8,128)}, f32[256,1024]{1,0:T(8,128)S(1)}, u32[]{:S(2)}, u32[]{:S(2)}) collective-permute-start(f32[256,1024]{1,0:T(8,128)} %get-tuple-element.166), channel_id=1, source_target_pairs={{0,64},{8,72},{16,80},{24,88},{32,96},{40,104},{48,112},{56,120},{... | collective-permute-start | bytes 3145736 | tf_op jit(solution)/shard_map/ppermute | solution.py:285
  252.0 31.3 %collective-permute-start.24 = (f32[256,512]{1,0:T(8,128)}, f32[256,512]{1,0:T(8,128)}, u32[]{:S(2)}, u32[]{:S(2)}) collective-permute-start(f32[256,512]{1,0:T(8,128)} %get-tuple-element.177), channel_id=1, source_target_pairs={{0,48},{8,56},{16,32},{24,40},{32,16},{40,24},{48,0},{56,8},{64,11... | collective-permute-start | bytes 1572872 | tf_op jit(solution)/shard_map/ppermute | solution.py:285
  254.0 34.7 %collective-permute-start.28 = (f32[1,2,256,256]{3,2,1,0:T(8,128)}, f32[1,2,256,256]{3,2,1,0:T(8,128)}, u32[]{:S(2)}, u32[]{:S(2)}) collective-permute-start(f32[1,2,256,256]{3,2,1,0:T(8,128)} %get-tuple-element.187), channel_id=1, source_target_pairs={{0,16},{16,0},{40,56},{56,40},{64,80},{80,64},{104,120},{120,104},... | collective-permute-start | bytes 1572872 | tf_op jit(solution)/shard_map/ppermute | solution.py:285
  270.2 51.5 %all-to-all-start.1 = ((f32[8,256,128]{2,1,0:T(8,128)}), f32[8,256,128]{2,1,0:T(8,128)}, u32[]{:S(2)}, u32[]{:S(2)}) async-start(f32[8,256,128]{2,1,0:T(8,128)} %total_1.1), calls=%async_computation.1 | async-start | bytes 2097152 | tf_op jit(solution)/shard_map/all_to_all | solution.py:368
  278.8 35.7 %collective-permute-start.32 = (f32[256,512]{1,0:T(8,128)}, f32[256,512]{1,0:T(8,128)S(1)}, u32[]{:S(2)}, u32[]{:S(2)}) collective-permute-start(f32[256,512]{1,0:T(8,128)} %get-tuple-element.198), channel_id=1, source_target_pairs={{0,48},{8,56},{16,32},{24,40},{32,16},{40,24},{48,0},{56,8},{64,11... | collective-permute-start | bytes 1572872 | tf_op jit(solution)/shard_map/ppermute | solution.py:285
  279.5 44.1 %collective-permute-start.23 = (f32[256,512]{1,0:T(8,128)}, f32[256,512]{1,0:T(8,128)}, u32[]{:S(2)}, u32[]{:S(2)}) collective-permute-start(f32[256,512]{1,0:T(8,128)} %get-tuple-element.168), channel_id=1, source_target_pairs={{0,16},{8,24},{16,0},{24,8},{32,48},{40,56},{48,32},{56,40},{64,80... | collective-permute-start | bytes 1572872 | tf_op jit(solution)/shard_map/ppermute | solution.py:285
  288.5 38.5 %collective-permute-start.25 = (f32[256,1024]{1,0:T(8,128)}, f32[256,1024]{1,0:T(8,128)}, u32[]{:S(2)}, u32[]{:S(2)}) collective-permute-start(f32[256,1024]{1,0:T(8,128)} %get-tuple-element.180), channel_id=1, source_target_pairs={{0,64},{8,72},{16,80},{24,88},{32,96},{40,104},{48,112},{56,120},{... | collective-permute-start | bytes 3145736 | tf_op jit(solution)/shard_map/ppermute | solution.py:285
  317.9 35.8 %collective-permute-start.33 = (f32[256,512]{1,0:T(8,128)}, f32[256,512]{1,0:T(8,128)}, u32[]{:S(2)}, u32[]{:S(2)}) collective-permute-start(f32[256,512]{1,0:T(8,128)} %get-tuple-element.200), channel_id=1, source_target_pairs={{0,64},{8,72},{16,80},{24,88},{32,96},{40,104},{48,112},{56,120},{... | collective-permute-start | bytes 1572872 | tf_op jit(solution)/shard_map/ppermute | solution.py:285
  327.0 23.1 %collective-permute-start.27 = (f32[256,512]{1,0:T(8,128)}, f32[256,512]{1,0:T(8,128)S(1)}, u32[]{:S(2)}, u32[]{:S(2)}) collective-permute-start(f32[256,512]{1,0:T(8,128)} %get-tuple-element.186), channel_id=1, source_target_pairs={{0,48},{8,56},{16,32},{24,40},{32,16},{40,24},{48,0},{56,8},{64,11... | collective-permute-start | bytes 1572872 | tf_op jit(solution)/shard_map/ppermute | solution.py:285
  329.8 26.4 %all-to-all-start.2 = ((f32[8,256,128]{2,1,0:T(8,128)}), f32[8,256,128]{2,1,0:T(8,128)}, u32[]{:S(2)}, u32[]{:S(2)}) async-start(f32[8,256,128]{2,1,0:T(8,128)} %total_2.1), calls=%async_computation.2 | async-start | bytes 2097152 | tf_op jit(solution)/shard_map/all_to_all | solution.py:368
  353.4 13.6 %collective-permute-start.29 = (f32[256,512]{1,0:T(8,128)}, f32[256,512]{1,0:T(8,128)S(1)}, u32[]{:S(2)}, u32[]{:S(2)}) collective-permute-start(f32[256,512]{1,0:T(8,128)} %get-tuple-element.190), channel_id=1, source_target_pairs={{0,64},{8,72},{16,80},{24,88},{32,96},{40,104},{48,112},{56,120},{... | collective-permute-start | bytes 1572872 | tf_op jit(solution)/shard_map/ppermute | solution.py:285
  356.2 12.3 %collective-permute-start.34 = (f32[256,256]{1,0:T(8,128)}, f32[256,256]{1,0:T(8,128)S(1)}, u32[]{:S(2)}, u32[]{:S(2)}) collective-permute-start(f32[256,256]{1,0:T(8,128)} %get-tuple-element.202), channel_id=1, source_target_pairs={{0,2},{1,3},{2,0},{3,1},{4,6},{5,7},{6,4},{7,5},{8,10},{9,11},{10,... | collective-permute-start | bytes 786440 | tf_op jit(solution)/shard_map/ppermute | solution.py:285
  368.5 10.7 %collective-permute-start.30 = (f32[256,256]{1,0:T(8,128)}, f32[256,256]{1,0:T(8,128)S(1)}, u32[]{:S(2)}, u32[]{:S(2)}) collective-permute-start(f32[256,256]{1,0:T(8,128)} %get-tuple-element.192), channel_id=1, source_target_pairs={{0,2},{1,3},{2,0},{3,1},{4,6},{5,7},{6,4},{7,5},{8,10},{9,11},{10,... | collective-permute-start | bytes 786440 | tf_op jit(solution)/shard_map/ppermute | solution.py:285
  369.8 10.6 %collective-permute-start.35 = (f32[256,128]{1,0:T(8,128)}, f32[256,128]{1,0:T(8,128)S(1)}, u32[]{:S(2)}, u32[]{:S(2)}) collective-permute-start(f32[256,128]{1,0:T(8,128)} %get-tuple-element.204), channel_id=1, source_target_pairs={{0,1},{1,0},{2,3},{3,2},{4,5},{5,4},{6,7},{7,6},{8,9},{9,8},{10,11... | collective-permute-start | bytes 393224 | tf_op jit(solution)/shard_map/ppermute | solution.py:285
  369.8 21.4 %collective-permute-start.26 = (f32[3,256,128]{2,1,0:T(8,128)S(1)}, f32[3,256,128]{2,1,0:T(8,128)S(1)}, u32[]{:S(2)}, u32[]{:S(2)}) collective-permute-start(f32[3,256,128]{2,1,0:T(8,128)S(1)} %copy-done.38), channel_id=1, source_target_pairs={{0,16},{16,0},{40,56},{56,40},{64,80},{80,64},{104,120},{120,104},... | collective-permute-start | bytes 1179656 | tf_op jit(solution)/shard_map/ppermute | solution.py:285
  380.4 5.2 %collective-permute-start.31 = (f32[256,128]{1,0:T(8,128)}, f32[256,128]{1,0:T(8,128)S(1)}, u32[]{:S(2)}, u32[]{:S(2)}) collective-permute-start(f32[256,128]{1,0:T(8,128)} %get-tuple-element.194), channel_id=1, source_target_pairs={{0,1},{1,0},{2,3},{3,2},{4,5},{5,4},{6,7},{7,6},{8,9},{9,8},{10,11... | collective-permute-start | bytes 393224 | tf_op jit(solution)/shard_map/ppermute | solution.py:285
  386.6 7.0 %collective-permute-start.37 = (f32[256,128]{1,0:T(8,128)S(1)}, f32[256,128]{1,0:T(8,128)S(1)}, u32[]{:S(2)}, u32[]{:S(2)}) collective-permute-start(f32[256,128]{1,0:T(8,128)S(1)} %get-tuple-element.206), channel_id=1, source_target_pairs={{0,20},{1,21},{2,22},{3,23},{4,16},{5,17},{6,18},{7,19},{8,12},{9,... | collective-permute-start | bytes 393224 | tf_op jit(solution)/shard_map/ppermute | solution.py:430
  387.5 9.2 %collective-permute-start.36 = (f32[256,128]{1,0:T(8,128)S(1)}, f32[256,128]{1,0:T(8,128)S(1)}, u32[]{:S(2)}, u32[]{:S(2)}) collective-permute-start(f32[256,128]{1,0:T(8,128)S(1)} %get-tuple-element.205), channel_id=1, source_target_pairs={{0,16},{1,17},{2,18},{3,19},{4,20},{5,21},{6,22},{7,23},{16,0},{17... | collective-permute-start | bytes 393224 | tf_op jit(solution)/shard_map/ppermute | solution.py:429
  (37 other events, 428.1 us)
